TPU v7x, 32 devices: a whole 2x2x4 slice. The times are simulated.
32 devices in a mesh: blk: 8 (over y, x, core), uly: 4 (over z).
Axes of the slice: x: 2, y: 2, z: 4, core: 2. Of those that a mesh axis runs over, the one named last changes fastest.
Arguments:
- qkv: bfloat16 [2048, 3, 3072], P(('blk', 'uly')), may hold values from -9 to 9
Outputs:
- attended: float32 [2048, 3072], P('blk', 'uly')
- log_total: float32 [24, 2048], P('uly', 'blk')
All inputs are finite; a program needn't handle non-finite values.
Results may differ from a plain program's by a relative error of at most 0.0027.
Values may be sent and summed in bfloat16 or wider, within the bound.
No kernel may reach another device: no remote copies, remote signals or barrier semaphores. Data moves between devices by JAX's collectives and lax.ppermute only.
A program may use at most 64 MiB of HBM per device.

v0:
```python
import math

import jax
import jax.numpy as jnp
from jax import lax
from jax.sharding import PartitionSpec as P

HEAD_DIM = 128


def from_behind(value, axis, steps):
    count = lax.axis_size(axis)
    pairs = [(source, (source + steps) % count) for source in range(count)]
    return lax.ppermute(value, axis, pairs)


def block_scores(query_rows, key_rows, temper):
    return (
        jnp.einsum("rhd,khd->hrk", query_rows, key_rows, preferred_element_type=jnp.float32)
        * temper
    )


def attend_first(query_rows, key_rows, value_rows, temper):
    scores = block_scores(query_rows, key_rows, temper)
    top = jnp.max(scores, axis=2)
    weights = jnp.exp(scores - top[:, :, None])
    total = jnp.sum(weights, axis=2)
    accum = jnp.einsum(
        "hrk,khd->hrd", weights.astype(jnp.bfloat16), value_rows, preferred_element_type=jnp.float32
    )
    return (top, total, accum)


def attend_next(running, query_rows, key_rows, value_rows, temper):
    top, total, accum = running
    scores = block_scores(query_rows, key_rows, temper)
    newtop = jnp.maximum(top, jnp.max(scores, axis=2))
    factor = jnp.exp(top - newtop)
    weights = jnp.exp(scores - newtop[:, :, None])
    total = total * factor + jnp.sum(weights, axis=2)
    accum = accum * factor[:, :, None] + jnp.einsum(
        "hrk,khd->hrd", weights.astype(jnp.bfloat16), value_rows, preferred_element_type=jnp.float32
    )
    return (newtop, total, accum)


def shards(qkv):
    width = qkv.shape[2] // lax.axis_size("uly")
    heads_local = width // HEAD_DIM
    temper = 1.0 / math.sqrt(HEAD_DIM)
    grouped = lax.all_to_all(qkv, "uly", split_axis=2, concat_axis=0, tiled=True)
    prev_pairs = from_behind(grouped[:, 1:], "blk", 1)
    block_len = grouped.shape[0]
    row_count = math.gcd(block_len, 512)
    queries = grouped[:, 0].reshape(block_len // row_count, row_count, heads_local, HEAD_DIM)
    own_keys = grouped[:, 1].reshape(block_len, heads_local, HEAD_DIM)
    own_values = grouped[:, 2].reshape(block_len, heads_local, HEAD_DIM)
    prev_keys = prev_pairs[:, 0].reshape(block_len, heads_local, HEAD_DIM)
    prev_values = prev_pairs[:, 1].reshape(block_len, heads_local, HEAD_DIM)

    def per_rows(query_rows):
        running = attend_first(query_rows, own_keys, own_values, temper)
        top, total, accum = attend_next(running, query_rows, prev_keys, prev_values, temper)
        normed = accum / total[:, :, None]
        return (jnp.transpose(normed, (1, 0, 2)).reshape(row_count, width), top + jnp.log(total))

    attended_rows, log_rows = lax.map(per_rows, queries)
    attended = attended_rows.reshape(block_len, width)
    log_total = jnp.transpose(log_rows, (1, 0, 2)).reshape(heads_local, block_len)
    return (attended, log_total)


def solution(mesh):
    placed = (P(("blk", "uly"), None, None),)
    return jax.shard_map(
        shards,
        mesh=mesh,
        in_specs=placed,
        out_specs=(P("blk", "uly"), P("uly", "blk")),
        check_vma=False,
    )
```

profile of v0, /device:TPU:0, one launch (start us, length us, event | category | flops | bytes accessed | tf_op | source)
XLA Modules:
  0.0 74.6 jit_solution(17815620228269308837)
XLA Ops:
  0.6 4.6 %copy.32 = bf16[64,3,3072]{0,1,2:T(4,128)(2,1)S(1)} copy(bf16[64,3,3072]{2,0,1:T(8,128)(2,1)} %param.1) | data formatting | bytes 2359296 | tf_op args[0]
  5.2 3.1 %reshape.40 = bf16[4,2,73728]{2,1,0:T(2,128)(2,1)} reshape(bf16[3072,3,64]{2,1,0:T(4,128)(2,1)S(1)} %bitcast.42) | data formatting | bytes 2359296
  8.3 35.0 %all_to_all.18 = bf16[4,2,73728]{2,1,0:T(2,128)(2,1)} all-to-all(bf16[4,2,73728]{2,1,0:T(2,128)(2,1)} %reshape.40), channel_id=1, replica_groups=mesh['blk'=8,'uly'=4] {'uly'}, dimensions={0} | all-to-all | bytes 2359296 | tf_op jit(solution)/shard_map/all_to_all | solution.py:52
  43.2 3.5 %reshape.41 = bf16[3072,3,64]{2,1,0:T(4,128)(2,1)S(1)} reshape(bf16[4,2,73728]{2,1,0:T(2,128)(2,1)} %all_to_all.18) | data formatting | bytes 2359296
  46.7 3.2 %copy.34 = bf16[4,64,3,768]{3,1,0,2:T(8,128)(2,1)} copy(bf16[4,64,3,768]{1,2,3,0:T(4,128)(2,1)S(1)} %bitcast.41) | data formatting | bytes 2359296 | tf_op jit(solution)/shard_map/all_to_all | solution.py:52
  49.9 0.0 copy-start
  49.9 2.2 %slice.27 = bf16[256,2,768]{2,0,1:T(8,128)(2,1)} slice(bf16[256,3,768]{2,0,1:T(8,128)(2,1)} %bitcast.43), slice={[0:256], [1:3], [0:768]} | slice | bytes 1572864 | tf_op jit(solution)/shard_map/slice | solution.py:53
  52.1 0.0 collective-permute-start
  52.1 0.0 copy-done
  52.1 0.1 fusion.13
  52.2 0.2 copy.36
  52.3 0.9 %copy.39 = bf16[256,1,768]{0,2,1:T(8,128)(2,1)} copy(bf16[256,1,768]{2,0,1:T(8,128)(2,1)S(1)} %get-tuple-element.37) | data formatting | bytes 786432 | tf_op jit(solution)/shard_map/slice | solution.py:58
  53.2 0.2 copy.35
  53.4 0.4 fusion.15
  53.8 10.9 %collective-permute-done = bf16[256,2,768]{2,0,1:T(8,128)(2,1)} collective-permute-done((bf16[256,2,768]{2,0,1:T(8,128)(2,1)}, bf16[256,2,768]{2,0,1:T(8,128)(2,1)}, u32[]{:S(2)}, u32[]{:S(2)}) %collective-permute-start) | collective-permute-done | bytes 786464 | tf_op jit(solution)/shard_map/ppermute | solution.py:14
  64.7 1.9 %fusion.14 = (bf16[256,1,768]{2,0,1:T(8,128)(2,1)}, bf16[256,1,768]{2,0,1:T(8,128)(2,1)S(1)}) fusion(bf16[256,2,768]{2,0,1:T(8,128)(2,1)} %collective-permute-done), kind=kLoop, calls=%fused_computation.21 | loop fusion | bytes 1572864 | tf_op jit(solution)/shard_map/slice | solution.py:60
  66.6 0.9 %copy.41 = bf16[256,1,768]{0,2,1:T(8,128)(2,1)} copy(bf16[256,1,768]{2,0,1:T(8,128)(2,1)S(1)} %get-tuple-element.40) | data formatting | bytes 786432 | tf_op jit(solution)/shard_map/slice | solution.py:59
  67.5 1.4 %fusion.16 = (f32[6,256]{1,0:T(8,128)S(1)}, f32[6,256,256]{1,2,0:T(8,128)S(1)}) fusion(bf16[256,6,128]{0,2,1:T(8,128)(2,1)S(1)} %bitcast.46, bf16[256,6,128]{0,2,1:T(8,128)(2,1)} %bitcast.48), kind=kOutput, calls=%fused_computation.23 | convolution fusion | flops 101448192 | bytes 2365440 | tf_op jit(solution)/shard_map/while/body/eval_jaxpr/rhd,khd->hrk/dot_general | solution.py:19
  69.0 0.0 copy-start.1
  69.0 0.4 fusion
  69.4 0.6 log_add_fusion
  70.0 0.6 bitcast_add_fusion
  70.7 0.0 copy-done.1
  70.7 0.9 %copy.44 = bf16[256,1,768]{0,2,1:T(8,128)(2,1)} copy(bf16[256,1,768]{2,0,1:T(8,128)(2,1)S(1)} %copy-done.1) | data formatting | bytes 786432 | tf_op jit(solution)/shard_map/slice | solution.py:60
  71.6 0.0 copy-start.2
  71.6 0.0 copy-start.3
  71.6 1.5 %fusion.4 = f32[256,6,128]{0,2,1:T(8,128)S(1)} fusion(bf16[256,6,128]{0,2,1:T(8,128)(2,1)} %bitcast.49, f32[6,256,256]{1,2,0:T(8,128)S(1)} %get-tuple-element.42, f32[6,256]{1,0:T(8,128)S(1)} %get-tuple-element.41, f32[256,6]{0,1:T(8,128)} %get-tuple-element.35), kind=kOutput, calls=%fused_computation.10 | convolution fusion | flops 101646336 | bytes 2764800 | tf_op jit(solution)/shard_map/while/body/eval_jaxpr/hrk,khd->hrd/dot_general | solution.py:29
  73.0 0.0 copy-done.2
  73.0 0.0 copy-done.3
  73.1 0.4 fusion.6
  73.5 1.1 %copy.46 = f32[256,768]{1,0:T(8,128)} copy(f32[256,768]{0,1:T(8,128)S(1)} %bitcast.50) | data formatting | bytes 1572864
  (1 shorter events, 0.0 us)
Async XLA Ops:
  49.9 2.2 %copy-start = (bf16[4,64,3,768]{3,1,0,2:T(8,128)(2,1)S(1)}, bf16[4,64,3,768]{3,1,0,2:T(8,128)(2,1)}, u32[]{:S(2)}) copy-start(bf16[4,64,3,768]{3,1,0,2:T(8,128)(2,1)} %copy.34) | copy-start | bytes 3538948
  52.1 12.6 %collective-permute-start = (bf16[256,2,768]{2,0,1:T(8,128)(2,1)}, bf16[256,2,768]{2,0,1:T(8,128)(2,1)}, u32[]{:S(2)}, u32[]{:S(2)}) collective-permute-start(bf16[256,2,768]{2,0,1:T(8,128)(2,1)} %slice.27), channel_id=1, source_target_pairs={{0,4},{4,8},{8,12},{12,16},{16,20},{20,24},{24,28},{28,0},{1,5},{5... | collective-permute-start | bytes 2359304 | tf_op jit(solution)/shard_map/ppermute | solution.py:14
  69.0 1.7 %copy-start.1 = (bf16[256,1,768]{2,0,1:T(8,128)(2,1)S(1)}, bf16[256,1,768]{2,0,1:T(8,128)(2,1)}, u32[]{:S(2)}) copy-start(bf16[256,1,768]{2,0,1:T(8,128)(2,1)} %get-tuple-element.39) | copy-start | bytes 1179652
  71.6 1.5 %copy-start.2 = (bf16[256,1,768]{0,2,1:T(8,128)(2,1)S(1)}, bf16[256,1,768]{0,2,1:T(8,128)(2,1)}, u32[]{:S(2)}) copy-start(bf16[256,1,768]{0,2,1:T(8,128)(2,1)} %copy.44) | copy-start | bytes 1179652
  71.6 1.5 %copy-start.3 = (f32[256,6]{0,1:T(8,128)S(1)}, f32[256,6]{0,1:T(8,128)}, u32[]{:S(2)}) copy-start(f32[256,6]{0,1:T(8,128)} %get-tuple-element.34) | copy-start | bytes 18436
where the time goes:
time: 75 us; the launch traced here: 74.6 us
  blocking collectives  35 us (47%)
  local copies, waits for them, and re-layouts  22.7 us (30%)
  waiting for transfers between devices  10.9 us (15%)
  matrix products  3.71 us (5%)
  other arithmetic  1.68 us (2%)
    all_to_all x1, blocking collectives, shards(): lax.all_to_all(qkv, 'uly', split_axis=2, concat_axis=0, tiled=True)  35 us
    unnamed x12, local copies, waits for them, and re-layouts  12.3 us
    ppermute x1, waiting for transfers between devices, from_behind(): return lax.ppermute(value, axis, pairs)  10.9 us
    all_to_all x1, local copies, waits for them, and re-layouts, shards(): lax.all_to_all(qkv, 'uly', split_axis=2, concat_axis=0, tiled=True)  3.21 us
    slice x2, local copies, waits for them, and re-layouts, shards(): prev_values = prev_pairs[:, 1].reshape(block_len, heads_local, HEAD_DIM)  2.83 us
    slice x1, local copies, waits for them, and re-layouts, shards(): prev_pairs = from_behind(grouped[:, 1:], 'blk', 1)  2.16 us
    dot_general x2, matrix products, block_scores(): jnp.einsum('rhd,khd->hrk', query_rows, key_rows, preferred_element_type=j...  1.84 us
  transfers between devices with their start and end apart: 1, of which 1 were waited for; matrix products, arithmetic and copies ran while one was open for 2% of the time, Pallas kernels for 0%

commit v1 on v0

v1 whole, which is shorter than its diff:
```python
import functools
import math

import jax
import jax.numpy as jnp
from jax import lax
from jax.experimental import pallas as pl
from jax.experimental.pallas import tpu as pltpu
from jax.sharding import PartitionSpec as P

HEAD_DIM = 128


def shift(value, axis, steps):
    count = lax.axis_size(axis)
    return lax.ppermute(value, axis, [(i, (i + steps) % count) for i in range(count)])


def attend_kernel(count, heads, rows, *refs):
    slot = refs[0]
    ins = refs[1 : 1 + 3 * count]
    out, log_out = refs[1 + 3 * count : 3 + 3 * count]
    q_all, own, prev, stat, sem = refs[3 + 3 * count :]
    piece = ins[0].shape[0]
    copies = []
    for i in range(count):
        start = pl.multiple_of(slot[i] * piece, piece)
        copies.append(pltpu.make_async_copy(ins[i], q_all.at[pl.ds(start, piece)], sem.at[0]))
        fixed = pl.ds(i * piece, piece)
        copies.append(pltpu.make_async_copy(ins[count + i], own.at[:, fixed], sem.at[1]))
        copies.append(pltpu.make_async_copy(ins[2 * count + i], prev.at[:, fixed], sem.at[2]))
    for copy in copies:
        copy.start()
    for copy in copies:
        copy.wait()
    temper = 1.0 / math.sqrt(HEAD_DIM)
    block_len = q_all.shape[0]
    contract = (((1,), (1,)), ((), ()))

    for r in range(block_len // rows):
        span = slice(r * rows, (r + 1) * rows)
        lane = lax.broadcasted_iota(jnp.int32, (rows, HEAD_DIM), 1)
        logs = jnp.zeros((rows, HEAD_DIM), jnp.float32)
        for h in range(heads):
            cols = slice(h * HEAD_DIM, (h + 1) * HEAD_DIM)
            query = q_all[span, cols]
            s0 = lax.dot_general(query, own[0, :, cols], contract, preferred_element_type=jnp.float32) * temper
            s1 = lax.dot_general(query, prev[0, :, cols], contract, preferred_element_type=jnp.float32) * temper
            top = jnp.max(s0, axis=1, keepdims=True)
            newtop = jnp.maximum(top, jnp.max(s1, axis=1, keepdims=True))
            w0 = jnp.exp(s0 - top)
            w1 = jnp.exp(s1 - newtop)
            factor = jnp.exp(top - newtop)
            total = jnp.sum(w0, axis=1, keepdims=True) * factor + jnp.sum(w1, axis=1, keepdims=True)
            a0 = jnp.dot(w0.astype(jnp.bfloat16), own[1, :, cols], preferred_element_type=jnp.float32)
            a1 = jnp.dot(w1.astype(jnp.bfloat16), prev[1, :, cols], preferred_element_type=jnp.float32)
            out[span, cols] = (a0 * factor + a1) / total
            logs = jnp.where(lane == h, newtop + jnp.log(total), logs)
        stat[:, span] = logs.T
    log_out[...] = stat[:heads, :]


def attend(slots, queries, own, prev, block_len, width):
    count = len(queries)
    heads = width // HEAD_DIM
    rows = math.gcd(block_len, 256)
    flops = 8 * block_len * block_len * width
    return pl.pallas_call(
        functools.partial(attend_kernel, count, heads, rows),
        out_shape=(
            jax.ShapeDtypeStruct((block_len, width), jnp.float32),
            jax.ShapeDtypeStruct((heads, block_len), jnp.float32),
        ),
        in_specs=[pl.BlockSpec(memory_space=pltpu.SMEM)]
        + [pl.BlockSpec(memory_space=pl.ANY)] * (3 * count),
        out_specs=(pl.BlockSpec(memory_space=pltpu.VMEM), pl.BlockSpec(memory_space=pltpu.VMEM)),
        scratch_shapes=[
            pltpu.VMEM((block_len, width), jnp.bfloat16),
            pltpu.VMEM((2, block_len, width), jnp.bfloat16),
            pltpu.VMEM((2, block_len, width), jnp.bfloat16),
            pltpu.VMEM((HEAD_DIM, block_len), jnp.float32),
            pltpu.SemaphoreType.DMA((3,)),
        ],
        compiler_params=pltpu.CompilerParams(vmem_limit_bytes=48 << 20),
        cost_estimate=pl.CostEstimate(
            flops=flops, bytes_accessed=14 * block_len * width, transcendentals=2 * block_len * block_len * heads
        ),
        name="attend",
    )(slots, *queries, *own, *prev)


def shards(qkv):
    count = lax.axis_size("uly")
    me = lax.axis_index("uly")
    width = qkv.shape[2] // count
    block_len = qkv.shape[0] * count
    planes = jnp.transpose(qkv, (1, 0, 2))

    def cut(first, last, k):
        return lax.dynamic_slice_in_dim(planes[first:last], lax.rem(me + k, count) * width, width, 2)

    own = [cut(1, 3, 0)]
    prev = [shift(own[0], "blk", 1)]
    queries = [cut(0, 1, 0)[0]]
    for k in range(1, count):
        own.append(shift(cut(1, 3, k), "uly", k))
    for k in range(1, count):
        prev.append(shift(own[k], "blk", 1))
    for k in range(1, count):
        queries.append(shift(cut(0, 1, k)[0], "uly", k))
    slots = lax.rem(me - jnp.arange(count, dtype=jnp.int32) + count, count)
    return attend(slots, queries, own, prev, block_len, width)


def solution(mesh):
    placed = (P(("blk", "uly"), None, None),)
    return jax.shard_map(
        shards,
        mesh=mesh,
        in_specs=placed,
        out_specs=(P("blk", "uly"), P("uly", "blk")),
        check_vma=False,
    )
```

time: 75 us -> 44 us (0.59)
  the two profiles are of different devices: /device:TPU:0 before, /device:TPU:8 now
where the time goes in v1:
time: 44 us; the launch traced here: 43.8 us
  waiting for transfers between devices  25.4 us (58%)
  starting transfers between devices  10.3 us (23%)
  Pallas kernels  5.04 us (11%)
  local copies, waits for them, and re-layouts  2.34 us (5%)
  between operations  0.72 us (2%)
    ppermute x10, waiting for transfers between devices, shift(): lax.ppermute(value, axis, [(i, (i + steps) % count) for i in range(count)])  25.4 us
    ppermute x10, starting transfers between devices, shift(): lax.ppermute(value, axis, [(i, (i + steps) % count) for i in range(count)])  10.3 us
    pallas_call x1, Pallas kernels, attend(): pl.pallas_call(functools.partial(attend_kernel, count, heads, rows), out_...  5.04 us
    slice x2, local copies, waits for them, and re-layouts, cut(): planes[first:last]  2.21 us
  transfers between devices with their start and end apart: 10, of which 5 were waited for; matrix products, arithmetic and copies ran while one was open for 2% of the time, Pallas kernels for 0%

profile of v1, /device:TPU:8, one launch (start us, length us, event | category | flops | bytes accessed | tf_op | source)
XLA Modules:
  0.0 43.8 jit_solution(1769229188422627172)
XLA Ops:
  0.7 1.2 %slice.7 = bf16[2,64,3072]{2,1,0:T(8,128)(2,1)S(1)} slice(bf16[3,64,3072]{2,1,0:T(8,128)(2,1)} %bitcast.9), slice={[1:3], [0:64], [0:3072]} | slice | bytes 1572864 | tf_op jit(solution)/shard_map/slice | solution.py:100
  1.9 0.1 constant_dynamic-slice_fusion
  2.0 0.1 collective-permute-start.5
  2.0 3.0 %collective-permute-start.4 = (bf16[2,64,768]{2,1,0:T(8,128)(2,1)S(1)}, bf16[2,64,768]{2,1,0:T(8,128)(2,1)S(1)}, u32[]{:S(2)}, u32[]{:S(2)}) collective-permute-start(bf16[2,64,768]{2,1,0:T(8,128)(2,1)S(1)} %get-tuple-element.3), channel_id=1, source_target_pairs={{0,2},{1,3},{2,0},{3,1},{4,6},{5,7},{6,4},{7,5},{8,10},{9,11},{10,... | collective-permute-start | bytes 589832 | tf_op jit(solution)/shard_map/ppermute | solution.py:16
  5.0 2.5 %collective-permute-start.3 = (bf16[2,64,768]{2,1,0:T(8,128)(2,1)S(1)}, bf16[2,64,768]{2,1,0:T(8,128)(2,1)S(1)}, u32[]{:S(2)}, u32[]{:S(2)}) collective-permute-start(bf16[2,64,768]{2,1,0:T(8,128)(2,1)S(1)} %get-tuple-element.4), channel_id=1, source_target_pairs={{0,1},{1,2},{2,3},{3,0},{4,5},{5,6},{6,7},{7,4},{8,9},{9,10},{10,1... | collective-permute-start | bytes 589832 | tf_op jit(solution)/shard_map/ppermute | solution.py:16
  7.5 1.0 %slice.6 = bf16[1,64,3072]{2,1,0:T(8,128)(2,1)S(1)} slice(bf16[3,64,3072]{2,1,0:T(8,128)(2,1)} %bitcast.10), slice={[0:1], [0:64], [0:3072]} | slice | bytes 786432 | tf_op jit(solution)/shard_map/slice | solution.py:100
  8.6 0.1 collective-permute-start.2
  8.7 1.5 %collective-permute-start.1 = (bf16[64,768]{1,0:T(8,128)(2,1)S(1)}, bf16[64,768]{1,0:T(8,128)(2,1)S(1)}, u32[]{:S(2)}, u32[]{:S(2)}) collective-permute-start(bf16[64,768]{1,0:T(8,128)(2,1)S(1)} %get-tuple-element.7), channel_id=1, source_target_pairs={{0,2},{1,3},{2,0},{3,1},{4,6},{5,7},{6,4},{7,5},{8,10},{9,11},{10,... | collective-permute-start | bytes 294920 | tf_op jit(solution)/shard_map/ppermute | solution.py:16
  10.1 16.3 %collective-permute-done.2.refs_4_ = bf16[64,768]{1,0:T(8,128)(2,1)S(1)} collective-permute-done((bf16[64,768]{1,0:T(8,128)(2,1)S(1)}, bf16[64,768]{1,0:T(8,128)(2,1)S(1)}, u32[]{:S(2)}, u32[]{:S(2)}) %collective-permute-start.2) | collective-permute-done | bytes 98336 | tf_op jit(solution)/shard_map/ppermute | solution.py:16
  26.4 0.0 collective-permute-start.6
  26.4 0.0 collective-permute-done.5.refs_8_
  26.4 1.6 %collective-permute-start.9 = (bf16[2,64,768]{2,1,0:T(8,128)(2,1)S(1)}, bf16[2,64,768]{2,1,0:T(8,128)(2,1)S(1)}, u32[]{:S(2)}, u32[]{:S(2)}) collective-permute-start(bf16[2,64,768]{2,1,0:T(8,128)(2,1)S(1)} %collective-permute-done.5.refs_8_), channel_id=1, source_target_pairs={{0,4},{4,8},{8,12},{12,16},{16,20},{20,24},{24,28},{28,0},{1,5},{5... | collective-permute-start | bytes 589832 | tf_op jit(solution)/shard_map/ppermute | solution.py:16
  28.1 0.0 collective-permute-done.4.refs_7_
  28.1 0.1 collective-permute-start.8
  28.1 0.0 collective-permute-done.3.refs_6_
  28.1 1.6 %collective-permute-start.7 = (bf16[2,64,768]{2,1,0:T(8,128)(2,1)S(1)}, bf16[2,64,768]{2,1,0:T(8,128)(2,1)S(1)}, u32[]{:S(2)}, u32[]{:S(2)}) collective-permute-start(bf16[2,64,768]{2,1,0:T(8,128)(2,1)S(1)} %collective-permute-done.3.refs_6_), channel_id=1, source_target_pairs={{0,4},{4,8},{8,12},{12,16},{16,20},{20,24},{24,28},{28,0},{1,5},{5... | collective-permute-start | bytes 589832 | tf_op jit(solution)/shard_map/ppermute | solution.py:16
  29.7 0.0 collective-permute-done.1.refs_3_
  29.7 0.0 collective-permute-start
  29.7 4.7 %collective-permute-done.refs_2_ = bf16[64,768]{1,0:T(8,128)(2,1)S(1)} collective-permute-done((bf16[64,768]{1,0:T(8,128)(2,1)S(1)}, bf16[64,768]{1,0:T(8,128)(2,1)S(1)}, u32[]{:S(2)}, u32[]{:S(2)}) %collective-permute-start) | collective-permute-done | bytes 98336 | tf_op jit(solution)/shard_map/ppermute | solution.py:16
  34.4 0.0 collective-permute-done.6.refs_9_
  34.4 0.1 collective-permute-done.9.refs_12_
  34.5 2.1 %collective-permute-done.8.refs_11_ = bf16[2,64,768]{2,1,0:T(8,128)(2,1)S(1)} collective-permute-done((bf16[2,64,768]{2,1,0:T(8,128)(2,1)S(1)}, bf16[2,64,768]{2,1,0:T(8,128)(2,1)S(1)}, u32[]{:S(2)}, u32[]{:S(2)}) %collective-permute-start.8) | collective-permute-done | bytes 196640 | tf_op jit(solution)/shard_map/ppermute | solution.py:16
  36.6 2.1 %collective-permute-done.7.refs_10_ = bf16[2,64,768]{2,1,0:T(8,128)(2,1)S(1)} collective-permute-done((bf16[2,64,768]{2,1,0:T(8,128)(2,1)S(1)}, bf16[2,64,768]{2,1,0:T(8,128)(2,1)S(1)}, u32[]{:S(2)}, u32[]{:S(2)}) %collective-permute-start.7) | collective-permute-done | bytes 196640 | tf_op jit(solution)/shard_map/ppermute | solution.py:16
  38.8 5.0 %attend.1 = (f32[256,768]{1,0:T(8,128)}, f32[6,256]{1,0:T(8,128)}) custom-call(s32[4]{0:T(128)S(1)} %compare_select_fusion.refs_0_, bf16[64,768]{1,0:T(8,128)(2,1)S(1)} %get-tuple-element.9.refs_1_, bf16[64,768]{1,0:T(8,128)(2,1)S(1)} %collective-permute-done.refs_2_, bf16[64,768]{1,0:T(8,128)(2,1)S(1)} %collective-permute-done.1.refs_3_, ...), custom_call_target="tpu_custom_call" | custom-call | flops 402653184 | bytes 2752512 | tf_op jit(solution)/shard_map/attend/pallas_call | solution.py:68
  (2 shorter events, 0.1 us)
Async XLA Ops:
  2.0 24.5 %collective-permute-start.5 = (bf16[2,64,768]{2,1,0:T(8,128)(2,1)S(1)}, bf16[2,64,768]{2,1,0:T(8,128)(2,1)S(1)}, u32[]{:S(2)}, u32[]{:S(2)}) collective-permute-start(bf16[2,64,768]{2,1,0:T(8,128)(2,1)S(1)} %get-tuple-element.2), channel_id=1, source_target_pairs={{0,3},{1,0},{2,1},{3,2},{4,7},{5,4},{6,5},{7,6},{8,11},{9,8},{10,9... | collective-permute-start | bytes 589832 | tf_op jit(solution)/shard_map/ppermute | solution.py:16
  2.0 26.0 %collective-permute-start.4 = (bf16[2,64,768]{2,1,0:T(8,128)(2,1)S(1)}, bf16[2,64,768]{2,1,0:T(8,128)(2,1)S(1)}, u32[]{:S(2)}, u32[]{:S(2)}) collective-permute-start(bf16[2,64,768]{2,1,0:T(8,128)(2,1)S(1)} %get-tuple-element.3), channel_id=1, source_target_pairs={{0,2},{1,3},{2,0},{3,1},{4,6},{5,7},{6,4},{7,5},{8,10},{9,11},{10,... | collective-permute-start | bytes 589832 | tf_op jit(solution)/shard_map/ppermute | solution.py:16
  5.0 23.1 %collective-permute-start.3 = (bf16[2,64,768]{2,1,0:T(8,128)(2,1)S(1)}, bf16[2,64,768]{2,1,0:T(8,128)(2,1)S(1)}, u32[]{:S(2)}, u32[]{:S(2)}) collective-permute-start(bf16[2,64,768]{2,1,0:T(8,128)(2,1)S(1)} %get-tuple-element.4), channel_id=1, source_target_pairs={{0,1},{1,2},{2,3},{3,0},{4,5},{5,6},{6,7},{7,4},{8,9},{9,10},{10,1... | collective-permute-start | bytes 589832 | tf_op jit(solution)/shard_map/ppermute | solution.py:16
  8.6 17.8 %collective-permute-start.2 = (bf16[64,768]{1,0:T(8,128)(2,1)S(1)}, bf16[64,768]{1,0:T(8,128)(2,1)S(1)}, u32[]{:S(2)}, u32[]{:S(2)}) collective-permute-start(bf16[64,768]{1,0:T(8,128)(2,1)S(1)} %get-tuple-element.6), channel_id=1, source_target_pairs={{0,3},{1,0},{2,1},{3,2},{4,7},{5,4},{6,5},{7,6},{8,11},{9,8},{10,9... | collective-permute-start | bytes 294920 | tf_op jit(solution)/shard_map/ppermute | solution.py:16
  8.7 21.0 %collective-permute-start.1 = (bf16[64,768]{1,0:T(8,128)(2,1)S(1)}, bf16[64,768]{1,0:T(8,128)(2,1)S(1)}, u32[]{:S(2)}, u32[]{:S(2)}) collective-permute-start(bf16[64,768]{1,0:T(8,128)(2,1)S(1)} %get-tuple-element.7), channel_id=1, source_target_pairs={{0,2},{1,3},{2,0},{3,1},{4,6},{5,7},{6,4},{7,5},{8,10},{9,11},{10,... | collective-permute-start | bytes 294920 | tf_op jit(solution)/shard_map/ppermute | solution.py:16
  26.4 8.0 %collective-permute-start.6 = (bf16[2,64,768]{2,1,0:T(8,128)(2,1)S(1)}, bf16[2,64,768]{2,1,0:T(8,128)(2,1)S(1)}, u32[]{:S(2)}, u32[]{:S(2)}) collective-permute-start(bf16[2,64,768]{2,1,0:T(8,128)(2,1)S(1)} %get-tuple-element.5.refs_5_), channel_id=1, source_target_pairs={{0,4},{4,8},{8,12},{12,16},{16,20},{20,24},{24,28},{28,0},{1,5},{5... | collective-permute-start | bytes 589832 | tf_op jit(solution)/shard_map/ppermute | solution.py:16
  26.4 8.1 %collective-permute-start.9 = (bf16[2,64,768]{2,1,0:T(8,128)(2,1)S(1)}, bf16[2,64,768]{2,1,0:T(8,128)(2,1)S(1)}, u32[]{:S(2)}, u32[]{:S(2)}) collective-permute-start(bf16[2,64,768]{2,1,0:T(8,128)(2,1)S(1)} %collective-permute-done.5.refs_8_), channel_id=1, source_target_pairs={{0,4},{4,8},{8,12},{12,16},{16,20},{20,24},{24,28},{28,0},{1,5},{5... | collective-permute-start | bytes 589832 | tf_op jit(solution)/shard_map/ppermute | solution.py:16
  28.1 8.6 %collective-permute-start.8 = (bf16[2,64,768]{2,1,0:T(8,128)(2,1)S(1)}, bf16[2,64,768]{2,1,0:T(8,128)(2,1)S(1)}, u32[]{:S(2)}, u32[]{:S(2)}) collective-permute-start(bf16[2,64,768]{2,1,0:T(8,128)(2,1)S(1)} %collective-permute-done.4.refs_7_), channel_id=1, source_target_pairs={{0,4},{4,8},{8,12},{12,16},{16,20},{20,24},{24,28},{28,0},{1,5},{5... | collective-permute-start | bytes 589832 | tf_op jit(solution)/shard_map/ppermute | solution.py:16
  28.1 10.6 %collective-permute-start.7 = (bf16[2,64,768]{2,1,0:T(8,128)(2,1)S(1)}, bf16[2,64,768]{2,1,0:T(8,128)(2,1)S(1)}, u32[]{:S(2)}, u32[]{:S(2)}) collective-permute-start(bf16[2,64,768]{2,1,0:T(8,128)(2,1)S(1)} %collective-permute-done.3.refs_6_), channel_id=1, source_target_pairs={{0,4},{4,8},{8,12},{12,16},{16,20},{20,24},{24,28},{28,0},{1,5},{5... | collective-permute-start | bytes 589832 | tf_op jit(solution)/shard_map/ppermute | solution.py:16
  29.7 4.8 %collective-permute-start = (bf16[64,768]{1,0:T(8,128)(2,1)S(1)}, bf16[64,768]{1,0:T(8,128)(2,1)S(1)}, u32[]{:S(2)}, u32[]{:S(2)}) collective-permute-start(bf16[64,768]{1,0:T(8,128)(2,1)S(1)} %get-tuple-element.8), channel_id=1, source_target_pairs={{0,1},{1,2},{2,3},{3,0},{4,5},{5,6},{6,7},{7,4},{8,9},{9,10},{10,1... | collective-permute-start | bytes 294920 | tf_op jit(solution)/shard_map/ppermute | solution.py:16

commit v2 on v1

v2 whole, which is shorter than its diff:
```python
import functools
import math

import jax
import jax.numpy as jnp
from jax import lax
from jax.experimental import pallas as pl
from jax.experimental.pallas import tpu as pltpu
from jax.sharding import PartitionSpec as P

HEAD_DIM = 128
TEMPER = 1.0 / math.sqrt(HEAD_DIM)


def shift(value, axis, steps):
    count = lax.axis_size(axis)
    return lax.ppermute(value, axis, [(i, (i + steps) % count) for i in range(count)])


def after(value, *others):
    return lax.optimization_barrier((value, *others))[0]


def stack(parts):
    return parts[0] if len(parts) == 1 else jnp.concatenate(parts, axis=0)


def attend_kernel(count, heads, group, *refs):
    me = lax.axis_index("uly")
    refs = (None, *refs)
    home = refs[1]
    fulls = refs[1:3]
    pairs = refs[3 : 1 + count]
    singles = refs[1 + count : 2 * count - 1]
    prev_home, prev_early, *prev_last = refs[2 * count - 1 : 2 * count + 3]
    out, log_out, result, stat, turned, sem = refs[2 * count + 3 :]
    piece = home.shape[1]
    contract = (((1,), (1,)), ((), ()))

    def rows_of(k):
        slot = jnp.where(me < k, me + (count - k), me - k)
        return pl.ds(pl.multiple_of(slot * piece, piece), piece)

    def queries(k, cols):
        return fulls[k][0, :, cols] if k < 2 else singles[k - 2][:, cols]

    def own(which, cols):
        return stack(
            [ref[1 + which, :, cols] for ref in fulls] + [ref[which, :, cols] for ref in pairs]
        )

    def prev(which, cols):
        parts = [prev_early[i, which, :, cols] for i in range(count - 2)]
        return stack([prev_home[which, :, cols]] + parts + [prev_last[which][:, cols]])

    lane = lax.broadcasted_iota(jnp.int32, (group * piece, HEAD_DIM), 1)
    logs = [jnp.zeros((group * piece, HEAD_DIM), jnp.float32) for _ in range(count // group)]
    copies = []
    for h in range(heads):
        cols = slice(h * HEAD_DIM, (h + 1) * HEAD_DIM)
        own_keys, own_values = own(0, cols), own(1, cols)
        prev_keys, prev_values = prev(0, cols), prev(1, cols)
        for g in range(count // group):
            query = stack([queries(k, cols) for k in range(g * group, (g + 1) * group)])
            s0 = lax.dot_general(query, own_keys, contract, preferred_element_type=jnp.float32)
            s1 = lax.dot_general(query, prev_keys, contract, preferred_element_type=jnp.float32)
            top = jnp.max(s0, axis=1, keepdims=True)
            newtop = jnp.maximum(top, jnp.max(s1, axis=1, keepdims=True))
            scale = TEMPER * math.log2(math.e)
            w0 = jnp.exp2((s0 - top) * scale)
            w1 = jnp.exp2((s1 - newtop) * scale)
            factor = jnp.exp2((top - newtop) * scale)
            total = jnp.sum(w0, axis=1, keepdims=True) * factor + jnp.sum(w1, axis=1, keepdims=True)
            a0 = jnp.dot(w0.astype(jnp.bfloat16), own_values, preferred_element_type=jnp.float32)
            a1 = jnp.dot(w1.astype(jnp.bfloat16), prev_values, preferred_element_type=jnp.float32)
            normed = (a0 * factor + a1) / total
            logs[g] = jnp.where(lane == h, newtop * TEMPER + jnp.log(total), logs[g])
            for i in range(group):
                result[rows_of(g * group + i), cols] = normed[i * piece : (i + 1) * piece]
        copies.append(pltpu.make_async_copy(result.at[:, cols], out.at[:, cols], sem))
        copies[-1].start()
    for g in range(count // group):
        for i in range(group):
            stat[rows_of(g * group + i), :] = logs[g][i * piece : (i + 1) * piece]
    turned[...] = stat[...].T[:heads, :]
    copies.append(pltpu.make_async_copy(turned, log_out, sem))
    copies[-1].start()
    for copy in copies:
        copy.wait()


def attend(fulls, pairs, singles, prevs, block_len, width):
    count = len(pairs) + 2
    heads = width // HEAD_DIM
    group = math.gcd(count, 4)
    in_vmem = pl.BlockSpec(memory_space=pltpu.VMEM)
    return pl.pallas_call(
        functools.partial(attend_kernel, count, heads, group),
        out_shape=(
            jax.ShapeDtypeStruct((block_len, width), jnp.float32),
            jax.ShapeDtypeStruct((heads, block_len), jnp.float32),
        ),
        in_specs=[in_vmem] * (2 * count + 2),
        out_specs=(pl.BlockSpec(memory_space=pl.ANY), pl.BlockSpec(memory_space=pl.ANY)),
        scratch_shapes=[
            pltpu.VMEM((block_len, width), jnp.float32),
            pltpu.VMEM((block_len, HEAD_DIM), jnp.float32),
            pltpu.VMEM((heads, block_len), jnp.float32),
            pltpu.SemaphoreType.DMA(()),
        ],
        compiler_params=pltpu.CompilerParams(vmem_limit_bytes=48 << 20),
        cost_estimate=pl.CostEstimate(
            flops=8 * block_len * block_len * width,
            bytes_accessed=14 * block_len * width,
            transcendentals=2 * block_len * block_len * heads,
        ),
        name="attend",
    )(*fulls, *pairs, *singles, *prevs)


def shards(qkv):
    count = lax.axis_size("uly")
    me = lax.axis_index("uly")
    tokens, planes_count, width = qkv.shape[0], qkv.shape[1], qkv.shape[2] // count
    planes = jnp.transpose(qkv, (1, 0, 2))

    def cut(first, last, k):
        start = jnp.where(me + k < count, me + k, me + k - count) * width
        return lax.dynamic_slice(planes, (first, 0, start), (last - first, tokens, width))

    home = cut(0, planes_count, 0)
    first = shift(cut(0, planes_count, 1), "uly", 1)
    prevs = [shift(home[1:], "blk", 1)]
    last = count // 2
    pairs, singles = [], []
    for k in range(2, count):
        pair, single = cut(1, planes_count, k), cut(0, 1, k)[0]
        pairs.append(shift(after(pair, prevs[0]) if k == last else pair, "uly", k))
        singles.append(shift(after(single, prevs[0]), "uly", k))
    early = [first[1:]] + [pair for k, pair in enumerate(pairs, 2) if k != last]
    prevs.append(shift(jnp.stack(early), "blk", 1))
    prevs += [shift(pairs[last - 2][i], "blk", 1) for i in range(2)]
    return attend([home, first], pairs, singles, prevs, tokens * count, width)


def solution(mesh):
    placed = (P(("blk", "uly"), None, None),)
    return jax.shard_map(
        shards,
        mesh=mesh,
        in_specs=placed,
        out_specs=(P("blk", "uly"), P("uly", "blk")),
        check_vma=False,
    )
```

time: 44 us -> 37.2 us (0.85)
  the two profiles are of different devices: /device:TPU:8 before, /device:TPU:0 now
where the time goes in v2:
time: 37.2 us; the launch traced here: 37.1 us
  waiting for transfers between devices  16.4 us (44%)
  starting transfers between devices  16 us (43%)
  Pallas kernels  2.65 us (7%)
  local copies, waits for them, and re-layouts  1.29 us (3%)
  between operations  0.73 us (2%)
    ppermute x9, waiting for transfers between devices, shift(): lax.ppermute(value, axis, [(i, (i + steps) % count) for i in range(count)])  16.4 us
    ppermute x9, starting transfers between devices, shift(): lax.ppermute(value, axis, [(i, (i + steps) % count) for i in range(count)])  16 us
    pallas_call x1, Pallas kernels, attend(): pl.pallas_call(functools.partial(attend_kernel, count, heads, group), out...  2.65 us
    dynamic_slice x2, local copies, waits for them, and re-layouts, cut(): lax.dynamic_slice(planes, (first, 0, start), (last - first, tokens, width))  1.23 us
  transfers between devices with their start and end apart: 9, of which 8 were waited for; matrix products, arithmetic and copies ran while one was open for 0% of the time, Pallas kernels for 0%

profile of v2, /device:TPU:0, one launch (start us, length us, event | category | flops | bytes accessed | tf_op | source)
XLA Modules:
  0.0 37.1 jit_solution(4755048962258491010)
XLA Ops:
  0.6 0.0 copy-start
  0.7 1.2 %dynamic-slice_bitcast_fusion = (bf16[3,64,768]{2,1,0:T(8,128)(2,1)S(1)}, bf16[3,64,768]{2,1,0:T(8,128)(2,1)S(1)}) fusion(bf16[64,3,3072]{2,0,1:T(8,128)(2,1)} %param.1, s32[]{:T(128)S(6)} %select_n.32, s32[]{:T(128)S(6)} %select_n.30), kind=kLoop, calls=%fused_computation.1 | loop fusion | bytes 1179656 | tf_op jit(solution)/shard_map/dynamic_slice | solution.py:129
  1.8 3.1 %collective-permute-start = (bf16[3,64,768]{2,1,0:T(8,128)(2,1)S(1)}, bf16[3,64,768]{2,1,0:T(8,128)(2,1)S(1)}, u32[]{:S(2)}, u32[]{:S(2)}) collective-permute-start(bf16[3,64,768]{2,1,0:T(8,128)(2,1)S(1)} %get-tuple-element.12), channel_id=1, source_target_pairs={{0,1},{1,2},{2,3},{3,0},{4,5},{5,6},{6,7},{7,4},{8,9},{9,10},{10,1... | collective-permute-start | bytes 884744 | tf_op jit(solution)/shard_map/ppermute | solution.py:17
  4.9 0.1 collective-permute-start.1
  5.0 0.0 copy-done
  5.1 2.1 %collective-permute-start.3 = (bf16[2,64,768]{2,1,0:T(8,128)(2,1)S(1)}, bf16[2,64,768]{2,1,0:T(8,128)(2,1)S(1)}, u32[]{:S(2)}, u32[]{:S(2)}) collective-permute-start(bf16[2,64,768]{2,1,0:T(8,128)(2,1)S(1)} %get-tuple-element.10), channel_id=1, source_target_pairs={{0,3},{1,0},{2,1},{3,2},{4,7},{5,4},{6,5},{7,6},{8,11},{9,8},{10,9... | collective-permute-start | bytes 589832 | tf_op jit(solution)/shard_map/ppermute | solution.py:17
  7.2 3.8 %collective-permute-done.1.refs_6_ = bf16[2,64,768]{2,1,0:T(8,128)(2,1)S(1)} collective-permute-done((bf16[2,64,768]{2,1,0:T(8,128)(2,1)S(1)}, bf16[2,64,768]{2,1,0:T(8,128)(2,1)S(1)}, u32[]{:S(2)}, u32[]{:S(2)}) %collective-permute-start.1) | collective-permute-done | bytes 196640 | tf_op jit(solution)/shard_map/ppermute | solution.py:17
  11.0 2.6 %collective-permute-start.2 = (bf16[2,64,768]{2,1,0:T(8,128)(2,1)S(1)}, bf16[2,64,768]{2,1,0:T(8,128)(2,1)S(1)}, u32[]{:S(2)}, u32[]{:S(2)}) collective-permute-start(bf16[2,64,768]{2,1,0:T(8,128)(2,1)S(1)} %get-tuple-element.5), channel_id=1, source_target_pairs={{0,2},{1,3},{2,0},{3,1},{4,6},{5,7},{6,4},{7,5},{8,10},{9,11},{10,... | collective-permute-start | bytes 589832 | tf_op jit(solution)/shard_map/ppermute | solution.py:17
  13.6 1.3 %collective-permute-done.refs_1_ = bf16[3,64,768]{2,1,0:T(8,128)(2,1)S(1)} collective-permute-done((bf16[3,64,768]{2,1,0:T(8,128)(2,1)S(1)}, bf16[3,64,768]{2,1,0:T(8,128)(2,1)S(1)}, u32[]{:S(2)}, u32[]{:S(2)}) %collective-permute-start) | collective-permute-done | bytes 294944 | tf_op jit(solution)/shard_map/ppermute | solution.py:17
  14.8 3.3 %collective-permute-done.3.refs_3_ = bf16[2,64,768]{2,1,0:T(8,128)(2,1)S(1)} collective-permute-done((bf16[2,64,768]{2,1,0:T(8,128)(2,1)S(1)}, bf16[2,64,768]{2,1,0:T(8,128)(2,1)S(1)}, u32[]{:S(2)}, u32[]{:S(2)}) %collective-permute-start.3) | collective-permute-done | bytes 196640 | tf_op jit(solution)/shard_map/ppermute | solution.py:17
  18.2 0.2 collective-permute-start.6
  18.3 5.9 %collective-permute-start.4 = (bf16[64,768]{1,0:T(8,128)(2,1)S(1)}, bf16[64,768]{1,0:T(8,128)(2,1)S(1)}, u32[]{:S(2)}, u32[]{:S(2)}) collective-permute-start(bf16[64,768]{1,0:T(8,128)(2,1)S(1)} %get-tuple-element.6), channel_id=1, source_target_pairs={{0,2},{1,3},{2,0},{3,1},{4,6},{5,7},{6,4},{7,5},{8,10},{9,11},{10,... | collective-permute-start | bytes 294920 | tf_op jit(solution)/shard_map/ppermute | solution.py:17
  24.2 0.4 %collective-permute-start.5 = (bf16[64,768]{1,0:T(8,128)(2,1)S(1)}, bf16[64,768]{1,0:T(8,128)(2,1)S(1)}, u32[]{:S(2)}, u32[]{:S(2)}) collective-permute-start(bf16[64,768]{1,0:T(8,128)(2,1)S(1)} %get-tuple-element.7), channel_id=1, source_target_pairs={{0,3},{1,0},{2,1},{3,2},{4,7},{5,4},{6,5},{7,6},{8,11},{9,8},{10,9... | collective-permute-start | bytes 294920 | tf_op jit(solution)/shard_map/ppermute | solution.py:17
  24.7 3.7 %collective-permute-done.2.refs_2_ = bf16[2,64,768]{2,1,0:T(8,128)(2,1)S(1)} collective-permute-done((bf16[2,64,768]{2,1,0:T(8,128)(2,1)S(1)}, bf16[2,64,768]{2,1,0:T(8,128)(2,1)S(1)}, u32[]{:S(2)}, u32[]{:S(2)}) %collective-permute-start.2) | collective-permute-done | bytes 196640 | tf_op jit(solution)/shard_map/ppermute | solution.py:17
  28.4 0.4 %collective-permute-start.8 = (bf16[64,768]{1,0:T(8,128)(2,1)S(1)}, bf16[64,768]{1,0:T(8,128)(2,1)S(1)}, u32[]{:S(2)}, u32[]{:S(2)}) collective-permute-start(bf16[64,768]{1,0:T(8,128)(2,1)S(1)} %get-tuple-element.14), channel_id=1, source_target_pairs={{0,4},{4,8},{8,12},{12,16},{16,20},{20,24},{24,28},{28,0},{1,5},{5... | collective-permute-start | bytes 294920 | tf_op jit(solution)/shard_map/ppermute | solution.py:17
  28.8 1.3 %collective-permute-start.7 = (bf16[64,768]{1,0:T(8,128)(2,1)S(1)}, bf16[64,768]{1,0:T(8,128)(2,1)S(1)}, u32[]{:S(2)}, u32[]{:S(2)}) collective-permute-start(bf16[64,768]{1,0:T(8,128)(2,1)S(1)} %get-tuple-element.15), channel_id=1, source_target_pairs={{0,4},{4,8},{8,12},{12,16},{16,20},{20,24},{24,28},{28,0},{1,5},{5... | collective-permute-start | bytes 294920 | tf_op jit(solution)/shard_map/ppermute | solution.py:17
  30.1 0.8 %collective-permute-done.4.refs_4_ = bf16[64,768]{1,0:T(8,128)(2,1)S(1)} collective-permute-done((bf16[64,768]{1,0:T(8,128)(2,1)S(1)}, bf16[64,768]{1,0:T(8,128)(2,1)S(1)}, u32[]{:S(2)}, u32[]{:S(2)}) %collective-permute-start.4) | collective-permute-done | bytes 98336 | tf_op jit(solution)/shard_map/ppermute | solution.py:17
  30.9 1.2 %collective-permute-done.5.refs_5_ = bf16[64,768]{1,0:T(8,128)(2,1)S(1)} collective-permute-done((bf16[64,768]{1,0:T(8,128)(2,1)S(1)}, bf16[64,768]{1,0:T(8,128)(2,1)S(1)}, u32[]{:S(2)}, u32[]{:S(2)}) %collective-permute-start.5) | collective-permute-done | bytes 98336 | tf_op jit(solution)/shard_map/ppermute | solution.py:17
  32.1 1.3 %collective-permute-done.8.refs_9_ = bf16[64,768]{1,0:T(8,128)(2,1)S(1)} collective-permute-done((bf16[64,768]{1,0:T(8,128)(2,1)S(1)}, bf16[64,768]{1,0:T(8,128)(2,1)S(1)}, u32[]{:S(2)}, u32[]{:S(2)}) %collective-permute-start.8) | collective-permute-done | bytes 98336 | tf_op jit(solution)/shard_map/ppermute | solution.py:17
  33.4 1.1 %collective-permute-done.7.refs_8_ = bf16[64,768]{1,0:T(8,128)(2,1)S(1)} collective-permute-done((bf16[64,768]{1,0:T(8,128)(2,1)S(1)}, bf16[64,768]{1,0:T(8,128)(2,1)S(1)}, u32[]{:S(2)}, u32[]{:S(2)}) %collective-permute-start.7) | collective-permute-done | bytes 98336 | tf_op jit(solution)/shard_map/ppermute | solution.py:17
  34.4 0.0 collective-permute-done.6.refs_7_
  34.4 2.7 %attend.1 = (f32[256,768]{1,0:T(8,128)}, f32[6,256]{1,0:T(8,128)}) custom-call(bf16[3,64,768]{2,1,0:T(8,128)(2,1)S(1)} %get-tuple-element.13.refs_0_, bf16[3,64,768]{2,1,0:T(8,128)(2,1)S(1)} %collective-permute-done.refs_1_, bf16[2,64,768]{2,1,0:T(8,128)(2,1)S(1)} %collective-permute-done.2.refs_2_, bf16[2,64,768]{2,1,0:T(8,128)(2,1)S(1)} %collective-permute-done.3.refs_3_, ...), custom_call_target="tpu_custom_call" | custom-call | flops 402653184 | bytes 2752512 | tf_op jit(solution)/shard_map/attend/pallas_call | solution.py:97
  (6 shorter events, 0.1 us)
Async XLA Ops:
  0.6 4.4 %copy-start = (bf16[64,3,3072]{2,0,1:T(8,128)(2,1)S(1)}, bf16[64,3,3072]{2,0,1:T(8,128)(2,1)}, u32[]{:S(2)}) copy-start(bf16[64,3,3072]{2,0,1:T(8,128)(2,1)} %param.1) | copy-start | bytes 3538948
  1.8 13.0 %collective-permute-start = (bf16[3,64,768]{2,1,0:T(8,128)(2,1)S(1)}, bf16[3,64,768]{2,1,0:T(8,128)(2,1)S(1)}, u32[]{:S(2)}, u32[]{:S(2)}) collective-permute-start(bf16[3,64,768]{2,1,0:T(8,128)(2,1)S(1)} %get-tuple-element.12), channel_id=1, source_target_pairs={{0,1},{1,2},{2,3},{3,0},{4,5},{5,6},{6,7},{7,4},{8,9},{9,10},{10,1... | collective-permute-start | bytes 884744 | tf_op jit(solution)/shard_map/ppermute | solution.py:17
  4.9 6.0 %collective-permute-start.1 = (bf16[2,64,768]{2,1,0:T(8,128)(2,1)S(1)}, bf16[2,64,768]{2,1,0:T(8,128)(2,1)S(1)}, u32[]{:S(2)}, u32[]{:S(2)}) collective-permute-start(bf16[2,64,768]{2,1,0:T(8,128)(2,1)S(1)} %slice.16), channel_id=1, source_target_pairs={{0,4},{4,8},{8,12},{12,16},{16,20},{20,24},{24,28},{28,0},{1,5},{5... | collective-permute-start | bytes 589832 | tf_op jit(solution)/shard_map/ppermute | solution.py:17
  5.1 13.0 %collective-permute-start.3 = (bf16[2,64,768]{2,1,0:T(8,128)(2,1)S(1)}, bf16[2,64,768]{2,1,0:T(8,128)(2,1)S(1)}, u32[]{:S(2)}, u32[]{:S(2)}) collective-permute-start(bf16[2,64,768]{2,1,0:T(8,128)(2,1)S(1)} %get-tuple-element.10), channel_id=1, source_target_pairs={{0,3},{1,0},{2,1},{3,2},{4,7},{5,4},{6,5},{7,6},{8,11},{9,8},{10,9... | collective-permute-start | bytes 589832 | tf_op jit(solution)/shard_map/ppermute | solution.py:17
  11.0 17.4 %collective-permute-start.2 = (bf16[2,64,768]{2,1,0:T(8,128)(2,1)S(1)}, bf16[2,64,768]{2,1,0:T(8,128)(2,1)S(1)}, u32[]{:S(2)}, u32[]{:S(2)}) collective-permute-start(bf16[2,64,768]{2,1,0:T(8,128)(2,1)S(1)} %get-tuple-element.5), channel_id=1, source_target_pairs={{0,2},{1,3},{2,0},{3,1},{4,6},{5,7},{6,4},{7,5},{8,10},{9,11},{10,... | collective-permute-start | bytes 589832 | tf_op jit(solution)/shard_map/ppermute | solution.py:17
  18.2 16.3 %collective-permute-start.6 = (bf16[2,2,64,768]{3,2,1,0:T(8,128)(2,1)S(1)}, bf16[2,2,64,768]{3,2,1,0:T(8,128)(2,1)S(1)}, u32[]{:S(2)}, u32[]{:S(2)}) collective-permute-start(bf16[2,2,64,768]{3,2,1,0:T(8,128)(2,1)S(1)} %pad_maximum_fusion), channel_id=1, source_target_pairs={{0,4},{4,8},{8,12},{12,16},{16,20},{20,24},{24,28},{28,0},{1,5},{5... | collective-permute-start | bytes 1179656 | tf_op jit(solution)/shard_map/ppermute | solution.py:17
  18.3 12.5 %collective-permute-start.4 = (bf16[64,768]{1,0:T(8,128)(2,1)S(1)}, bf16[64,768]{1,0:T(8,128)(2,1)S(1)}, u32[]{:S(2)}, u32[]{:S(2)}) collective-permute-start(bf16[64,768]{1,0:T(8,128)(2,1)S(1)} %get-tuple-element.6), channel_id=1, source_target_pairs={{0,2},{1,3},{2,0},{3,1},{4,6},{5,7},{6,4},{7,5},{8,10},{9,11},{10,... | collective-permute-start | bytes 294920 | tf_op jit(solution)/shard_map/ppermute | solution.py:17
  24.2 7.8 %collective-permute-start.5 = (bf16[64,768]{1,0:T(8,128)(2,1)S(1)}, bf16[64,768]{1,0:T(8,128)(2,1)S(1)}, u32[]{:S(2)}, u32[]{:S(2)}) collective-permute-start(bf16[64,768]{1,0:T(8,128)(2,1)S(1)} %get-tuple-element.7), channel_id=1, source_target_pairs={{0,3},{1,0},{2,1},{3,2},{4,7},{5,4},{6,5},{7,6},{8,11},{9,8},{10,9... | collective-permute-start | bytes 294920 | tf_op jit(solution)/shard_map/ppermute | solution.py:17
  28.4 5.0 %collective-permute-start.8 = (bf16[64,768]{1,0:T(8,128)(2,1)S(1)}, bf16[64,768]{1,0:T(8,128)(2,1)S(1)}, u32[]{:S(2)}, u32[]{:S(2)}) collective-permute-start(bf16[64,768]{1,0:T(8,128)(2,1)S(1)} %get-tuple-element.14), channel_id=1, source_target_pairs={{0,4},{4,8},{8,12},{12,16},{16,20},{20,24},{24,28},{28,0},{1,5},{5... | collective-permute-start | bytes 294920 | tf_op jit(solution)/shard_map/ppermute | solution.py:17
  28.8 5.7 %collective-permute-start.7 = (bf16[64,768]{1,0:T(8,128)(2,1)S(1)}, bf16[64,768]{1,0:T(8,128)(2,1)S(1)}, u32[]{:S(2)}, u32[]{:S(2)}) collective-permute-start(bf16[64,768]{1,0:T(8,128)(2,1)S(1)} %get-tuple-element.15), channel_id=1, source_target_pairs={{0,4},{4,8},{8,12},{12,16},{16,20},{20,24},{24,28},{28,0},{1,5},{5... | collective-permute-start | bytes 294920 | tf_op jit(solution)/shard_map/ppermute | solution.py:17

commit v3 on v2

v3 whole, which is shorter than its diff:
```python
import functools
import math

import jax
import jax.numpy as jnp
from jax import lax
from jax.experimental import pallas as pl
from jax.experimental.pallas import tpu as pltpu
from jax.sharding import PartitionSpec as P

HEAD_DIM = 128
TEMPER = 1.0 / math.sqrt(HEAD_DIM)
SCALE = TEMPER * math.log2(math.e)
CONTRACT = (((1,), (1,)), ((), ()))


def shift(value, axis, steps):
    count = lax.axis_size(axis)
    return lax.ppermute(value, axis, [(i, (i + steps) % count) for i in range(count)])


def after(value, *others):
    return lax.optimization_barrier((value, *others))[0]


def stack(parts):
    return parts[0] if len(parts) == 1 else jnp.concatenate(parts, axis=0)


def own_kernel(count, heads, group, *refs):
    fulls = refs[:2]
    pairs = refs[2:count]
    singles = refs[count : 2 * count - 2]
    accum, top_out, total_out = refs[2 * count - 2 :]
    piece = fulls[0].shape[1]
    rows = group * piece

    def queries(k, cols):
        return fulls[k][0, :, cols] if k < 2 else singles[k - 2][:, cols]

    def own(which, cols):
        return stack(
            [ref[1 + which, :, cols] for ref in fulls] + [ref[which, :, cols] for ref in pairs]
        )

    for h in range(heads):
        cols = slice(h * HEAD_DIM, (h + 1) * HEAD_DIM)
        keys, values = own(0, cols), own(1, cols)
        for g in range(count // group):
            query = stack([queries(k, cols) for k in range(g * group, (g + 1) * group)])
            scores = lax.dot_general(query, keys, CONTRACT, preferred_element_type=jnp.float32)
            top = jnp.max(scores, axis=1, keepdims=True)
            weights = jnp.exp2((scores - top) * SCALE)
            total = jnp.sum(weights, axis=1, keepdims=True)
            span = slice(g * rows, (g + 1) * rows)
            accum[span, cols] = jnp.dot(
                weights.astype(jnp.bfloat16), values, preferred_element_type=jnp.float32
            )
            top_out[span, cols] = jnp.broadcast_to(top, (rows, HEAD_DIM))
            total_out[span, cols] = jnp.broadcast_to(total, (rows, HEAD_DIM))


def prev_kernel(count, heads, group, *refs):
    me = lax.axis_index("uly")
    fulls = refs[:2]
    singles = refs[2:count]
    prev_home, prev_early, *prev_last = refs[count : count + 4]
    accum, top_in, total_in, out, log_out, result, stat, turned, sem = refs[count + 4 :]
    piece = fulls[0].shape[1]
    rows = group * piece

    def rows_of(k):
        slot = jnp.where(me < k, me + (count - k), me - k)
        return pl.ds(pl.multiple_of(slot * piece, piece), piece)

    def queries(k, cols):
        return fulls[k][0, :, cols] if k < 2 else singles[k - 2][:, cols]

    def prev(which, cols):
        parts = [prev_early[i, which, :, cols] for i in range(count - 2)]
        return stack([prev_home[which, :, cols]] + parts + [prev_last[which][:, cols]])

    lane = lax.broadcasted_iota(jnp.int32, (rows, HEAD_DIM), 1)
    logs = [jnp.zeros((rows, HEAD_DIM), jnp.float32)] * (count // group)
    copies = []
    for h in range(heads):
        cols = slice(h * HEAD_DIM, (h + 1) * HEAD_DIM)
        keys, values = prev(0, cols), prev(1, cols)
        for g in range(count // group):
            span = slice(g * rows, (g + 1) * rows)
            query = stack([queries(k, cols) for k in range(g * group, (g + 1) * group)])
            scores = lax.dot_general(query, keys, CONTRACT, preferred_element_type=jnp.float32)
            top, total = top_in[span, cols], total_in[span, cols]
            newtop = jnp.maximum(top, jnp.max(scores, axis=1, keepdims=True))
            wide = jnp.concatenate([newtop] * (scores.shape[1] // HEAD_DIM), axis=1)
            weights = jnp.exp2((scores - wide) * SCALE)
            factor = jnp.exp2((top - newtop) * SCALE)
            total = total * factor + jnp.sum(weights, axis=1, keepdims=True)
            added = jnp.dot(weights.astype(jnp.bfloat16), values, preferred_element_type=jnp.float32)
            normed = (accum[span, cols] * factor + added) / total
            logs[g] = jnp.where(lane == h, newtop * TEMPER + jnp.log(total), logs[g])
            for i in range(group):
                result[rows_of(g * group + i), cols] = normed[i * piece : (i + 1) * piece]
        copies.append(pltpu.make_async_copy(result.at[:, cols], out.at[:, cols], sem))
        copies[-1].start()
    for g in range(count // group):
        for i in range(group):
            stat[rows_of(g * group + i), :] = logs[g][i * piece : (i + 1) * piece]
    turned[...] = stat[...].T[:heads, :]
    copies.append(pltpu.make_async_copy(turned, log_out, sem))
    copies[-1].start()
    for copy in copies:
        copy.wait()


def cost(block_len, width):
    return pl.CostEstimate(
        flops=4 * block_len * block_len * width,
        bytes_accessed=7 * block_len * width,
        transcendentals=block_len * block_len * width // HEAD_DIM,
    )


def attend(fulls, pairs, singles, prevs, block_len, width):
    count = len(pairs) + 2
    heads = width // HEAD_DIM
    group = math.gcd(count, 4)
    in_vmem = pl.BlockSpec(memory_space=pltpu.VMEM)
    whole = jax.ShapeDtypeStruct((block_len, width), jnp.float32)
    running = pl.pallas_call(
        functools.partial(own_kernel, count, heads, group),
        out_shape=(whole, whole, whole),
        in_specs=[in_vmem] * (2 * count - 2),
        out_specs=(in_vmem,) * 3,
        compiler_params=pltpu.CompilerParams(vmem_limit_bytes=24 << 20),
        cost_estimate=cost(block_len, width),
        name="attend_own",
    )(*fulls, *pairs, *singles)
    return pl.pallas_call(
        functools.partial(prev_kernel, count, heads, group),
        out_shape=(whole, jax.ShapeDtypeStruct((heads, block_len), jnp.float32)),
        in_specs=[in_vmem] * (count + 7),
        out_specs=(pl.BlockSpec(memory_space=pl.ANY), pl.BlockSpec(memory_space=pl.ANY)),
        scratch_shapes=[
            pltpu.VMEM((block_len, width), jnp.float32),
            pltpu.VMEM((block_len, HEAD_DIM), jnp.float32),
            pltpu.VMEM((heads, block_len), jnp.float32),
            pltpu.SemaphoreType.DMA(()),
        ],
        compiler_params=pltpu.CompilerParams(vmem_limit_bytes=24 << 20),
        cost_estimate=cost(block_len, width),
        name="attend_prev",
    )(*fulls, *singles, *prevs, *running)


def shards(qkv):
    count = lax.axis_size("uly")
    me = lax.axis_index("uly")
    tokens, planes_count, width = qkv.shape[0], qkv.shape[1], qkv.shape[2] // count
    planes = jnp.transpose(qkv, (1, 0, 2))

    def cut(first, last, k):
        start = jnp.where(me + k < count, me + k, me + k - count) * width
        return lax.dynamic_slice(planes, (first, 0, start), (last - first, tokens, width))

    home = cut(0, planes_count, 0)
    first = shift(cut(0, planes_count, 1), "uly", 1)
    prevs = [shift(home[1:], "blk", 1)]
    last = count // 2
    pairs, singles = [], []
    for k in range(2, count):
        pair, single = cut(1, planes_count, k), cut(0, 1, k)[0]
        pairs.append(shift(after(pair, prevs[0]) if k == last else pair, "uly", k))
        singles.append(shift(after(single, prevs[0]), "uly", k))
    early = [first[1:]] + [pair for k, pair in enumerate(pairs, 2) if k != last]
    prevs.append(shift(jnp.stack(early), "blk", 1))
    prevs += [shift(pairs[last - 2][i], "blk", 1) for i in range(2)]
    return attend([home, first], pairs, singles, prevs, tokens * count, width)


def solution(mesh):
    placed = (P(("blk", "uly"), None, None),)
    return jax.shard_map(
        shards,
        mesh=mesh,
        in_specs=placed,
        out_specs=(P("blk", "uly"), P("uly", "blk")),
        check_vma=False,
    )
```

time: 37.2 us -> 36.4 us (0.978)
  waiting for transfers between devices: 16.4 us -> 15.4 us
    ppermute x9, waiting for transfers between devices: 16.4 us -> 15.4 us  [shift(): lax.ppermute(value, axis, [(i, (i + steps) % count) for i in range(count)])]
    pallas_call x1 -> x2, Pallas kernels: 2.65 us -> 2.78 us  [the longest x1 1.81 us: attend(): pl.pallas_call(functools.partial(prev_kernel, count, heads, group), out_s...]
  transfers between devices with their start and end apart: 9 -> 9, of which waited for: 8 -> 8; matrix products, arithmetic and copies ran while one was open for 0% -> 0% of each run, Pallas kernels for 0% -> 3%
where the time goes in v3:
time: 36.4 us; the launch traced here: 36.3 us
  starting transfers between devices  16 us (44%)
  waiting for transfers between devices  15.4 us (42%)
  Pallas kernels  2.78 us (8%)
  local copies, waits for them, and re-layouts  1.29 us (4%)
  between operations  0.74 us (2%)
    ppermute x9, starting transfers between devices, shift(): lax.ppermute(value, axis, [(i, (i + steps) % count) for i in range(count)])  16 us
    ppermute x9, waiting for transfers between devices, shift(): lax.ppermute(value, axis, [(i, (i + steps) % count) for i in range(count)])  15.4 us
    pallas_call x1, Pallas kernels, attend(): pl.pallas_call(functools.partial(prev_kernel, count, heads, group), out_s...  1.81 us
    dynamic_slice x2, local copies, waits for them, and re-layouts, cut(): lax.dynamic_slice(planes, (first, 0, start), (last - first, tokens, width))  1.23 us
    pallas_call x1, Pallas kernels, attend(): pl.pallas_call(functools.partial(own_kernel, count, heads, group), out_sh...  0.97 us
  transfers between devices with their start and end apart: 9, of which 8 were waited for; matrix products, arithmetic and copies ran while one was open for 0% of the time, Pallas kernels for 3%

profile of v3, /device:TPU:0, one launch (start us, length us, event | category | flops | bytes accessed | tf_op | source)
XLA Modules:
  0.0 36.3 jit_solution(16383167842985315757)
XLA Ops:
  0.6 0.0 copy-start
  0.7 1.2 %dynamic-slice_bitcast_fusion = (bf16[3,64,768]{2,1,0:T(8,128)(2,1)S(1)}, bf16[3,64,768]{2,1,0:T(8,128)(2,1)S(1)}) fusion(bf16[64,3,3072]{2,0,1:T(8,128)(2,1)} %param.1, s32[]{:T(128)S(6)} %select_n.32, s32[]{:T(128)S(6)} %select_n.30), kind=kLoop, calls=%fused_computation.1 | loop fusion | bytes 1179656 | tf_op jit(solution)/shard_map/dynamic_slice | solution.py:164
  1.8 3.1 %collective-permute-start = (bf16[3,64,768]{2,1,0:T(8,128)(2,1)S(1)}, bf16[3,64,768]{2,1,0:T(8,128)(2,1)S(1)}, u32[]{:S(2)}, u32[]{:S(2)}) collective-permute-start(bf16[3,64,768]{2,1,0:T(8,128)(2,1)S(1)} %get-tuple-element.18), channel_id=1, source_target_pairs={{0,1},{1,2},{2,3},{3,0},{4,5},{5,6},{6,7},{7,4},{8,9},{9,10},{10,1... | collective-permute-start | bytes 884744 | tf_op jit(solution)/shard_map/ppermute | solution.py:19
  4.9 0.1 collective-permute-start.1
  5.0 0.0 copy-done
  5.1 2.1 %collective-permute-start.4 = (bf16[2,64,768]{2,1,0:T(8,128)(2,1)S(1)}, bf16[2,64,768]{2,1,0:T(8,128)(2,1)S(1)}, u32[]{:S(2)}, u32[]{:S(2)}) collective-permute-start(bf16[2,64,768]{2,1,0:T(8,128)(2,1)S(1)} %get-tuple-element.15), channel_id=1, source_target_pairs={{0,3},{1,0},{2,1},{3,2},{4,7},{5,4},{6,5},{7,6},{8,11},{9,8},{10,9... | collective-permute-start | bytes 589832 | tf_op jit(solution)/shard_map/ppermute | solution.py:19
  7.2 3.8 %collective-permute-done.1.refs_4_ = bf16[2,64,768]{2,1,0:T(8,128)(2,1)S(1)} collective-permute-done((bf16[2,64,768]{2,1,0:T(8,128)(2,1)S(1)}, bf16[2,64,768]{2,1,0:T(8,128)(2,1)S(1)}, u32[]{:S(2)}, u32[]{:S(2)}) %collective-permute-start.1) | collective-permute-done | bytes 196640 | tf_op jit(solution)/shard_map/ppermute | solution.py:19
  11.0 2.6 %collective-permute-start.6 = (bf16[2,64,768]{2,1,0:T(8,128)(2,1)S(1)}, bf16[2,64,768]{2,1,0:T(8,128)(2,1)S(1)}, u32[]{:S(2)}, u32[]{:S(2)}) collective-permute-start(bf16[2,64,768]{2,1,0:T(8,128)(2,1)S(1)} %get-tuple-element.10), channel_id=1, source_target_pairs={{0,2},{1,3},{2,0},{3,1},{4,6},{5,7},{6,4},{7,5},{8,10},{9,11},{10,... | collective-permute-start | bytes 589832 | tf_op jit(solution)/shard_map/ppermute | solution.py:19
  13.6 1.3 %collective-permute-done.refs_1_ = bf16[3,64,768]{2,1,0:T(8,128)(2,1)S(1)} collective-permute-done((bf16[3,64,768]{2,1,0:T(8,128)(2,1)S(1)}, bf16[3,64,768]{2,1,0:T(8,128)(2,1)S(1)}, u32[]{:S(2)}, u32[]{:S(2)}) %collective-permute-start) | collective-permute-done | bytes 294944 | tf_op jit(solution)/shard_map/ppermute | solution.py:19
  14.8 3.3 %collective-permute-done.4.refs_3_ = bf16[2,64,768]{2,1,0:T(8,128)(2,1)S(1)} collective-permute-done((bf16[2,64,768]{2,1,0:T(8,128)(2,1)S(1)}, bf16[2,64,768]{2,1,0:T(8,128)(2,1)S(1)}, u32[]{:S(2)}, u32[]{:S(2)}) %collective-permute-start.4) | collective-permute-done | bytes 196640 | tf_op jit(solution)/shard_map/ppermute | solution.py:19
  18.2 0.2 collective-permute-start.5
  18.3 5.9 %collective-permute-start.2 = (bf16[64,768]{1,0:T(8,128)(2,1)S(1)}, bf16[64,768]{1,0:T(8,128)(2,1)S(1)}, u32[]{:S(2)}, u32[]{:S(2)}) collective-permute-start(bf16[64,768]{1,0:T(8,128)(2,1)S(1)} %get-tuple-element.8), channel_id=1, source_target_pairs={{0,2},{1,3},{2,0},{3,1},{4,6},{5,7},{6,4},{7,5},{8,10},{9,11},{10,... | collective-permute-start | bytes 294920 | tf_op jit(solution)/shard_map/ppermute | solution.py:19
  24.2 0.4 %collective-permute-start.3 = (bf16[64,768]{1,0:T(8,128)(2,1)S(1)}, bf16[64,768]{1,0:T(8,128)(2,1)S(1)}, u32[]{:S(2)}, u32[]{:S(2)}) collective-permute-start(bf16[64,768]{1,0:T(8,128)(2,1)S(1)} %get-tuple-element.9), channel_id=1, source_target_pairs={{0,3},{1,0},{2,1},{3,2},{4,7},{5,4},{6,5},{7,6},{8,11},{9,8},{10,9... | collective-permute-start | bytes 294920 | tf_op jit(solution)/shard_map/ppermute | solution.py:19
  24.7 3.7 %collective-permute-done.6.refs_2_ = bf16[2,64,768]{2,1,0:T(8,128)(2,1)S(1)} collective-permute-done((bf16[2,64,768]{2,1,0:T(8,128)(2,1)S(1)}, bf16[2,64,768]{2,1,0:T(8,128)(2,1)S(1)}, u32[]{:S(2)}, u32[]{:S(2)}) %collective-permute-start.6) | collective-permute-done | bytes 196640 | tf_op jit(solution)/shard_map/ppermute | solution.py:19
  28.4 0.4 %collective-permute-start.8 = (bf16[64,768]{1,0:T(8,128)(2,1)S(1)}, bf16[64,768]{1,0:T(8,128)(2,1)S(1)}, u32[]{:S(2)}, u32[]{:S(2)}) collective-permute-start(bf16[64,768]{1,0:T(8,128)(2,1)S(1)} %get-tuple-element.20), channel_id=1, source_target_pairs={{0,4},{4,8},{8,12},{12,16},{16,20},{20,24},{24,28},{28,0},{1,5},{5... | collective-permute-start | bytes 294920 | tf_op jit(solution)/shard_map/ppermute | solution.py:19
  28.8 1.3 %collective-permute-start.7 = (bf16[64,768]{1,0:T(8,128)(2,1)S(1)}, bf16[64,768]{1,0:T(8,128)(2,1)S(1)}, u32[]{:S(2)}, u32[]{:S(2)}) collective-permute-start(bf16[64,768]{1,0:T(8,128)(2,1)S(1)} %get-tuple-element.21), channel_id=1, source_target_pairs={{0,4},{4,8},{8,12},{12,16},{16,20},{20,24},{24,28},{28,0},{1,5},{5... | collective-permute-start | bytes 294920 | tf_op jit(solution)/shard_map/ppermute | solution.py:19
  30.1 0.8 %collective-permute-done.2.refs_4_.refs_2_ = bf16[64,768]{1,0:T(8,128)(2,1)S(1)} collective-permute-done((bf16[64,768]{1,0:T(8,128)(2,1)S(1)}, bf16[64,768]{1,0:T(8,128)(2,1)S(1)}, u32[]{:S(2)}, u32[]{:S(2)}) %collective-permute-start.2) | collective-permute-done | bytes 98336 | tf_op jit(solution)/shard_map/ppermute | solution.py:19
  30.9 1.2 %collective-permute-done.3.refs_5_.refs_3_ = bf16[64,768]{1,0:T(8,128)(2,1)S(1)} collective-permute-done((bf16[64,768]{1,0:T(8,128)(2,1)S(1)}, bf16[64,768]{1,0:T(8,128)(2,1)S(1)}, u32[]{:S(2)}, u32[]{:S(2)}) %collective-permute-start.3) | collective-permute-done | bytes 98336 | tf_op jit(solution)/shard_map/ppermute | solution.py:19
  32.1 1.0 %attend_own.1 = (f32[256,768]{1,0:T(8,128)S(1)}, f32[256,768]{1,0:T(8,128)S(1)}, f32[256,768]{1,0:T(8,128)S(1)}) custom-call(bf16[3,64,768]{2,1,0:T(8,128)(2,1)S(1)} %get-tuple-element.19.refs_0_, bf16[3,64,768]{2,1,0:T(8,128)(2,1)S(1)} %collective-permute-done.refs_1_, bf16[2,64,768]{2,1,0:T(8,128)(2,1)S(1)} %collective-permute-done.6.refs_2_, ...), custom_call_target="tpu_custom_call" | custom-call | flops 201326592 | bytes 1376256 | tf_op jit(solution)/shard_map/attend_own/pallas_call | solution.py:130
  33.0 0.4 collective-permute-done.8.refs_7_
  33.4 1.1 %collective-permute-done.7.refs_6_ = bf16[64,768]{1,0:T(8,128)(2,1)S(1)} collective-permute-done((bf16[64,768]{1,0:T(8,128)(2,1)S(1)}, bf16[64,768]{1,0:T(8,128)(2,1)S(1)}, u32[]{:S(2)}, u32[]{:S(2)}) %collective-permute-start.7) | collective-permute-done | bytes 98336 | tf_op jit(solution)/shard_map/ppermute | solution.py:19
  34.4 0.0 collective-permute-done.5.refs_5_
  34.4 1.8 %attend_prev.1 = (f32[256,768]{1,0:T(8,128)}, f32[6,256]{1,0:T(8,128)}) custom-call(bf16[3,64,768]{2,1,0:T(8,128)(2,1)S(1)} %get-tuple-element.19.refs_0_, bf16[3,64,768]{2,1,0:T(8,128)(2,1)S(1)} %collective-permute-done.refs_1_, bf16[64,768]{1,0:T(8,128)(2,1)S(1)} %collective-permute-done.2.refs_4_.refs_2_, ...), custom_call_target="tpu_custom_call" | custom-call | flops 201326592 | bytes 1376256 | tf_op jit(solution)/shard_map/attend_prev/pallas_call | solution.py:139
  (6 shorter events, 0.1 us)
Async XLA Ops:
  0.6 4.4 %copy-start = (bf16[64,3,3072]{2,0,1:T(8,128)(2,1)S(1)}, bf16[64,3,3072]{2,0,1:T(8,128)(2,1)}, u32[]{:S(2)}) copy-start(bf16[64,3,3072]{2,0,1:T(8,128)(2,1)} %param.1) | copy-start | bytes 3538948
  1.8 13.0 %collective-permute-start = (bf16[3,64,768]{2,1,0:T(8,128)(2,1)S(1)}, bf16[3,64,768]{2,1,0:T(8,128)(2,1)S(1)}, u32[]{:S(2)}, u32[]{:S(2)}) collective-permute-start(bf16[3,64,768]{2,1,0:T(8,128)(2,1)S(1)} %get-tuple-element.18), channel_id=1, source_target_pairs={{0,1},{1,2},{2,3},{3,0},{4,5},{5,6},{6,7},{7,4},{8,9},{9,10},{10,1... | collective-permute-start | bytes 884744 | tf_op jit(solution)/shard_map/ppermute | solution.py:19
  4.9 6.0 %collective-permute-start.1 = (bf16[2,64,768]{2,1,0:T(8,128)(2,1)S(1)}, bf16[2,64,768]{2,1,0:T(8,128)(2,1)S(1)}, u32[]{:S(2)}, u32[]{:S(2)}) collective-permute-start(bf16[2,64,768]{2,1,0:T(8,128)(2,1)S(1)} %slice.16), channel_id=1, source_target_pairs={{0,4},{4,8},{8,12},{12,16},{16,20},{20,24},{24,28},{28,0},{1,5},{5... | collective-permute-start | bytes 589832 | tf_op jit(solution)/shard_map/ppermute | solution.py:19
  5.1 13.0 %collective-permute-start.4 = (bf16[2,64,768]{2,1,0:T(8,128)(2,1)S(1)}, bf16[2,64,768]{2,1,0:T(8,128)(2,1)S(1)}, u32[]{:S(2)}, u32[]{:S(2)}) collective-permute-start(bf16[2,64,768]{2,1,0:T(8,128)(2,1)S(1)} %get-tuple-element.15), channel_id=1, source_target_pairs={{0,3},{1,0},{2,1},{3,2},{4,7},{5,4},{6,5},{7,6},{8,11},{9,8},{10,9... | collective-permute-start | bytes 589832 | tf_op jit(solution)/shard_map/ppermute | solution.py:19
  11.0 17.4 %collective-permute-start.6 = (bf16[2,64,768]{2,1,0:T(8,128)(2,1)S(1)}, bf16[2,64,768]{2,1,0:T(8,128)(2,1)S(1)}, u32[]{:S(2)}, u32[]{:S(2)}) collective-permute-start(bf16[2,64,768]{2,1,0:T(8,128)(2,1)S(1)} %get-tuple-element.10), channel_id=1, source_target_pairs={{0,2},{1,3},{2,0},{3,1},{4,6},{5,7},{6,4},{7,5},{8,10},{9,11},{10,... | collective-permute-start | bytes 589832 | tf_op jit(solution)/shard_map/ppermute | solution.py:19
  18.2 16.3 %collective-permute-start.5 = (bf16[2,2,64,768]{3,2,1,0:T(8,128)(2,1)S(1)}, bf16[2,2,64,768]{3,2,1,0:T(8,128)(2,1)S(1)}, u32[]{:S(2)}, u32[]{:S(2)}) collective-permute-start(bf16[2,2,64,768]{3,2,1,0:T(8,128)(2,1)S(1)} %pad_maximum_fusion), channel_id=1, source_target_pairs={{0,4},{4,8},{8,12},{12,16},{16,20},{20,24},{24,28},{28,0},{1,5},{5... | collective-permute-start | bytes 1179656 | tf_op jit(solution)/shard_map/ppermute | solution.py:19
  18.3 12.5 %collective-permute-start.2 = (bf16[64,768]{1,0:T(8,128)(2,1)S(1)}, bf16[64,768]{1,0:T(8,128)(2,1)S(1)}, u32[]{:S(2)}, u32[]{:S(2)}) collective-permute-start(bf16[64,768]{1,0:T(8,128)(2,1)S(1)} %get-tuple-element.8), channel_id=1, source_target_pairs={{0,2},{1,3},{2,0},{3,1},{4,6},{5,7},{6,4},{7,5},{8,10},{9,11},{10,... | collective-permute-start | bytes 294920 | tf_op jit(solution)/shard_map/ppermute | solution.py:19
  24.2 7.8 %collective-permute-start.3 = (bf16[64,768]{1,0:T(8,128)(2,1)S(1)}, bf16[64,768]{1,0:T(8,128)(2,1)S(1)}, u32[]{:S(2)}, u32[]{:S(2)}) collective-permute-start(bf16[64,768]{1,0:T(8,128)(2,1)S(1)} %get-tuple-element.9), channel_id=1, source_target_pairs={{0,3},{1,0},{2,1},{3,2},{4,7},{5,4},{6,5},{7,6},{8,11},{9,8},{10,9... | collective-permute-start | bytes 294920 | tf_op jit(solution)/shard_map/ppermute | solution.py:19
  28.4 5.0 %collective-permute-start.8 = (bf16[64,768]{1,0:T(8,128)(2,1)S(1)}, bf16[64,768]{1,0:T(8,128)(2,1)S(1)}, u32[]{:S(2)}, u32[]{:S(2)}) collective-permute-start(bf16[64,768]{1,0:T(8,128)(2,1)S(1)} %get-tuple-element.20), channel_id=1, source_target_pairs={{0,4},{4,8},{8,12},{12,16},{16,20},{20,24},{24,28},{28,0},{1,5},{5... | collective-permute-start | bytes 294920 | tf_op jit(solution)/shard_map/ppermute | solution.py:19
  28.8 5.7 %collective-permute-start.7 = (bf16[64,768]{1,0:T(8,128)(2,1)S(1)}, bf16[64,768]{1,0:T(8,128)(2,1)S(1)}, u32[]{:S(2)}, u32[]{:S(2)}) collective-permute-start(bf16[64,768]{1,0:T(8,128)(2,1)S(1)} %get-tuple-element.21), channel_id=1, source_target_pairs={{0,4},{4,8},{8,12},{12,16},{16,20},{20,24},{24,28},{28,0},{1,5},{5... | collective-permute-start | bytes 294920 | tf_op jit(solution)/shard_map/ppermute | solution.py:19

commit v4 on v3

--- a/solution.py
+++ b/solution.py
@@ -36,7 +36,7 @@
     rows = group * piece
 
     def queries(k, cols):
-        return fulls[k][0, :, cols] if k < 2 else singles[k - 2][:, cols]
+        return fulls[k][0, :, cols] if k < 2 else singles[count - 1 - k][:, cols]
 
     def own(which, cols):
         return stack(
@@ -74,7 +74,7 @@
         return pl.ds(pl.multiple_of(slot * piece, piece), piece)
 
     def queries(k, cols):
-        return fulls[k][0, :, cols] if k < 2 else singles[k - 2][:, cols]
+        return fulls[k][0, :, cols] if k < 2 else singles[count - 1 - k][:, cols]
 
     def prev(which, cols):
         parts = [prev_early[i, which, :, cols] for i in range(count - 2)]
@@ -135,7 +135,7 @@
         compiler_params=pltpu.CompilerParams(vmem_limit_bytes=24 << 20),
         cost_estimate=cost(block_len, width),
         name="attend_own",
-    )(*fulls, *pairs, *singles)
+    )(*fulls, *pairs, *reversed(singles))
     return pl.pallas_call(
         functools.partial(prev_kernel, count, heads, group),
         out_shape=(whole, jax.ShapeDtypeStruct((heads, block_len), jnp.float32)),
@@ -150,7 +150,7 @@
         compiler_params=pltpu.CompilerParams(vmem_limit_bytes=24 << 20),
         cost_estimate=cost(block_len, width),
         name="attend_prev",
-    )(*fulls, *singles, *prevs, *running)
+    )(*fulls, *reversed(singles), *prevs, *running)
 
 
 def shards(qkv):

time: 36.4 us -> 35.9 us (0.986)
  starting transfers between devices: 16 us -> 15.6 us
    ppermute x9, starting transfers between devices: 16 us -> 15.6 us  [shift(): lax.ppermute(value, axis, [(i, (i + steps) % count) for i in range(count)])]
  transfers between devices with their start and end apart: 9 -> 9, of which waited for: 8 -> 6; matrix products, arithmetic and copies ran while one was open for 0% -> 0% of each run, Pallas kernels for 3% -> 3%
where the time goes in v4:
time: 35.9 us; the launch traced here: 35.7 us
  starting transfers between devices  15.6 us (43%)
  waiting for transfers between devices  15.2 us (42%)
  Pallas kernels  2.78 us (8%)
  local copies, waits for them, and re-layouts  1.29 us (4%)
  between operations  0.76 us (2%)
    ppermute x9, starting transfers between devices, shift(): lax.ppermute(value, axis, [(i, (i + steps) % count) for i in range(count)])  15.6 us
    ppermute x9, waiting for transfers between devices, shift(): lax.ppermute(value, axis, [(i, (i + steps) % count) for i in range(count)])  15.2 us
    pallas_call x1, Pallas kernels, attend(): pl.pallas_call(functools.partial(prev_kernel, count, heads, group), out_s...  1.82 us
    dynamic_slice x2, local copies, waits for them, and re-layouts, cut(): lax.dynamic_slice(planes, (first, 0, start), (last - first, tokens, width))  1.23 us
    pallas_call x1, Pallas kernels, attend(): pl.pallas_call(functools.partial(own_kernel, count, heads, group), out_sh...  0.97 us
  transfers between devices with their start and end apart: 9, of which 6 were waited for; matrix products, arithmetic and copies ran while one was open for 0% of the time, Pallas kernels for 3%

profile of v4, /device:TPU:0, one launch (start us, length us, event | category | flops | bytes accessed | tf_op | source)
XLA Modules:
  0.0 35.7 jit_solution(14883678746183891899)
XLA Ops:
  0.6 0.0 copy-start
  0.7 1.2 %dynamic-slice_bitcast_fusion = (bf16[3,64,768]{2,1,0:T(8,128)(2,1)S(1)}, bf16[3,64,768]{2,1,0:T(8,128)(2,1)S(1)}) fusion(bf16[64,3,3072]{2,0,1:T(8,128)(2,1)} %param.1, s32[]{:T(128)S(6)} %select_n.32, s32[]{:T(128)S(6)} %select_n.30), kind=kLoop, calls=%fused_computation.1 | loop fusion | bytes 1179656 | tf_op jit(solution)/shard_map/dynamic_slice | solution.py:164
  1.8 3.1 %collective-permute-start = (bf16[3,64,768]{2,1,0:T(8,128)(2,1)S(1)}, bf16[3,64,768]{2,1,0:T(8,128)(2,1)S(1)}, u32[]{:S(2)}, u32[]{:S(2)}) collective-permute-start(bf16[3,64,768]{2,1,0:T(8,128)(2,1)S(1)} %get-tuple-element.18), channel_id=1, source_target_pairs={{0,1},{1,2},{2,3},{3,0},{4,5},{5,6},{6,7},{7,4},{8,9},{9,10},{10,1... | collective-permute-start | bytes 884744 | tf_op jit(solution)/shard_map/ppermute | solution.py:19
  4.9 0.1 collective-permute-start.1
  5.0 0.0 copy-done
  5.1 2.1 %collective-permute-start.4 = (bf16[2,64,768]{2,1,0:T(8,128)(2,1)S(1)}, bf16[2,64,768]{2,1,0:T(8,128)(2,1)S(1)}, u32[]{:S(2)}, u32[]{:S(2)}) collective-permute-start(bf16[2,64,768]{2,1,0:T(8,128)(2,1)S(1)} %get-tuple-element.15), channel_id=1, source_target_pairs={{0,3},{1,0},{2,1},{3,2},{4,7},{5,4},{6,5},{7,6},{8,11},{9,8},{10,9... | collective-permute-start | bytes 589832 | tf_op jit(solution)/shard_map/ppermute | solution.py:19
  7.2 3.8 %collective-permute-done.1.refs_4_ = bf16[2,64,768]{2,1,0:T(8,128)(2,1)S(1)} collective-permute-done((bf16[2,64,768]{2,1,0:T(8,128)(2,1)S(1)}, bf16[2,64,768]{2,1,0:T(8,128)(2,1)S(1)}, u32[]{:S(2)}, u32[]{:S(2)}) %collective-permute-start.1) | collective-permute-done | bytes 196640 | tf_op jit(solution)/shard_map/ppermute | solution.py:19
  11.0 2.6 %collective-permute-start.6 = (bf16[2,64,768]{2,1,0:T(8,128)(2,1)S(1)}, bf16[2,64,768]{2,1,0:T(8,128)(2,1)S(1)}, u32[]{:S(2)}, u32[]{:S(2)}) collective-permute-start(bf16[2,64,768]{2,1,0:T(8,128)(2,1)S(1)} %get-tuple-element.10), channel_id=1, source_target_pairs={{0,2},{1,3},{2,0},{3,1},{4,6},{5,7},{6,4},{7,5},{8,10},{9,11},{10,... | collective-permute-start | bytes 589832 | tf_op jit(solution)/shard_map/ppermute | solution.py:19
  13.6 1.3 %collective-permute-done.refs_1_ = bf16[3,64,768]{2,1,0:T(8,128)(2,1)S(1)} collective-permute-done((bf16[3,64,768]{2,1,0:T(8,128)(2,1)S(1)}, bf16[3,64,768]{2,1,0:T(8,128)(2,1)S(1)}, u32[]{:S(2)}, u32[]{:S(2)}) %collective-permute-start) | collective-permute-done | bytes 294944 | tf_op jit(solution)/shard_map/ppermute | solution.py:19
  14.8 3.3 %collective-permute-done.4.refs_3_ = bf16[2,64,768]{2,1,0:T(8,128)(2,1)S(1)} collective-permute-done((bf16[2,64,768]{2,1,0:T(8,128)(2,1)S(1)}, bf16[2,64,768]{2,1,0:T(8,128)(2,1)S(1)}, u32[]{:S(2)}, u32[]{:S(2)}) %collective-permute-start.4) | collective-permute-done | bytes 196640 | tf_op jit(solution)/shard_map/ppermute | solution.py:19
  18.2 0.2 collective-permute-start.5
  18.3 2.8 %collective-permute-start.2 = (bf16[64,768]{1,0:T(8,128)(2,1)S(1)}, bf16[64,768]{1,0:T(8,128)(2,1)S(1)}, u32[]{:S(2)}, u32[]{:S(2)}) collective-permute-start(bf16[64,768]{1,0:T(8,128)(2,1)S(1)} %get-tuple-element.8), channel_id=1, source_target_pairs={{0,3},{1,0},{2,1},{3,2},{4,7},{5,4},{6,5},{7,6},{8,11},{9,8},{10,9... | collective-permute-start | bytes 294920 | tf_op jit(solution)/shard_map/ppermute | solution.py:19
  21.1 3.2 %collective-permute-start.3 = (bf16[64,768]{1,0:T(8,128)(2,1)S(1)}, bf16[64,768]{1,0:T(8,128)(2,1)S(1)}, u32[]{:S(2)}, u32[]{:S(2)}) collective-permute-start(bf16[64,768]{1,0:T(8,128)(2,1)S(1)} %get-tuple-element.9), channel_id=1, source_target_pairs={{0,2},{1,3},{2,0},{3,1},{4,6},{5,7},{6,4},{7,5},{8,10},{9,11},{10,... | collective-permute-start | bytes 294920 | tf_op jit(solution)/shard_map/ppermute | solution.py:19
  24.3 2.3 %collective-permute-done.6.refs_2_ = bf16[2,64,768]{2,1,0:T(8,128)(2,1)S(1)} collective-permute-done((bf16[2,64,768]{2,1,0:T(8,128)(2,1)S(1)}, bf16[2,64,768]{2,1,0:T(8,128)(2,1)S(1)}, u32[]{:S(2)}, u32[]{:S(2)}) %collective-permute-start.6) | collective-permute-done | bytes 196640 | tf_op jit(solution)/shard_map/ppermute | solution.py:19
  26.7 0.1 collective-permute-start.8
  26.8 1.5 %collective-permute-start.7 = (bf16[64,768]{1,0:T(8,128)(2,1)S(1)}, bf16[64,768]{1,0:T(8,128)(2,1)S(1)}, u32[]{:S(2)}, u32[]{:S(2)}) collective-permute-start(bf16[64,768]{1,0:T(8,128)(2,1)S(1)} %get-tuple-element.21), channel_id=1, source_target_pairs={{0,4},{4,8},{8,12},{12,16},{16,20},{20,24},{24,28},{28,0},{1,5},{5... | collective-permute-start | bytes 294920 | tf_op jit(solution)/shard_map/ppermute | solution.py:19
  28.3 0.3 collective-permute-done.2.refs_4_.refs_2_
  28.6 4.3 %collective-permute-done.3.refs_5_.refs_3_ = bf16[64,768]{1,0:T(8,128)(2,1)S(1)} collective-permute-done((bf16[64,768]{1,0:T(8,128)(2,1)S(1)}, bf16[64,768]{1,0:T(8,128)(2,1)S(1)}, u32[]{:S(2)}, u32[]{:S(2)}) %collective-permute-start.3) | collective-permute-done | bytes 98336 | tf_op jit(solution)/shard_map/ppermute | solution.py:19
  32.9 1.0 %attend_own.1 = (f32[256,768]{1,0:T(8,128)S(1)}, f32[256,768]{1,0:T(8,128)S(1)}, f32[256,768]{1,0:T(8,128)S(1)}) custom-call(bf16[3,64,768]{2,1,0:T(8,128)(2,1)S(1)} %get-tuple-element.19.refs_0_, bf16[3,64,768]{2,1,0:T(8,128)(2,1)S(1)} %collective-permute-done.refs_1_, bf16[2,64,768]{2,1,0:T(8,128)(2,1)S(1)} %collective-permute-done.6.refs_2_, ...), custom_call_target="tpu_custom_call" | custom-call | flops 201326592 | bytes 1376256 | tf_op jit(solution)/shard_map/attend_own/pallas_call | solution.py:130
  33.9 0.0 collective-permute-done.8.refs_7_
  33.9 0.0 collective-permute-done.7.refs_6_
  33.9 0.0 collective-permute-done.5.refs_5_
  33.9 1.8 %attend_prev.1 = (f32[256,768]{1,0:T(8,128)}, f32[6,256]{1,0:T(8,128)}) custom-call(bf16[3,64,768]{2,1,0:T(8,128)(2,1)S(1)} %get-tuple-element.19.refs_0_, bf16[3,64,768]{2,1,0:T(8,128)(2,1)S(1)} %collective-permute-done.refs_1_, bf16[64,768]{1,0:T(8,128)(2,1)S(1)} %collective-permute-done.2.refs_4_.refs_2_, ...), custom_call_target="tpu_custom_call" | custom-call | flops 201326592 | bytes 1376256 | tf_op jit(solution)/shard_map/attend_prev/pallas_call | solution.py:139
  (6 shorter events, 0.1 us)
Async XLA Ops:
  0.6 4.4 %copy-start = (bf16[64,3,3072]{2,0,1:T(8,128)(2,1)S(1)}, bf16[64,3,3072]{2,0,1:T(8,128)(2,1)}, u32[]{:S(2)}) copy-start(bf16[64,3,3072]{2,0,1:T(8,128)(2,1)} %param.1) | copy-start | bytes 3538948
  1.8 13.0 %collective-permute-start = (bf16[3,64,768]{2,1,0:T(8,128)(2,1)S(1)}, bf16[3,64,768]{2,1,0:T(8,128)(2,1)S(1)}, u32[]{:S(2)}, u32[]{:S(2)}) collective-permute-start(bf16[3,64,768]{2,1,0:T(8,128)(2,1)S(1)} %get-tuple-element.18), channel_id=1, source_target_pairs={{0,1},{1,2},{2,3},{3,0},{4,5},{5,6},{6,7},{7,4},{8,9},{9,10},{10,1... | collective-permute-start | bytes 884744 | tf_op jit(solution)/shard_map/ppermute | solution.py:19
  4.9 6.0 %collective-permute-start.1 = (bf16[2,64,768]{2,1,0:T(8,128)(2,1)S(1)}, bf16[2,64,768]{2,1,0:T(8,128)(2,1)S(1)}, u32[]{:S(2)}, u32[]{:S(2)}) collective-permute-start(bf16[2,64,768]{2,1,0:T(8,128)(2,1)S(1)} %slice.16), channel_id=1, source_target_pairs={{0,4},{4,8},{8,12},{12,16},{16,20},{20,24},{24,28},{28,0},{1,5},{5... | collective-permute-start | bytes 589832 | tf_op jit(solution)/shard_map/ppermute | solution.py:19
  5.1 13.0 %collective-permute-start.4 = (bf16[2,64,768]{2,1,0:T(8,128)(2,1)S(1)}, bf16[2,64,768]{2,1,0:T(8,128)(2,1)S(1)}, u32[]{:S(2)}, u32[]{:S(2)}) collective-permute-start(bf16[2,64,768]{2,1,0:T(8,128)(2,1)S(1)} %get-tuple-element.15), channel_id=1, source_target_pairs={{0,3},{1,0},{2,1},{3,2},{4,7},{5,4},{6,5},{7,6},{8,11},{9,8},{10,9... | collective-permute-start | bytes 589832 | tf_op jit(solution)/shard_map/ppermute | solution.py:19
  11.0 15.7 %collective-permute-start.6 = (bf16[2,64,768]{2,1,0:T(8,128)(2,1)S(1)}, bf16[2,64,768]{2,1,0:T(8,128)(2,1)S(1)}, u32[]{:S(2)}, u32[]{:S(2)}) collective-permute-start(bf16[2,64,768]{2,1,0:T(8,128)(2,1)S(1)} %get-tuple-element.10), channel_id=1, source_target_pairs={{0,2},{1,3},{2,0},{3,1},{4,6},{5,7},{6,4},{7,5},{8,10},{9,11},{10,... | collective-permute-start | bytes 589832 | tf_op jit(solution)/shard_map/ppermute | solution.py:19
  18.2 15.7 %collective-permute-start.5 = (bf16[2,2,64,768]{3,2,1,0:T(8,128)(2,1)S(1)}, bf16[2,2,64,768]{3,2,1,0:T(8,128)(2,1)S(1)}, u32[]{:S(2)}, u32[]{:S(2)}) collective-permute-start(bf16[2,2,64,768]{3,2,1,0:T(8,128)(2,1)S(1)} %pad_maximum_fusion), channel_id=1, source_target_pairs={{0,4},{4,8},{8,12},{12,16},{16,20},{20,24},{24,28},{28,0},{1,5},{5... | collective-permute-start | bytes 1179656 | tf_op jit(solution)/shard_map/ppermute | solution.py:19
  18.3 10.3 %collective-permute-start.2 = (bf16[64,768]{1,0:T(8,128)(2,1)S(1)}, bf16[64,768]{1,0:T(8,128)(2,1)S(1)}, u32[]{:S(2)}, u32[]{:S(2)}) collective-permute-start(bf16[64,768]{1,0:T(8,128)(2,1)S(1)} %get-tuple-element.8), channel_id=1, source_target_pairs={{0,3},{1,0},{2,1},{3,2},{4,7},{5,4},{6,5},{7,6},{8,11},{9,8},{10,9... | collective-permute-start | bytes 294920 | tf_op jit(solution)/shard_map/ppermute | solution.py:19
  21.1 11.8 %collective-permute-start.3 = (bf16[64,768]{1,0:T(8,128)(2,1)S(1)}, bf16[64,768]{1,0:T(8,128)(2,1)S(1)}, u32[]{:S(2)}, u32[]{:S(2)}) collective-permute-start(bf16[64,768]{1,0:T(8,128)(2,1)S(1)} %get-tuple-element.9), channel_id=1, source_target_pairs={{0,2},{1,3},{2,0},{3,1},{4,6},{5,7},{6,4},{7,5},{8,10},{9,11},{10,... | collective-permute-start | bytes 294920 | tf_op jit(solution)/shard_map/ppermute | solution.py:19
  26.7 7.2 %collective-permute-start.8 = (bf16[64,768]{1,0:T(8,128)(2,1)S(1)}, bf16[64,768]{1,0:T(8,128)(2,1)S(1)}, u32[]{:S(2)}, u32[]{:S(2)}) collective-permute-start(bf16[64,768]{1,0:T(8,128)(2,1)S(1)} %get-tuple-element.20), channel_id=1, source_target_pairs={{0,4},{4,8},{8,12},{12,16},{16,20},{20,24},{24,28},{28,0},{1,5},{5... | collective-permute-start | bytes 294920 | tf_op jit(solution)/shard_map/ppermute | solution.py:19
  26.8 7.1 %collective-permute-start.7 = (bf16[64,768]{1,0:T(8,128)(2,1)S(1)}, bf16[64,768]{1,0:T(8,128)(2,1)S(1)}, u32[]{:S(2)}, u32[]{:S(2)}) collective-permute-start(bf16[64,768]{1,0:T(8,128)(2,1)S(1)} %get-tuple-element.21), channel_id=1, source_target_pairs={{0,4},{4,8},{8,12},{12,16},{16,20},{20,24},{24,28},{28,0},{1,5},{5... | collective-permute-start | bytes 294920 | tf_op jit(solution)/shard_map/ppermute | solution.py:19

commit v5 on v3

v5 whole, which is shorter than its diff:
```python
import functools
import math

import jax
import jax.numpy as jnp
from jax import lax
from jax.experimental import pallas as pl
from jax.experimental.pallas import tpu as pltpu
from jax.sharding import PartitionSpec as P

HEAD_DIM = 128
TEMPER = 1.0 / math.sqrt(HEAD_DIM)
SCALE = TEMPER * math.log2(math.e)
CONTRACT = (((1,), (1,)), ((), ()))


def shift(value, axis, steps):
    count = lax.axis_size(axis)
    return lax.ppermute(value, axis, [(i, (i + steps) % count) for i in range(count)])


def after(value, *others):
    return lax.optimization_barrier((value, *others))[0]


def stack(parts):
    return parts[0] if len(parts) == 1 else jnp.concatenate(parts, axis=0)


def own_kernel(order, heads, group, *refs):
    count = len(order)
    fulls = refs[:2]
    pairs = refs[2:count]
    singles = refs[count : 2 * count - 2]
    accum, top_out, total_out = refs[2 * count - 2 :]
    piece = fulls[0].shape[1]
    rows = group * piece

    def queries(k, cols):
        return fulls[k][0, :, cols] if k < 2 else singles[k - 2][:, cols]

    def own(which, cols):
        return stack(
            [ref[1 + which, :, cols] for ref in fulls] + [ref[which, :, cols] for ref in pairs]
        )

    for h in range(heads):
        cols = slice(h * HEAD_DIM, (h + 1) * HEAD_DIM)
        keys, values = own(0, cols), own(1, cols)
        for g in range(count // group):
            query = stack([queries(k, cols) for k in range(g * group, (g + 1) * group)])
            scores = lax.dot_general(query, keys, CONTRACT, preferred_element_type=jnp.float32)
            top = jnp.max(scores, axis=1, keepdims=True)
            weights = jnp.exp2((scores - top) * SCALE)
            total = jnp.sum(weights, axis=1, keepdims=True)
            span = slice(g * rows, (g + 1) * rows)
            accum[span, cols] = jnp.dot(
                weights.astype(jnp.bfloat16), values, preferred_element_type=jnp.float32
            )
            top_out[span, cols] = jnp.broadcast_to(top, (rows, HEAD_DIM))
            total_out[span, cols] = jnp.broadcast_to(total, (rows, HEAD_DIM))


def prev_weights_kernel(order, heads, group, *refs):
    count = len(order)
    me = lax.axis_index("uly")
    fulls = refs[:2]
    singles = refs[2:count]
    prev_home, prev_early, prev_last = refs[count : count + 3]
    accum, top_in, total_in, scaled, inverse, packed, turned, stat = refs[count + 3 :]
    piece = fulls[0].shape[1]
    rows = group * piece

    def rows_of(i):
        k = order[i]
        slot = jnp.where(me < k, me + (count - k), me - k)
        return pl.ds(pl.multiple_of(slot * piece, piece), piece)

    def queries(k, cols):
        return fulls[k][0, :, cols] if k < 2 else singles[k - 2][:, cols]

    lane = lax.broadcasted_iota(jnp.int32, (rows, HEAD_DIM), 1)
    logs = [jnp.zeros((rows, HEAD_DIM), jnp.float32)] * (count // group)
    for h in range(heads):
        cols = slice(h * HEAD_DIM, (h + 1) * HEAD_DIM)
        parts = [prev_early[i, 0, :, cols] for i in range(count - 2)]
        keys = stack([prev_home[0, :, cols]] + parts + [prev_last[:, cols]])
        wide = keys.shape[0]
        for g in range(count // group):
            span = slice(g * rows, (g + 1) * rows)
            query = stack([queries(k, cols) for k in range(g * group, (g + 1) * group)])
            scores = lax.dot_general(query, keys, CONTRACT, preferred_element_type=jnp.float32)
            top, total = top_in[span, cols], total_in[span, cols]
            newtop = jnp.maximum(top, jnp.max(scores, axis=1, keepdims=True))
            spread = jnp.concatenate([newtop] * (wide // HEAD_DIM), axis=1)
            weights = jnp.exp2((scores - spread) * SCALE)
            factor = jnp.exp2((top - newtop) * SCALE)
            total = total * factor + jnp.sum(weights, axis=1, keepdims=True)
            packed[span, h * wide : (h + 1) * wide] = weights.astype(jnp.bfloat16)
            recip = 1.0 / total
            inverse[span, cols] = recip
            scaled[span, cols] = accum[span, cols] * (factor * recip)
            logs[g] = jnp.where(lane == h, newtop * TEMPER + jnp.log(total), logs[g])
    for g in range(count // group):
        for i in range(group):
            stat[rows_of(g * group + i), :] = logs[g][i * piece : (i + 1) * piece]
    turned[...] = stat[...].T[:heads, :]


def prev_values_kernel(order, heads, group, *refs):
    count = len(order)
    me = lax.axis_index("uly")
    prev_home, prev_early, prev_last = refs[:3]
    scaled, inverse, packed, turned, out, log_out, result, sem = refs[3:]
    piece = prev_last.shape[0]
    rows = group * piece

    def rows_of(i):
        k = order[i]
        slot = jnp.where(me < k, me + (count - k), me - k)
        return pl.ds(pl.multiple_of(slot * piece, piece), piece)

    copies = [pltpu.make_async_copy(turned, log_out, sem)]
    copies[0].start()
    for h in range(heads):
        cols = slice(h * HEAD_DIM, (h + 1) * HEAD_DIM)
        parts = [prev_early[i, 1, :, cols] for i in range(count - 2)]
        values = stack([prev_home[1, :, cols]] + parts + [prev_last[:, cols]])
        wide = values.shape[0]
        for g in range(count // group):
            span = slice(g * rows, (g + 1) * rows)
            weights = packed[span, h * wide : (h + 1) * wide]
            added = jnp.dot(weights, values, preferred_element_type=jnp.float32)
            normed = scaled[span, cols] + added * inverse[span, cols]
            for i in range(group):
                result[rows_of(g * group + i), cols] = normed[i * piece : (i + 1) * piece]
        copies.append(pltpu.make_async_copy(result.at[:, cols], out.at[:, cols], sem))
        copies[-1].start()
    for copy in copies:
        copy.wait()


def cost(block_len, width):
    return pl.CostEstimate(
        flops=4 * block_len * block_len * width,
        bytes_accessed=7 * block_len * width,
        transcendentals=block_len * block_len * width // HEAD_DIM,
    )


def attend(order, fulls, pairs, singles, prevs, block_len, width):
    count = len(order)
    heads = width // HEAD_DIM
    group = math.gcd(count, 4)
    in_vmem = pl.BlockSpec(memory_space=pltpu.VMEM)
    whole = jax.ShapeDtypeStruct((block_len, width), jnp.float32)
    running = pl.pallas_call(
        functools.partial(own_kernel, order, heads, group),
        out_shape=(whole, whole, whole),
        in_specs=[in_vmem] * (2 * count - 2),
        out_specs=(in_vmem,) * 3,
        compiler_params=pltpu.CompilerParams(vmem_limit_bytes=24 << 20),
        cost_estimate=cost(block_len, width),
        name="attend_own",
    )(*fulls, *pairs, *singles)
    prev_home, prev_early, last_keys, last_values = prevs
    logs = jax.ShapeDtypeStruct((heads, block_len), jnp.float32)
    scaled, inverse, packed, turned = pl.pallas_call(
        functools.partial(prev_weights_kernel, order, heads, group),
        out_shape=(whole, whole, jax.ShapeDtypeStruct((block_len, heads * block_len), jnp.bfloat16), logs),
        in_specs=[in_vmem] * (count + 6),
        out_specs=(in_vmem,) * 4,
        scratch_shapes=[pltpu.VMEM((block_len, HEAD_DIM), jnp.float32)],
        compiler_params=pltpu.CompilerParams(vmem_limit_bytes=24 << 20),
        cost_estimate=cost(block_len, width),
        name="attend_prev_weights",
    )(*fulls, *singles, prev_home, prev_early, last_keys, *running)
    return pl.pallas_call(
        functools.partial(prev_values_kernel, order, heads, group),
        out_shape=(whole, logs),
        in_specs=[in_vmem] * 7,
        out_specs=(pl.BlockSpec(memory_space=pl.ANY),) * 2,
        scratch_shapes=[pltpu.VMEM((block_len, width), jnp.float32), pltpu.SemaphoreType.DMA(())],
        compiler_params=pltpu.CompilerParams(vmem_limit_bytes=24 << 20),
        cost_estimate=cost(block_len, width),
        name="attend_prev_values",
    )(prev_home, prev_early, last_values, scaled, inverse, packed, turned)


def shards(qkv):
    count = lax.axis_size("uly")
    me = lax.axis_index("uly")
    tokens, planes_count, width = qkv.shape[0], qkv.shape[1], qkv.shape[2] // count
    planes = jnp.transpose(qkv, (1, 0, 2))

    def cut(first, last, k):
        start = jnp.where(me + k < count, me + k, me + k - count) * width
        return lax.dynamic_slice(planes, (first, 0, start), (last - first, tokens, width))

    mid = count // 2
    steps = [k for k in range(2, count) if k != mid] + [mid]
    home = cut(0, planes_count, 0)
    first = shift(cut(0, planes_count, 1), "uly", 1)
    prevs = [shift(home[1:], "blk", 1)]
    pairs = []
    for k in steps:
        pair = cut(1, planes_count, k)
        pairs.append(shift(after(pair, prevs[0]) if k == mid else pair, "uly", k))
    singles = [shift(after(cut(0, 1, k)[0], pairs[0]), "uly", k) for k in range(2, count)]
    prevs.append(shift(jnp.stack([first[1:]] + pairs[:-1]), "blk", 1))
    prevs += [shift(pairs[-1][i], "blk", 1) for i in range(2)]
    return attend(tuple(range(count)), [home, first], pairs, singles, prevs, tokens * count, width)


def solution(mesh):
    placed = (P(("blk", "uly"), None, None),)
    return jax.shard_map(
        shards,
        mesh=mesh,
        in_specs=placed,
        out_specs=(P("blk", "uly"), P("uly", "blk")),
        check_vma=False,
    )
```

time: 36.4 us -> 35.7 us (0.981)
  waiting for transfers between devices: 15.4 us -> 14.4 us
    ppermute x9, waiting for transfers between devices: 15.4 us -> 14.4 us  [shift(): lax.ppermute(value, axis, [(i, (i + steps) % count) for i in range(count)])]
    pallas_call x2 -> x3, Pallas kernels: 2.78 us -> 3.03 us  [the longest x1 1.1 us: attend(): pl.pallas_call(functools.partial(prev_values_kernel, order, heads, group)...]
  transfers between devices with their start and end apart: 9 -> 9, of which waited for: 8 -> 8; matrix products, arithmetic and copies ran while one was open for 0% -> 0% of each run, Pallas kernels for 3% -> 5%
where the time goes in v5:
time: 35.7 us; the launch traced here: 35.5 us
  starting transfers between devices  16 us (45%)
  waiting for transfers between devices  14.4 us (40%)
  Pallas kernels  3.03 us (8%)
  local copies, waits for them, and re-layouts  1.29 us (4%)
  between operations  0.74 us (2%)
    ppermute x9, starting transfers between devices, shift(): lax.ppermute(value, axis, [(i, (i + steps) % count) for i in range(count)])  16 us
    ppermute x9, waiting for transfers between devices, shift(): lax.ppermute(value, axis, [(i, (i + steps) % count) for i in range(count)])  14.4 us
    dynamic_slice x2, local copies, waits for them, and re-layouts, cut(): lax.dynamic_slice(planes, (first, 0, start), (last - first, tokens, width))  1.23 us
    pallas_call x1, Pallas kernels, attend(): pl.pallas_call(functools.partial(prev_values_kernel, order, heads, group)...  1.1 us
    pallas_call x1, Pallas kernels, attend(): pl.pallas_call(functools.partial(prev_weights_kernel, order, heads, group...  0.97 us
    pallas_call x1, Pallas kernels, attend(): pl.pallas_call(functools.partial(own_kernel, order, heads, group), out_sh...  0.97 us
  transfers between devices with their start and end apart: 9, of which 8 were waited for; matrix products, arithmetic and copies ran while one was open for 0% of the time, Pallas kernels for 5%

profile of v5, /device:TPU:0, one launch (start us, length us, event | category | flops | bytes accessed | tf_op | source)
XLA Modules:
  0.0 35.5 jit_solution(11777204412882759118)
XLA Ops:
  0.6 0.0 copy-start
  0.7 1.2 %dynamic-slice_bitcast_fusion = (bf16[3,64,768]{2,1,0:T(8,128)(2,1)S(1)}, bf16[3,64,768]{2,1,0:T(8,128)(2,1)S(1)}) fusion(bf16[64,3,3072]{2,0,1:T(8,128)(2,1)} %param.1, s32[]{:T(128)S(6)} %select_n.32, s32[]{:T(128)S(6)} %select_n.30), kind=kLoop, calls=%fused_computation.1 | loop fusion | bytes 1179656 | tf_op jit(solution)/shard_map/dynamic_slice | solution.py:198
  1.8 3.1 %collective-permute-start.1 = (bf16[3,64,768]{2,1,0:T(8,128)(2,1)S(1)}, bf16[3,64,768]{2,1,0:T(8,128)(2,1)S(1)}, u32[]{:S(2)}, u32[]{:S(2)}) collective-permute-start(bf16[3,64,768]{2,1,0:T(8,128)(2,1)S(1)} %get-tuple-element.26), channel_id=1, source_target_pairs={{0,1},{1,2},{2,3},{3,0},{4,5},{5,6},{6,7},{7,4},{8,9},{9,10},{10,1... | collective-permute-start | bytes 884744 | tf_op jit(solution)/shard_map/ppermute | solution.py:19
  4.9 0.1 collective-permute-start
  5.0 0.0 copy-done
  5.1 2.1 %collective-permute-start.2 = (bf16[2,64,768]{2,1,0:T(8,128)(2,1)S(1)}, bf16[2,64,768]{2,1,0:T(8,128)(2,1)S(1)}, u32[]{:S(2)}, u32[]{:S(2)}) collective-permute-start(bf16[2,64,768]{2,1,0:T(8,128)(2,1)S(1)} %get-tuple-element.25), channel_id=1, source_target_pairs={{0,3},{1,0},{2,1},{3,2},{4,7},{5,4},{6,5},{7,6},{8,11},{9,8},{10,9... | collective-permute-start | bytes 589832 | tf_op jit(solution)/shard_map/ppermute | solution.py:19
  7.2 3.8 %collective-permute-done.refs_4_.refs_0_ = bf16[2,64,768]{2,1,0:T(8,128)(2,1)S(1)} collective-permute-done((bf16[2,64,768]{2,1,0:T(8,128)(2,1)S(1)}, bf16[2,64,768]{2,1,0:T(8,128)(2,1)S(1)}, u32[]{:S(2)}, u32[]{:S(2)}) %collective-permute-start) | collective-permute-done | bytes 196640 | tf_op jit(solution)/shard_map/ppermute | solution.py:19
  11.0 2.6 %collective-permute-start.4 = (bf16[2,64,768]{2,1,0:T(8,128)(2,1)S(1)}, bf16[2,64,768]{2,1,0:T(8,128)(2,1)S(1)}, u32[]{:S(2)}, u32[]{:S(2)}) collective-permute-start(bf16[2,64,768]{2,1,0:T(8,128)(2,1)S(1)} %get-tuple-element.12), channel_id=1, source_target_pairs={{0,2},{1,3},{2,0},{3,1},{4,6},{5,7},{6,4},{7,5},{8,10},{9,11},{10,... | collective-permute-start | bytes 589832 | tf_op jit(solution)/shard_map/ppermute | solution.py:19
  13.6 1.3 %collective-permute-done.1.refs_1_ = bf16[3,64,768]{2,1,0:T(8,128)(2,1)S(1)} collective-permute-done((bf16[3,64,768]{2,1,0:T(8,128)(2,1)S(1)}, bf16[3,64,768]{2,1,0:T(8,128)(2,1)S(1)}, u32[]{:S(2)}, u32[]{:S(2)}) %collective-permute-start.1) | collective-permute-done | bytes 294944 | tf_op jit(solution)/shard_map/ppermute | solution.py:19
  14.8 3.3 %collective-permute-done.2.refs_2_ = bf16[2,64,768]{2,1,0:T(8,128)(2,1)S(1)} collective-permute-done((bf16[2,64,768]{2,1,0:T(8,128)(2,1)S(1)}, bf16[2,64,768]{2,1,0:T(8,128)(2,1)S(1)}, u32[]{:S(2)}, u32[]{:S(2)}) %collective-permute-start.2) | collective-permute-done | bytes 196640 | tf_op jit(solution)/shard_map/ppermute | solution.py:19
  18.2 0.2 collective-permute-start.3
  18.3 5.9 %collective-permute-start.6 = (bf16[64,768]{1,0:T(8,128)(2,1)S(1)}, bf16[64,768]{1,0:T(8,128)(2,1)S(1)}, u32[]{:S(2)}, u32[]{:S(2)}) collective-permute-start(bf16[64,768]{1,0:T(8,128)(2,1)S(1)} %get-tuple-element.13), channel_id=1, source_target_pairs={{0,2},{1,3},{2,0},{3,1},{4,6},{5,7},{6,4},{7,5},{8,10},{9,11},{10,... | collective-permute-start | bytes 294920 | tf_op jit(solution)/shard_map/ppermute | solution.py:19
  24.2 0.4 %collective-permute-start.7 = (bf16[64,768]{1,0:T(8,128)(2,1)S(1)}, bf16[64,768]{1,0:T(8,128)(2,1)S(1)}, u32[]{:S(2)}, u32[]{:S(2)}) collective-permute-start(bf16[64,768]{1,0:T(8,128)(2,1)S(1)} %get-tuple-element.14), channel_id=1, source_target_pairs={{0,3},{1,0},{2,1},{3,2},{4,7},{5,4},{6,5},{7,6},{8,11},{9,8},{10,9... | collective-permute-start | bytes 294920 | tf_op jit(solution)/shard_map/ppermute | solution.py:19
  24.7 3.7 %collective-permute-done.4.refs_3_ = bf16[2,64,768]{2,1,0:T(8,128)(2,1)S(1)} collective-permute-done((bf16[2,64,768]{2,1,0:T(8,128)(2,1)S(1)}, bf16[2,64,768]{2,1,0:T(8,128)(2,1)S(1)}, u32[]{:S(2)}, u32[]{:S(2)}) %collective-permute-start.4) | collective-permute-done | bytes 196640 | tf_op jit(solution)/shard_map/ppermute | solution.py:19
  28.4 0.4 %collective-permute-start.8 = (bf16[64,768]{1,0:T(8,128)(2,1)S(1)}, bf16[64,768]{1,0:T(8,128)(2,1)S(1)}, u32[]{:S(2)}, u32[]{:S(2)}) collective-permute-start(bf16[64,768]{1,0:T(8,128)(2,1)S(1)} %get-tuple-element.28), channel_id=1, source_target_pairs={{0,4},{4,8},{8,12},{12,16},{16,20},{20,24},{24,28},{28,0},{1,5},{5... | collective-permute-start | bytes 294920 | tf_op jit(solution)/shard_map/ppermute | solution.py:19
  28.8 1.3 %collective-permute-start.5 = (bf16[64,768]{1,0:T(8,128)(2,1)S(1)}, bf16[64,768]{1,0:T(8,128)(2,1)S(1)}, u32[]{:S(2)}, u32[]{:S(2)}) collective-permute-start(bf16[64,768]{1,0:T(8,128)(2,1)S(1)} %get-tuple-element.29), channel_id=1, source_target_pairs={{0,4},{4,8},{8,12},{12,16},{16,20},{20,24},{24,28},{28,0},{1,5},{5... | collective-permute-start | bytes 294920 | tf_op jit(solution)/shard_map/ppermute | solution.py:19
  30.1 0.8 %collective-permute-done.6.refs_4_.refs_2_ = bf16[64,768]{1,0:T(8,128)(2,1)S(1)} collective-permute-done((bf16[64,768]{1,0:T(8,128)(2,1)S(1)}, bf16[64,768]{1,0:T(8,128)(2,1)S(1)}, u32[]{:S(2)}, u32[]{:S(2)}) %collective-permute-start.6) | collective-permute-done | bytes 98336 | tf_op jit(solution)/shard_map/ppermute | solution.py:19
  30.9 1.2 %collective-permute-done.7.refs_5_.refs_3_ = bf16[64,768]{1,0:T(8,128)(2,1)S(1)} collective-permute-done((bf16[64,768]{1,0:T(8,128)(2,1)S(1)}, bf16[64,768]{1,0:T(8,128)(2,1)S(1)}, u32[]{:S(2)}, u32[]{:S(2)}) %collective-permute-start.7) | collective-permute-done | bytes 98336 | tf_op jit(solution)/shard_map/ppermute | solution.py:19
  32.1 1.0 %attend_own.1 = (f32[256,768]{1,0:T(8,128)S(1)}, f32[256,768]{1,0:T(8,128)S(1)}, f32[256,768]{1,0:T(8,128)S(1)}) custom-call(bf16[3,64,768]{2,1,0:T(8,128)(2,1)S(1)} %get-tuple-element.27.refs_0_, bf16[3,64,768]{2,1,0:T(8,128)(2,1)S(1)} %collective-permute-done.1.refs_1_, bf16[2,64,768]{2,1,0:T(8,128)(2,1)S(1)} %collective-permute-done.2.refs_2_, ...), custom_call_target="tpu_custom_call" | custom-call | flops 201326592 | bytes 1376256 | tf_op jit(solution)/shard_map/attend_own/pallas_call | solution.py:157
  33.0 0.4 collective-permute-done.8.refs_6_
  33.4 0.0 collective-permute-done.3.refs_5_.refs_1_
  33.4 1.0 %attend_prev_weights.1 = (f32[256,768]{1,0:T(8,128)S(1)}, f32[256,768]{1,0:T(8,128)S(1)}, bf16[256,1536]{1,0:T(8,128)(2,1)S(1)}, f32[6,256]{1,0:T(8,128)S(1)}) custom-call(bf16[3,64,768]{2,1,0:T(8,128)(2,1)S(1)} %get-tuple-element.27.refs_0_, bf16[3,64,768]{2,1,0:T(8,128)(2,1)S(1)} %collective-permute-done.1.refs_1_, ...), custom_call_target="tpu_custom_call" | custom-call | flops 201326592 | bytes 1376256 | tf_op jit(solution)/shard_map/attend_prev_weights/pallas_call | solution.py:168
  34.4 0.1 collective-permute-done.5.refs_2_
  34.4 1.1 %attend_prev_values.1 = (f32[256,768]{1,0:T(8,128)}, f32[6,256]{1,0:T(8,128)}) custom-call(bf16[2,64,768]{2,1,0:T(8,128)(2,1)S(1)} %collective-permute-done.refs_4_.refs_0_, bf16[2,2,64,768]{3,2,1,0:T(8,128)(2,1)S(1)} %collective-permute-done.3.refs_5_.refs_1_, bf16[64,768]{1,0:T(8,128)(2,1)S(1)} %collective-permute-done.5.refs_2_, ...), custom_call_target="tpu_custom_call" | custom-call | flops 201326592 | bytes 1376256 | tf_op jit(solution)/shard_map/attend_prev_values/pallas_call | solution.py:178
  (6 shorter events, 0.1 us)
Async XLA Ops:
  0.6 4.4 %copy-start = (bf16[64,3,3072]{2,0,1:T(8,128)(2,1)S(1)}, bf16[64,3,3072]{2,0,1:T(8,128)(2,1)}, u32[]{:S(2)}) copy-start(bf16[64,3,3072]{2,0,1:T(8,128)(2,1)} %param.1) | copy-start | bytes 3538948
  1.8 13.0 %collective-permute-start.1 = (bf16[3,64,768]{2,1,0:T(8,128)(2,1)S(1)}, bf16[3,64,768]{2,1,0:T(8,128)(2,1)S(1)}, u32[]{:S(2)}, u32[]{:S(2)}) collective-permute-start(bf16[3,64,768]{2,1,0:T(8,128)(2,1)S(1)} %get-tuple-element.26), channel_id=1, source_target_pairs={{0,1},{1,2},{2,3},{3,0},{4,5},{5,6},{6,7},{7,4},{8,9},{9,10},{10,1... | collective-permute-start | bytes 884744 | tf_op jit(solution)/shard_map/ppermute | solution.py:19
  4.9 6.0 %collective-permute-start = (bf16[2,64,768]{2,1,0:T(8,128)(2,1)S(1)}, bf16[2,64,768]{2,1,0:T(8,128)(2,1)S(1)}, u32[]{:S(2)}, u32[]{:S(2)}) collective-permute-start(bf16[2,64,768]{2,1,0:T(8,128)(2,1)S(1)} %slice.16), channel_id=1, source_target_pairs={{0,4},{4,8},{8,12},{12,16},{16,20},{20,24},{24,28},{28,0},{1,5},{5... | collective-permute-start | bytes 589832 | tf_op jit(solution)/shard_map/ppermute | solution.py:19
  5.1 13.0 %collective-permute-start.2 = (bf16[2,64,768]{2,1,0:T(8,128)(2,1)S(1)}, bf16[2,64,768]{2,1,0:T(8,128)(2,1)S(1)}, u32[]{:S(2)}, u32[]{:S(2)}) collective-permute-start(bf16[2,64,768]{2,1,0:T(8,128)(2,1)S(1)} %get-tuple-element.25), channel_id=1, source_target_pairs={{0,3},{1,0},{2,1},{3,2},{4,7},{5,4},{6,5},{7,6},{8,11},{9,8},{10,9... | collective-permute-start | bytes 589832 | tf_op jit(solution)/shard_map/ppermute | solution.py:19
  11.0 17.4 %collective-permute-start.4 = (bf16[2,64,768]{2,1,0:T(8,128)(2,1)S(1)}, bf16[2,64,768]{2,1,0:T(8,128)(2,1)S(1)}, u32[]{:S(2)}, u32[]{:S(2)}) collective-permute-start(bf16[2,64,768]{2,1,0:T(8,128)(2,1)S(1)} %get-tuple-element.12), channel_id=1, source_target_pairs={{0,2},{1,3},{2,0},{3,1},{4,6},{5,7},{6,4},{7,5},{8,10},{9,11},{10,... | collective-permute-start | bytes 589832 | tf_op jit(solution)/shard_map/ppermute | solution.py:19
  18.2 15.2 %collective-permute-start.3 = (bf16[2,2,64,768]{3,2,1,0:T(8,128)(2,1)S(1)}, bf16[2,2,64,768]{3,2,1,0:T(8,128)(2,1)S(1)}, u32[]{:S(2)}, u32[]{:S(2)}) collective-permute-start(bf16[2,2,64,768]{3,2,1,0:T(8,128)(2,1)S(1)} %pad_maximum_fusion), channel_id=1, source_target_pairs={{0,4},{4,8},{8,12},{12,16},{16,20},{20,24},{24,28},{28,0},{1,5},{5... | collective-permute-start | bytes 1179656 | tf_op jit(solution)/shard_map/ppermute | solution.py:19
  18.3 12.5 %collective-permute-start.6 = (bf16[64,768]{1,0:T(8,128)(2,1)S(1)}, bf16[64,768]{1,0:T(8,128)(2,1)S(1)}, u32[]{:S(2)}, u32[]{:S(2)}) collective-permute-start(bf16[64,768]{1,0:T(8,128)(2,1)S(1)} %get-tuple-element.13), channel_id=1, source_target_pairs={{0,2},{1,3},{2,0},{3,1},{4,6},{5,7},{6,4},{7,5},{8,10},{9,11},{10,... | collective-permute-start | bytes 294920 | tf_op jit(solution)/shard_map/ppermute | solution.py:19
  24.2 7.8 %collective-permute-start.7 = (bf16[64,768]{1,0:T(8,128)(2,1)S(1)}, bf16[64,768]{1,0:T(8,128)(2,1)S(1)}, u32[]{:S(2)}, u32[]{:S(2)}) collective-permute-start(bf16[64,768]{1,0:T(8,128)(2,1)S(1)} %get-tuple-element.14), channel_id=1, source_target_pairs={{0,3},{1,0},{2,1},{3,2},{4,7},{5,4},{6,5},{7,6},{8,11},{9,8},{10,9... | collective-permute-start | bytes 294920 | tf_op jit(solution)/shard_map/ppermute | solution.py:19
  28.4 5.0 %collective-permute-start.8 = (bf16[64,768]{1,0:T(8,128)(2,1)S(1)}, bf16[64,768]{1,0:T(8,128)(2,1)S(1)}, u32[]{:S(2)}, u32[]{:S(2)}) collective-permute-start(bf16[64,768]{1,0:T(8,128)(2,1)S(1)} %get-tuple-element.28), channel_id=1, source_target_pairs={{0,4},{4,8},{8,12},{12,16},{16,20},{20,24},{24,28},{28,0},{1,5},{5... | collective-permute-start | bytes 294920 | tf_op jit(solution)/shard_map/ppermute | solution.py:19
  28.8 5.7 %collective-permute-start.5 = (bf16[64,768]{1,0:T(8,128)(2,1)S(1)}, bf16[64,768]{1,0:T(8,128)(2,1)S(1)}, u32[]{:S(2)}, u32[]{:S(2)}) collective-permute-start(bf16[64,768]{1,0:T(8,128)(2,1)S(1)} %get-tuple-element.29), channel_id=1, source_target_pairs={{0,4},{4,8},{8,12},{12,16},{16,20},{20,24},{24,28},{28,0},{1,5},{5... | collective-permute-start | bytes 294920 | tf_op jit(solution)/shard_map/ppermute | solution.py:19

commit v6 on v5

--- a/solution.py
+++ b/solution.py
@@ -205,7 +205,7 @@
     pairs = []
     for k in steps:
         pair = cut(1, planes_count, k)
-        pairs.append(shift(after(pair, prevs[0]) if k == mid else pair, "uly", k))
+        pairs.append(shift(after(pair, prevs[0]), "uly", k))
     singles = [shift(after(cut(0, 1, k)[0], pairs[0]), "uly", k) for k in range(2, count)]
     prevs.append(shift(jnp.stack([first[1:]] + pairs[:-1]), "blk", 1))
     prevs += [shift(pairs[-1][i], "blk", 1) for i in range(2)]

time: 35.7 us -> 35.1 us (0.983)
  waiting for transfers between devices: 14.4 us -> 14 us
    ppermute x9, waiting for transfers between devices: 14.4 us -> 14 us  [shift(): lax.ppermute(value, axis, [(i, (i + steps) % count) for i in range(count)])]
  transfers between devices with their start and end apart: 9 -> 9, of which waited for: 8 -> 5; matrix products, arithmetic and copies ran while one was open for 0% -> 0% of each run, Pallas kernels for 5% -> 6%
where the time goes in v6:
time: 35.1 us; the launch traced here: 34.9 us
  starting transfers between devices  15.7 us (45%)
  waiting for transfers between devices  14 us (40%)
  Pallas kernels  3.05 us (9%)
  local copies, waits for them, and re-layouts  1.3 us (4%)
  between operations  0.78 us (2%)
    ppermute x9, starting transfers between devices, shift(): lax.ppermute(value, axis, [(i, (i + steps) % count) for i in range(count)])  15.7 us
    ppermute x9, waiting for transfers between devices, shift(): lax.ppermute(value, axis, [(i, (i + steps) % count) for i in range(count)])  14 us
    dynamic_slice x2, local copies, waits for them, and re-layouts, cut(): lax.dynamic_slice(planes, (first, 0, start), (last - first, tokens, width))  1.23 us
    pallas_call x1, Pallas kernels, attend(): pl.pallas_call(functools.partial(prev_values_kernel, order, heads, group)...  1.11 us
    pallas_call x1, Pallas kernels, attend(): pl.pallas_call(functools.partial(prev_weights_kernel, order, heads, group...  0.98 us
    pallas_call x1, Pallas kernels, attend(): pl.pallas_call(functools.partial(own_kernel, order, heads, group), out_sh...  0.97 us
  transfers between devices with their start and end apart: 9, of which 5 were waited for; matrix products, arithmetic and copies ran while one was open for 0% of the time, Pallas kernels for 6%

profile of v6, /device:TPU:0, one launch (start us, length us, event | category | flops | bytes accessed | tf_op | source)
XLA Modules:
  0.0 34.9 jit_solution(16404451504817746343)
XLA Ops:
  0.6 0.0 copy-start
  0.7 1.2 %dynamic-slice_bitcast_fusion = (bf16[3,64,768]{2,1,0:T(8,128)(2,1)S(1)}, bf16[3,64,768]{2,1,0:T(8,128)(2,1)S(1)}) fusion(bf16[64,3,3072]{2,0,1:T(8,128)(2,1)} %param.1, s32[]{:T(128)S(6)} %select_n.32, s32[]{:T(128)S(6)} %select_n.30), kind=kLoop, calls=%fused_computation.1 | loop fusion | bytes 1179656 | tf_op jit(solution)/shard_map/dynamic_slice | solution.py:198
  1.8 3.1 %collective-permute-start.1 = (bf16[3,64,768]{2,1,0:T(8,128)(2,1)S(1)}, bf16[3,64,768]{2,1,0:T(8,128)(2,1)S(1)}, u32[]{:S(2)}, u32[]{:S(2)}) collective-permute-start(bf16[3,64,768]{2,1,0:T(8,128)(2,1)S(1)} %get-tuple-element.28), channel_id=1, source_target_pairs={{0,1},{1,2},{2,3},{3,0},{4,5},{5,6},{6,7},{7,4},{8,9},{9,10},{10,1... | collective-permute-start | bytes 884744 | tf_op jit(solution)/shard_map/ppermute | solution.py:19
  4.9 0.1 collective-permute-start
  5.0 0.0 copy-done
  5.1 5.9 %collective-permute-done.refs_4_.refs_0_ = bf16[2,64,768]{2,1,0:T(8,128)(2,1)S(1)} collective-permute-done((bf16[2,64,768]{2,1,0:T(8,128)(2,1)S(1)}, bf16[2,64,768]{2,1,0:T(8,128)(2,1)S(1)}, u32[]{:S(2)}, u32[]{:S(2)}) %collective-permute-start) | collective-permute-done | bytes 196640 | tf_op jit(solution)/shard_map/ppermute | solution.py:19
  11.0 2.0 %collective-permute-start.2 = (bf16[2,64,768]{2,1,0:T(8,128)(2,1)S(1)}, bf16[2,64,768]{2,1,0:T(8,128)(2,1)S(1)}, u32[]{:S(2)}, u32[]{:S(2)}) collective-permute-start(bf16[2,64,768]{2,1,0:T(8,128)(2,1)S(1)} %get-tuple-element.13), channel_id=1, source_target_pairs={{0,3},{1,0},{2,1},{3,2},{4,7},{5,4},{6,5},{7,6},{8,11},{9,8},{10,9... | collective-permute-start | bytes 589832 | tf_op jit(solution)/shard_map/ppermute | solution.py:19
  13.0 1.0 %collective-permute-start.4 = (bf16[2,64,768]{2,1,0:T(8,128)(2,1)S(1)}, bf16[2,64,768]{2,1,0:T(8,128)(2,1)S(1)}, u32[]{:S(2)}, u32[]{:S(2)}) collective-permute-start(bf16[2,64,768]{2,1,0:T(8,128)(2,1)S(1)} %get-tuple-element.14), channel_id=1, source_target_pairs={{0,2},{1,3},{2,0},{3,1},{4,6},{5,7},{6,4},{7,5},{8,10},{9,11},{10,... | collective-permute-start | bytes 589832 | tf_op jit(solution)/shard_map/ppermute | solution.py:19
  14.0 0.1 collective-permute-done.1.refs_1_
  14.1 4.3 %collective-permute-done.2.refs_2_ = bf16[2,64,768]{2,1,0:T(8,128)(2,1)S(1)} collective-permute-done((bf16[2,64,768]{2,1,0:T(8,128)(2,1)S(1)}, bf16[2,64,768]{2,1,0:T(8,128)(2,1)S(1)}, u32[]{:S(2)}, u32[]{:S(2)}) %collective-permute-start.2) | collective-permute-done | bytes 196640 | tf_op jit(solution)/shard_map/ppermute | solution.py:19
  18.4 0.1 collective-permute-start.3
  18.5 5.3 %collective-permute-start.6 = (bf16[64,768]{1,0:T(8,128)(2,1)S(1)}, bf16[64,768]{1,0:T(8,128)(2,1)S(1)}, u32[]{:S(2)}, u32[]{:S(2)}) collective-permute-start(bf16[64,768]{1,0:T(8,128)(2,1)S(1)} %get-tuple-element.15), channel_id=1, source_target_pairs={{0,2},{1,3},{2,0},{3,1},{4,6},{5,7},{6,4},{7,5},{8,10},{9,11},{10,... | collective-permute-start | bytes 294920 | tf_op jit(solution)/shard_map/ppermute | solution.py:19
  23.8 3.4 %collective-permute-start.7 = (bf16[64,768]{1,0:T(8,128)(2,1)S(1)}, bf16[64,768]{1,0:T(8,128)(2,1)S(1)}, u32[]{:S(2)}, u32[]{:S(2)}) collective-permute-start(bf16[64,768]{1,0:T(8,128)(2,1)S(1)} %get-tuple-element.16), channel_id=1, source_target_pairs={{0,3},{1,0},{2,1},{3,2},{4,7},{5,4},{6,5},{7,6},{8,11},{9,8},{10,9... | collective-permute-start | bytes 294920 | tf_op jit(solution)/shard_map/ppermute | solution.py:19
  27.2 0.6 %collective-permute-done.4.refs_3_ = bf16[2,64,768]{2,1,0:T(8,128)(2,1)S(1)} collective-permute-done((bf16[2,64,768]{2,1,0:T(8,128)(2,1)S(1)}, bf16[2,64,768]{2,1,0:T(8,128)(2,1)S(1)}, u32[]{:S(2)}, u32[]{:S(2)}) %collective-permute-start.4) | collective-permute-done | bytes 196640 | tf_op jit(solution)/shard_map/ppermute | solution.py:19
  27.8 0.1 collective-permute-start.8
  27.8 0.8 %collective-permute-start.5 = (bf16[64,768]{1,0:T(8,128)(2,1)S(1)}, bf16[64,768]{1,0:T(8,128)(2,1)S(1)}, u32[]{:S(2)}, u32[]{:S(2)}) collective-permute-start(bf16[64,768]{1,0:T(8,128)(2,1)S(1)} %get-tuple-element.31), channel_id=1, source_target_pairs={{0,4},{4,8},{8,12},{12,16},{16,20},{20,24},{24,28},{28,0},{1,5},{5... | collective-permute-start | bytes 294920 | tf_op jit(solution)/shard_map/ppermute | solution.py:19
  28.6 3.2 %collective-permute-done.6.refs_4_.refs_2_ = bf16[64,768]{1,0:T(8,128)(2,1)S(1)} collective-permute-done((bf16[64,768]{1,0:T(8,128)(2,1)S(1)}, bf16[64,768]{1,0:T(8,128)(2,1)S(1)}, u32[]{:S(2)}, u32[]{:S(2)}) %collective-permute-start.6) | collective-permute-done | bytes 98336 | tf_op jit(solution)/shard_map/ppermute | solution.py:19
  31.8 0.0 collective-permute-done.7.refs_5_.refs_3_
  31.8 1.0 %attend_own.1 = (f32[256,768]{1,0:T(8,128)S(1)}, f32[256,768]{1,0:T(8,128)S(1)}, f32[256,768]{1,0:T(8,128)S(1)}) custom-call(bf16[3,64,768]{2,1,0:T(8,128)(2,1)S(1)} %get-tuple-element.29.refs_0_, bf16[3,64,768]{2,1,0:T(8,128)(2,1)S(1)} %collective-permute-done.1.refs_1_, bf16[2,64,768]{2,1,0:T(8,128)(2,1)S(1)} %collective-permute-done.2.refs_2_, ...), custom_call_target="tpu_custom_call" | custom-call | flops 201326592 | bytes 1376256 | tf_op jit(solution)/shard_map/attend_own/pallas_call | solution.py:157
  32.8 0.0 collective-permute-done.8.refs_6_
  32.8 0.0 collective-permute-done.3.refs_5_.refs_1_
  32.8 1.0 %attend_prev_weights.1 = (f32[256,768]{1,0:T(8,128)S(1)}, f32[256,768]{1,0:T(8,128)S(1)}, bf16[256,1536]{1,0:T(8,128)(2,1)S(1)}, f32[6,256]{1,0:T(8,128)S(1)}) custom-call(bf16[3,64,768]{2,1,0:T(8,128)(2,1)S(1)} %get-tuple-element.29.refs_0_, bf16[3,64,768]{2,1,0:T(8,128)(2,1)S(1)} %collective-permute-done.1.refs_1_, ...), custom_call_target="tpu_custom_call" | custom-call | flops 201326592 | bytes 1376256 | tf_op jit(solution)/shard_map/attend_prev_weights/pallas_call | solution.py:168
  33.8 0.0 collective-permute-done.5.refs_2_
  33.8 1.1 %attend_prev_values.1 = (f32[256,768]{1,0:T(8,128)}, f32[6,256]{1,0:T(8,128)}) custom-call(bf16[2,64,768]{2,1,0:T(8,128)(2,1)S(1)} %collective-permute-done.refs_4_.refs_0_, bf16[2,2,64,768]{3,2,1,0:T(8,128)(2,1)S(1)} %collective-permute-done.3.refs_5_.refs_1_, bf16[64,768]{1,0:T(8,128)(2,1)S(1)} %collective-permute-done.5.refs_2_, ...), custom_call_target="tpu_custom_call" | custom-call | flops 201326592 | bytes 1376256 | tf_op jit(solution)/shard_map/attend_prev_values/pallas_call | solution.py:178
  (6 shorter events, 0.1 us)
Async XLA Ops:
  0.6 4.4 %copy-start = (bf16[64,3,3072]{2,0,1:T(8,128)(2,1)S(1)}, bf16[64,3,3072]{2,0,1:T(8,128)(2,1)}, u32[]{:S(2)}) copy-start(bf16[64,3,3072]{2,0,1:T(8,128)(2,1)} %param.1) | copy-start | bytes 3538948
  1.8 12.3 %collective-permute-start.1 = (bf16[3,64,768]{2,1,0:T(8,128)(2,1)S(1)}, bf16[3,64,768]{2,1,0:T(8,128)(2,1)S(1)}, u32[]{:S(2)}, u32[]{:S(2)}) collective-permute-start(bf16[3,64,768]{2,1,0:T(8,128)(2,1)S(1)} %get-tuple-element.28), channel_id=1, source_target_pairs={{0,1},{1,2},{2,3},{3,0},{4,5},{5,6},{6,7},{7,4},{8,9},{9,10},{10,1... | collective-permute-start | bytes 884744 | tf_op jit(solution)/shard_map/ppermute | solution.py:19
  4.9 6.0 %collective-permute-start = (bf16[2,64,768]{2,1,0:T(8,128)(2,1)S(1)}, bf16[2,64,768]{2,1,0:T(8,128)(2,1)S(1)}, u32[]{:S(2)}, u32[]{:S(2)}) collective-permute-start(bf16[2,64,768]{2,1,0:T(8,128)(2,1)S(1)} %slice.16), channel_id=1, source_target_pairs={{0,4},{4,8},{8,12},{12,16},{16,20},{20,24},{24,28},{28,0},{1,5},{5... | collective-permute-start | bytes 589832 | tf_op jit(solution)/shard_map/ppermute | solution.py:19
  11.0 7.4 %collective-permute-start.2 = (bf16[2,64,768]{2,1,0:T(8,128)(2,1)S(1)}, bf16[2,64,768]{2,1,0:T(8,128)(2,1)S(1)}, u32[]{:S(2)}, u32[]{:S(2)}) collective-permute-start(bf16[2,64,768]{2,1,0:T(8,128)(2,1)S(1)} %get-tuple-element.13), channel_id=1, source_target_pairs={{0,3},{1,0},{2,1},{3,2},{4,7},{5,4},{6,5},{7,6},{8,11},{9,8},{10,9... | collective-permute-start | bytes 589832 | tf_op jit(solution)/shard_map/ppermute | solution.py:19
  13.0 14.7 %collective-permute-start.4 = (bf16[2,64,768]{2,1,0:T(8,128)(2,1)S(1)}, bf16[2,64,768]{2,1,0:T(8,128)(2,1)S(1)}, u32[]{:S(2)}, u32[]{:S(2)}) collective-permute-start(bf16[2,64,768]{2,1,0:T(8,128)(2,1)S(1)} %get-tuple-element.14), channel_id=1, source_target_pairs={{0,2},{1,3},{2,0},{3,1},{4,6},{5,7},{6,4},{7,5},{8,10},{9,11},{10,... | collective-permute-start | bytes 589832 | tf_op jit(solution)/shard_map/ppermute | solution.py:19
  18.4 14.4 %collective-permute-start.3 = (bf16[2,2,64,768]{3,2,1,0:T(8,128)(2,1)S(1)}, bf16[2,2,64,768]{3,2,1,0:T(8,128)(2,1)S(1)}, u32[]{:S(2)}, u32[]{:S(2)}) collective-permute-start(bf16[2,2,64,768]{3,2,1,0:T(8,128)(2,1)S(1)} %pad_maximum_fusion), channel_id=1, source_target_pairs={{0,4},{4,8},{8,12},{12,16},{16,20},{20,24},{24,28},{28,0},{1,5},{5... | collective-permute-start | bytes 1179656 | tf_op jit(solution)/shard_map/ppermute | solution.py:19
  18.5 13.3 %collective-permute-start.6 = (bf16[64,768]{1,0:T(8,128)(2,1)S(1)}, bf16[64,768]{1,0:T(8,128)(2,1)S(1)}, u32[]{:S(2)}, u32[]{:S(2)}) collective-permute-start(bf16[64,768]{1,0:T(8,128)(2,1)S(1)} %get-tuple-element.15), channel_id=1, source_target_pairs={{0,2},{1,3},{2,0},{3,1},{4,6},{5,7},{6,4},{7,5},{8,10},{9,11},{10,... | collective-permute-start | bytes 294920 | tf_op jit(solution)/shard_map/ppermute | solution.py:19
  23.8 8.0 %collective-permute-start.7 = (bf16[64,768]{1,0:T(8,128)(2,1)S(1)}, bf16[64,768]{1,0:T(8,128)(2,1)S(1)}, u32[]{:S(2)}, u32[]{:S(2)}) collective-permute-start(bf16[64,768]{1,0:T(8,128)(2,1)S(1)} %get-tuple-element.16), channel_id=1, source_target_pairs={{0,3},{1,0},{2,1},{3,2},{4,7},{5,4},{6,5},{7,6},{8,11},{9,8},{10,9... | collective-permute-start | bytes 294920 | tf_op jit(solution)/shard_map/ppermute | solution.py:19
  27.8 5.1 %collective-permute-start.8 = (bf16[64,768]{1,0:T(8,128)(2,1)S(1)}, bf16[64,768]{1,0:T(8,128)(2,1)S(1)}, u32[]{:S(2)}, u32[]{:S(2)}) collective-permute-start(bf16[64,768]{1,0:T(8,128)(2,1)S(1)} %get-tuple-element.30), channel_id=1, source_target_pairs={{0,4},{4,8},{8,12},{12,16},{16,20},{20,24},{24,28},{28,0},{1,5},{5... | collective-permute-start | bytes 294920 | tf_op jit(solution)/shard_map/ppermute | solution.py:19
  27.8 6.0 %collective-permute-start.5 = (bf16[64,768]{1,0:T(8,128)(2,1)S(1)}, bf16[64,768]{1,0:T(8,128)(2,1)S(1)}, u32[]{:S(2)}, u32[]{:S(2)}) collective-permute-start(bf16[64,768]{1,0:T(8,128)(2,1)S(1)} %get-tuple-element.31), channel_id=1, source_target_pairs={{0,4},{4,8},{8,12},{12,16},{16,20},{20,24},{24,28},{28,0},{1,5},{5... | collective-permute-start | bytes 294920 | tf_op jit(solution)/shard_map/ppermute | solution.py:19

commit v7 on v6

--- a/solution.py
+++ b/solution.py
@@ -205,8 +205,8 @@
     pairs = []
     for k in steps:
         pair = cut(1, planes_count, k)
-        pairs.append(shift(after(pair, prevs[0]), "uly", k))
-    singles = [shift(after(cut(0, 1, k)[0], pairs[0]), "uly", k) for k in range(2, count)]
+        pairs.append(shift(after(pair, prevs[0]) if k != mid else after(pair, prevs[0], first), "uly", k))
+    singles = [shift(after(cut(0, 1, k)[0], first), "uly", k) for k in range(2, count)]
     prevs.append(shift(jnp.stack([first[1:]] + pairs[:-1]), "blk", 1))
     prevs += [shift(pairs[-1][i], "blk", 1) for i in range(2)]
     return attend(tuple(range(count)), [home, first], pairs, singles, prevs, tokens * count, width)

time: 35.1 us -> 35.1 us (level)
  waiting for transfers between devices: 14 us -> 14.5 us
  starting transfers between devices: 15.7 us -> 15.3 us
    ppermute x9, waiting for transfers between devices: 14 us -> 14.5 us  [shift(): lax.ppermute(value, axis, [(i, (i + steps) % count) for i in range(count)])]
    ppermute x9, starting transfers between devices: 15.7 us -> 15.3 us  [shift(): lax.ppermute(value, axis, [(i, (i + steps) % count) for i in range(count)])]
where the time goes in v7:
time: 35.1 us; the launch traced here: 34.9 us
  starting transfers between devices  15.3 us (44%)
  waiting for transfers between devices  14.5 us (41%)
  Pallas kernels  3.05 us (9%)
  local copies, waits for them, and re-layouts  1.3 us (4%)
  between operations  0.78 us (2%)
    ppermute x9, starting transfers between devices, shift(): lax.ppermute(value, axis, [(i, (i + steps) % count) for i in range(count)])  15.3 us
    ppermute x9, waiting for transfers between devices, shift(): lax.ppermute(value, axis, [(i, (i + steps) % count) for i in range(count)])  14.5 us
    dynamic_slice x2, local copies, waits for them, and re-layouts, cut(): lax.dynamic_slice(planes, (first, 0, start), (last - first, tokens, width))  1.23 us
    pallas_call x1, Pallas kernels, attend(): pl.pallas_call(functools.partial(prev_values_kernel, order, heads, group)...  1.11 us
    pallas_call x1, Pallas kernels, attend(): pl.pallas_call(functools.partial(prev_weights_kernel, order, heads, group...  0.98 us
    pallas_call x1, Pallas kernels, attend(): pl.pallas_call(functools.partial(own_kernel, order, heads, group), out_sh...  0.97 us
  transfers between devices with their start and end apart: 9, of which 5 were waited for; matrix products, arithmetic and copies ran while one was open for 0% of the time, Pallas kernels for 6%

profile of v7, /device:TPU:0, one launch (start us, length us, event | category | flops | bytes accessed | tf_op | source)
XLA Modules:
  0.0 34.9 jit_solution(17973140487431630399)
XLA Ops:
  0.6 0.0 copy-start
  0.7 1.2 %dynamic-slice_bitcast_fusion = (bf16[3,64,768]{2,1,0:T(8,128)(2,1)S(1)}, bf16[3,64,768]{2,1,0:T(8,128)(2,1)S(1)}) fusion(bf16[64,3,3072]{2,0,1:T(8,128)(2,1)} %param.1, s32[]{:T(128)S(6)} %select_n.32, s32[]{:T(128)S(6)} %select_n.30), kind=kLoop, calls=%fused_computation.1 | loop fusion | bytes 1179656 | tf_op jit(solution)/shard_map/dynamic_slice | solution.py:198
  1.8 3.1 %collective-permute-start.1 = (bf16[3,64,768]{2,1,0:T(8,128)(2,1)S(1)}, bf16[3,64,768]{2,1,0:T(8,128)(2,1)S(1)}, u32[]{:S(2)}, u32[]{:S(2)}) collective-permute-start(bf16[3,64,768]{2,1,0:T(8,128)(2,1)S(1)} %get-tuple-element.28), channel_id=1, source_target_pairs={{0,1},{1,2},{2,3},{3,0},{4,5},{5,6},{6,7},{7,4},{8,9},{9,10},{10,1... | collective-permute-start | bytes 884744 | tf_op jit(solution)/shard_map/ppermute | solution.py:19
  4.9 0.1 collective-permute-start
  5.0 0.0 copy-done
  5.1 5.9 %collective-permute-done.refs_4_.refs_0_ = bf16[2,64,768]{2,1,0:T(8,128)(2,1)S(1)} collective-permute-done((bf16[2,64,768]{2,1,0:T(8,128)(2,1)S(1)}, bf16[2,64,768]{2,1,0:T(8,128)(2,1)S(1)}, u32[]{:S(2)}, u32[]{:S(2)}) %collective-permute-start) | collective-permute-done | bytes 196640 | tf_op jit(solution)/shard_map/ppermute | solution.py:19
  11.0 2.0 %collective-permute-start.2 = (bf16[2,64,768]{2,1,0:T(8,128)(2,1)S(1)}, bf16[2,64,768]{2,1,0:T(8,128)(2,1)S(1)}, u32[]{:S(2)}, u32[]{:S(2)}) collective-permute-start(bf16[2,64,768]{2,1,0:T(8,128)(2,1)S(1)} %get-tuple-element.13), channel_id=1, source_target_pairs={{0,3},{1,0},{2,1},{3,2},{4,7},{5,4},{6,5},{7,6},{8,11},{9,8},{10,9... | collective-permute-start | bytes 589832 | tf_op jit(solution)/shard_map/ppermute | solution.py:19
  13.0 1.1 %collective-permute-done.1.refs_1_ = bf16[3,64,768]{2,1,0:T(8,128)(2,1)S(1)} collective-permute-done((bf16[3,64,768]{2,1,0:T(8,128)(2,1)S(1)}, bf16[3,64,768]{2,1,0:T(8,128)(2,1)S(1)}, u32[]{:S(2)}, u32[]{:S(2)}) %collective-permute-start.1) | collective-permute-done | bytes 294944 | tf_op jit(solution)/shard_map/ppermute | solution.py:19
  14.1 0.6 %collective-permute-start.4 = (bf16[2,64,768]{2,1,0:T(8,128)(2,1)S(1)}, bf16[2,64,768]{2,1,0:T(8,128)(2,1)S(1)}, u32[]{:S(2)}, u32[]{:S(2)}) collective-permute-start(bf16[2,64,768]{2,1,0:T(8,128)(2,1)S(1)} %get-tuple-element.14), channel_id=1, source_target_pairs={{0,2},{1,3},{2,0},{3,1},{4,6},{5,7},{6,4},{7,5},{8,10},{9,11},{10,... | collective-permute-start | bytes 589832 | tf_op jit(solution)/shard_map/ppermute | solution.py:19
  14.7 3.7 %collective-permute-done.2.refs_2_ = bf16[2,64,768]{2,1,0:T(8,128)(2,1)S(1)} collective-permute-done((bf16[2,64,768]{2,1,0:T(8,128)(2,1)S(1)}, bf16[2,64,768]{2,1,0:T(8,128)(2,1)S(1)}, u32[]{:S(2)}, u32[]{:S(2)}) %collective-permute-start.2) | collective-permute-done | bytes 196640 | tf_op jit(solution)/shard_map/ppermute | solution.py:19
  18.4 0.1 collective-permute-start.3
  18.5 5.3 %collective-permute-start.6 = (bf16[64,768]{1,0:T(8,128)(2,1)S(1)}, bf16[64,768]{1,0:T(8,128)(2,1)S(1)}, u32[]{:S(2)}, u32[]{:S(2)}) collective-permute-start(bf16[64,768]{1,0:T(8,128)(2,1)S(1)} %get-tuple-element.15), channel_id=1, source_target_pairs={{0,2},{1,3},{2,0},{3,1},{4,6},{5,7},{6,4},{7,5},{8,10},{9,11},{10,... | collective-permute-start | bytes 294920 | tf_op jit(solution)/shard_map/ppermute | solution.py:19
  23.8 3.4 %collective-permute-start.7 = (bf16[64,768]{1,0:T(8,128)(2,1)S(1)}, bf16[64,768]{1,0:T(8,128)(2,1)S(1)}, u32[]{:S(2)}, u32[]{:S(2)}) collective-permute-start(bf16[64,768]{1,0:T(8,128)(2,1)S(1)} %get-tuple-element.16), channel_id=1, source_target_pairs={{0,3},{1,0},{2,1},{3,2},{4,7},{5,4},{6,5},{7,6},{8,11},{9,8},{10,9... | collective-permute-start | bytes 294920 | tf_op jit(solution)/shard_map/ppermute | solution.py:19
  27.2 0.6 %collective-permute-done.4.refs_3_ = bf16[2,64,768]{2,1,0:T(8,128)(2,1)S(1)} collective-permute-done((bf16[2,64,768]{2,1,0:T(8,128)(2,1)S(1)}, bf16[2,64,768]{2,1,0:T(8,128)(2,1)S(1)}, u32[]{:S(2)}, u32[]{:S(2)}) %collective-permute-start.4) | collective-permute-done | bytes 196640 | tf_op jit(solution)/shard_map/ppermute | solution.py:19
  27.8 0.1 collective-permute-start.8
  27.8 0.8 %collective-permute-start.5 = (bf16[64,768]{1,0:T(8,128)(2,1)S(1)}, bf16[64,768]{1,0:T(8,128)(2,1)S(1)}, u32[]{:S(2)}, u32[]{:S(2)}) collective-permute-start(bf16[64,768]{1,0:T(8,128)(2,1)S(1)} %get-tuple-element.31), channel_id=1, source_target_pairs={{0,4},{4,8},{8,12},{12,16},{16,20},{20,24},{24,28},{28,0},{1,5},{5... | collective-permute-start | bytes 294920 | tf_op jit(solution)/shard_map/ppermute | solution.py:19
  28.6 3.2 %collective-permute-done.6.refs_4_.refs_2_ = bf16[64,768]{1,0:T(8,128)(2,1)S(1)} collective-permute-done((bf16[64,768]{1,0:T(8,128)(2,1)S(1)}, bf16[64,768]{1,0:T(8,128)(2,1)S(1)}, u32[]{:S(2)}, u32[]{:S(2)}) %collective-permute-start.6) | collective-permute-done | bytes 98336 | tf_op jit(solution)/shard_map/ppermute | solution.py:19
  31.8 0.0 collective-permute-done.7.refs_5_.refs_3_
  31.8 1.0 %attend_own.1 = (f32[256,768]{1,0:T(8,128)S(1)}, f32[256,768]{1,0:T(8,128)S(1)}, f32[256,768]{1,0:T(8,128)S(1)}) custom-call(bf16[3,64,768]{2,1,0:T(8,128)(2,1)S(1)} %get-tuple-element.29.refs_0_, bf16[3,64,768]{2,1,0:T(8,128)(2,1)S(1)} %collective-permute-done.1.refs_1_, bf16[2,64,768]{2,1,0:T(8,128)(2,1)S(1)} %collective-permute-done.2.refs_2_, ...), custom_call_target="tpu_custom_call" | custom-call | flops 201326592 | bytes 1376256 | tf_op jit(solution)/shard_map/attend_own/pallas_call | solution.py:157
  32.8 0.0 collective-permute-done.8.refs_6_
  32.8 0.0 collective-permute-done.3.refs_5_.refs_1_
  32.8 1.0 %attend_prev_weights.1 = (f32[256,768]{1,0:T(8,128)S(1)}, f32[256,768]{1,0:T(8,128)S(1)}, bf16[256,1536]{1,0:T(8,128)(2,1)S(1)}, f32[6,256]{1,0:T(8,128)S(1)}) custom-call(bf16[3,64,768]{2,1,0:T(8,128)(2,1)S(1)} %get-tuple-element.29.refs_0_, bf16[3,64,768]{2,1,0:T(8,128)(2,1)S(1)} %collective-permute-done.1.refs_1_, ...), custom_call_target="tpu_custom_call" | custom-call | flops 201326592 | bytes 1376256 | tf_op jit(solution)/shard_map/attend_prev_weights/pallas_call | solution.py:168
  33.8 0.0 collective-permute-done.5.refs_2_
  33.8 1.1 %attend_prev_values.1 = (f32[256,768]{1,0:T(8,128)}, f32[6,256]{1,0:T(8,128)}) custom-call(bf16[2,64,768]{2,1,0:T(8,128)(2,1)S(1)} %collective-permute-done.refs_4_.refs_0_, bf16[2,2,64,768]{3,2,1,0:T(8,128)(2,1)S(1)} %collective-permute-done.3.refs_5_.refs_1_, bf16[64,768]{1,0:T(8,128)(2,1)S(1)} %collective-permute-done.5.refs_2_, ...), custom_call_target="tpu_custom_call" | custom-call | flops 201326592 | bytes 1376256 | tf_op jit(solution)/shard_map/attend_prev_values/pallas_call | solution.py:178
  (6 shorter events, 0.1 us)
Async XLA Ops:
  0.6 4.4 %copy-start = (bf16[64,3,3072]{2,0,1:T(8,128)(2,1)S(1)}, bf16[64,3,3072]{2,0,1:T(8,128)(2,1)}, u32[]{:S(2)}) copy-start(bf16[64,3,3072]{2,0,1:T(8,128)(2,1)} %param.1) | copy-start | bytes 3538948
  1.8 12.3 %collective-permute-start.1 = (bf16[3,64,768]{2,1,0:T(8,128)(2,1)S(1)}, bf16[3,64,768]{2,1,0:T(8,128)(2,1)S(1)}, u32[]{:S(2)}, u32[]{:S(2)}) collective-permute-start(bf16[3,64,768]{2,1,0:T(8,128)(2,1)S(1)} %get-tuple-element.28), channel_id=1, source_target_pairs={{0,1},{1,2},{2,3},{3,0},{4,5},{5,6},{6,7},{7,4},{8,9},{9,10},{10,1... | collective-permute-start | bytes 884744 | tf_op jit(solution)/shard_map/ppermute | solution.py:19
  4.9 6.0 %collective-permute-start = (bf16[2,64,768]{2,1,0:T(8,128)(2,1)S(1)}, bf16[2,64,768]{2,1,0:T(8,128)(2,1)S(1)}, u32[]{:S(2)}, u32[]{:S(2)}) collective-permute-start(bf16[2,64,768]{2,1,0:T(8,128)(2,1)S(1)} %slice.16), channel_id=1, source_target_pairs={{0,4},{4,8},{8,12},{12,16},{16,20},{20,24},{24,28},{28,0},{1,5},{5... | collective-permute-start | bytes 589832 | tf_op jit(solution)/shard_map/ppermute | solution.py:19
  11.0 7.4 %collective-permute-start.2 = (bf16[2,64,768]{2,1,0:T(8,128)(2,1)S(1)}, bf16[2,64,768]{2,1,0:T(8,128)(2,1)S(1)}, u32[]{:S(2)}, u32[]{:S(2)}) collective-permute-start(bf16[2,64,768]{2,1,0:T(8,128)(2,1)S(1)} %get-tuple-element.13), channel_id=1, source_target_pairs={{0,3},{1,0},{2,1},{3,2},{4,7},{5,4},{6,5},{7,6},{8,11},{9,8},{10,9... | collective-permute-start | bytes 589832 | tf_op jit(solution)/shard_map/ppermute | solution.py:19
  14.1 13.6 %collective-permute-start.4 = (bf16[2,64,768]{2,1,0:T(8,128)(2,1)S(1)}, bf16[2,64,768]{2,1,0:T(8,128)(2,1)S(1)}, u32[]{:S(2)}, u32[]{:S(2)}) collective-permute-start(bf16[2,64,768]{2,1,0:T(8,128)(2,1)S(1)} %get-tuple-element.14), channel_id=1, source_target_pairs={{0,2},{1,3},{2,0},{3,1},{4,6},{5,7},{6,4},{7,5},{8,10},{9,11},{10,... | collective-permute-start | bytes 589832 | tf_op jit(solution)/shard_map/ppermute | solution.py:19
  18.4 14.4 %collective-permute-start.3 = (bf16[2,2,64,768]{3,2,1,0:T(8,128)(2,1)S(1)}, bf16[2,2,64,768]{3,2,1,0:T(8,128)(2,1)S(1)}, u32[]{:S(2)}, u32[]{:S(2)}) collective-permute-start(bf16[2,2,64,768]{3,2,1,0:T(8,128)(2,1)S(1)} %pad_maximum_fusion), channel_id=1, source_target_pairs={{0,4},{4,8},{8,12},{12,16},{16,20},{20,24},{24,28},{28,0},{1,5},{5... | collective-permute-start | bytes 1179656 | tf_op jit(solution)/shard_map/ppermute | solution.py:19
  18.5 13.3 %collective-permute-start.6 = (bf16[64,768]{1,0:T(8,128)(2,1)S(1)}, bf16[64,768]{1,0:T(8,128)(2,1)S(1)}, u32[]{:S(2)}, u32[]{:S(2)}) collective-permute-start(bf16[64,768]{1,0:T(8,128)(2,1)S(1)} %get-tuple-element.15), channel_id=1, source_target_pairs={{0,2},{1,3},{2,0},{3,1},{4,6},{5,7},{6,4},{7,5},{8,10},{9,11},{10,... | collective-permute-start | bytes 294920 | tf_op jit(solution)/shard_map/ppermute | solution.py:19
  23.8 8.0 %collective-permute-start.7 = (bf16[64,768]{1,0:T(8,128)(2,1)S(1)}, bf16[64,768]{1,0:T(8,128)(2,1)S(1)}, u32[]{:S(2)}, u32[]{:S(2)}) collective-permute-start(bf16[64,768]{1,0:T(8,128)(2,1)S(1)} %get-tuple-element.16), channel_id=1, source_target_pairs={{0,3},{1,0},{2,1},{3,2},{4,7},{5,4},{6,5},{7,6},{8,11},{9,8},{10,9... | collective-permute-start | bytes 294920 | tf_op jit(solution)/shard_map/ppermute | solution.py:19
  27.8 5.1 %collective-permute-start.8 = (bf16[64,768]{1,0:T(8,128)(2,1)S(1)}, bf16[64,768]{1,0:T(8,128)(2,1)S(1)}, u32[]{:S(2)}, u32[]{:S(2)}) collective-permute-start(bf16[64,768]{1,0:T(8,128)(2,1)S(1)} %get-tuple-element.30), channel_id=1, source_target_pairs={{0,4},{4,8},{8,12},{12,16},{16,20},{20,24},{24,28},{28,0},{1,5},{5... | collective-permute-start | bytes 294920 | tf_op jit(solution)/shard_map/ppermute | solution.py:19
  27.8 6.0 %collective-permute-start.5 = (bf16[64,768]{1,0:T(8,128)(2,1)S(1)}, bf16[64,768]{1,0:T(8,128)(2,1)S(1)}, u32[]{:S(2)}, u32[]{:S(2)}) collective-permute-start(bf16[64,768]{1,0:T(8,128)(2,1)S(1)} %get-tuple-element.31), channel_id=1, source_target_pairs={{0,4},{4,8},{8,12},{12,16},{16,20},{20,24},{24,28},{28,0},{1,5},{5... | collective-permute-start | bytes 294920 | tf_op jit(solution)/shard_map/ppermute | solution.py:19

commit v8 on v7

--- a/solution.py
+++ b/solution.py
@@ -133,9 +133,10 @@
             added = jnp.dot(weights, values, preferred_element_type=jnp.float32)
             normed = scaled[span, cols] + added * inverse[span, cols]
             for i in range(group):
-                result[rows_of(g * group + i), cols] = normed[i * piece : (i + 1) * piece]
-        copies.append(pltpu.make_async_copy(result.at[:, cols], out.at[:, cols], sem))
-        copies[-1].start()
+                place = rows_of(g * group + i)
+                result[place, cols] = normed[i * piece : (i + 1) * piece]
+                copies.append(pltpu.make_async_copy(result.at[place, cols], out.at[place, cols], sem))
+                copies[-1].start()
     for copy in copies:
         copy.wait()
 
@@ -205,7 +206,7 @@
     pairs = []
     for k in steps:
         pair = cut(1, planes_count, k)
-        pairs.append(shift(after(pair, prevs[0]) if k != mid else after(pair, prevs[0], first), "uly", k))
+        pairs.append(shift(after(pair, prevs[0]), "uly", k))
     singles = [shift(after(cut(0, 1, k)[0], first), "uly", k) for k in range(2, count)]
     prevs.append(shift(jnp.stack([first[1:]] + pairs[:-1]), "blk", 1))
     prevs += [shift(pairs[-1][i], "blk", 1) for i in range(2)]

time: 35.1 us -> 35 us (level)
  waiting for transfers between devices: 14.5 us -> 14 us
  starting transfers between devices: 15.3 us -> 15.7 us
    ppermute x9, waiting for transfers between devices: 14.5 us -> 14 us  [shift(): lax.ppermute(value, axis, [(i, (i + steps) % count) for i in range(count)])]
    ppermute x9, starting transfers between devices: 15.3 us -> 15.7 us  [shift(): lax.ppermute(value, axis, [(i, (i + steps) % count) for i in range(count)])]
where the time goes in v8:
time: 35 us; the launch traced here: 34.9 us
  starting transfers between devices  15.7 us (45%)
  waiting for transfers between devices  14 us (40%)
  Pallas kernels  3.01 us (9%)
  local copies, waits for them, and re-layouts  1.3 us (4%)
  between operations  0.78 us (2%)
    ppermute x9, starting transfers between devices, shift(): lax.ppermute(value, axis, [(i, (i + steps) % count) for i in range(count)])  15.7 us
    ppermute x9, waiting for transfers between devices, shift(): lax.ppermute(value, axis, [(i, (i + steps) % count) for i in range(count)])  14 us
    dynamic_slice x2, local copies, waits for them, and re-layouts, cut(): lax.dynamic_slice(planes, (first, 0, start), (last - first, tokens, width))  1.23 us
    pallas_call x1, Pallas kernels, attend(): pl.pallas_call(functools.partial(prev_values_kernel, order, heads, group)...  1.07 us
    pallas_call x1, Pallas kernels, attend(): pl.pallas_call(functools.partial(prev_weights_kernel, order, heads, group...  0.98 us
    pallas_call x1, Pallas kernels, attend(): pl.pallas_call(functools.partial(own_kernel, order, heads, group), out_sh...  0.97 us
  transfers between devices with their start and end apart: 9, of which 5 were waited for; matrix products, arithmetic and copies ran while one was open for 0% of the time, Pallas kernels for 6%

profile of v8, /device:TPU:0, one launch (start us, length us, event | category | flops | bytes accessed | tf_op | source)
XLA Modules:
  0.0 34.9 jit_solution(9987011255090814870)
XLA Ops:
  0.6 0.0 copy-start
  0.7 1.2 %dynamic-slice_bitcast_fusion = (bf16[3,64,768]{2,1,0:T(8,128)(2,1)S(1)}, bf16[3,64,768]{2,1,0:T(8,128)(2,1)S(1)}) fusion(bf16[64,3,3072]{2,0,1:T(8,128)(2,1)} %param.1, s32[]{:T(128)S(6)} %select_n.32, s32[]{:T(128)S(6)} %select_n.30), kind=kLoop, calls=%fused_computation.1 | loop fusion | bytes 1179656 | tf_op jit(solution)/shard_map/dynamic_slice | solution.py:199
  1.8 3.1 %collective-permute-start.1 = (bf16[3,64,768]{2,1,0:T(8,128)(2,1)S(1)}, bf16[3,64,768]{2,1,0:T(8,128)(2,1)S(1)}, u32[]{:S(2)}, u32[]{:S(2)}) collective-permute-start(bf16[3,64,768]{2,1,0:T(8,128)(2,1)S(1)} %get-tuple-element.28), channel_id=1, source_target_pairs={{0,1},{1,2},{2,3},{3,0},{4,5},{5,6},{6,7},{7,4},{8,9},{9,10},{10,1... | collective-permute-start | bytes 884744 | tf_op jit(solution)/shard_map/ppermute | solution.py:19
  4.9 0.1 collective-permute-start
  5.0 0.0 copy-done
  5.1 5.9 %collective-permute-done.refs_4_.refs_0_ = bf16[2,64,768]{2,1,0:T(8,128)(2,1)S(1)} collective-permute-done((bf16[2,64,768]{2,1,0:T(8,128)(2,1)S(1)}, bf16[2,64,768]{2,1,0:T(8,128)(2,1)S(1)}, u32[]{:S(2)}, u32[]{:S(2)}) %collective-permute-start) | collective-permute-done | bytes 196640 | tf_op jit(solution)/shard_map/ppermute | solution.py:19
  11.0 2.0 %collective-permute-start.2 = (bf16[2,64,768]{2,1,0:T(8,128)(2,1)S(1)}, bf16[2,64,768]{2,1,0:T(8,128)(2,1)S(1)}, u32[]{:S(2)}, u32[]{:S(2)}) collective-permute-start(bf16[2,64,768]{2,1,0:T(8,128)(2,1)S(1)} %get-tuple-element.13), channel_id=1, source_target_pairs={{0,3},{1,0},{2,1},{3,2},{4,7},{5,4},{6,5},{7,6},{8,11},{9,8},{10,9... | collective-permute-start | bytes 589832 | tf_op jit(solution)/shard_map/ppermute | solution.py:19
  13.0 1.0 %collective-permute-start.4 = (bf16[2,64,768]{2,1,0:T(8,128)(2,1)S(1)}, bf16[2,64,768]{2,1,0:T(8,128)(2,1)S(1)}, u32[]{:S(2)}, u32[]{:S(2)}) collective-permute-start(bf16[2,64,768]{2,1,0:T(8,128)(2,1)S(1)} %get-tuple-element.14), channel_id=1, source_target_pairs={{0,2},{1,3},{2,0},{3,1},{4,6},{5,7},{6,4},{7,5},{8,10},{9,11},{10,... | collective-permute-start | bytes 589832 | tf_op jit(solution)/shard_map/ppermute | solution.py:19
  14.0 0.1 collective-permute-done.1.refs_1_
  14.1 4.3 %collective-permute-done.2.refs_2_ = bf16[2,64,768]{2,1,0:T(8,128)(2,1)S(1)} collective-permute-done((bf16[2,64,768]{2,1,0:T(8,128)(2,1)S(1)}, bf16[2,64,768]{2,1,0:T(8,128)(2,1)S(1)}, u32[]{:S(2)}, u32[]{:S(2)}) %collective-permute-start.2) | collective-permute-done | bytes 196640 | tf_op jit(solution)/shard_map/ppermute | solution.py:19
  18.4 0.1 collective-permute-start.3
  18.5 5.3 %collective-permute-start.6 = (bf16[64,768]{1,0:T(8,128)(2,1)S(1)}, bf16[64,768]{1,0:T(8,128)(2,1)S(1)}, u32[]{:S(2)}, u32[]{:S(2)}) collective-permute-start(bf16[64,768]{1,0:T(8,128)(2,1)S(1)} %get-tuple-element.15), channel_id=1, source_target_pairs={{0,2},{1,3},{2,0},{3,1},{4,6},{5,7},{6,4},{7,5},{8,10},{9,11},{10,... | collective-permute-start | bytes 294920 | tf_op jit(solution)/shard_map/ppermute | solution.py:19
  23.8 3.4 %collective-permute-start.7 = (bf16[64,768]{1,0:T(8,128)(2,1)S(1)}, bf16[64,768]{1,0:T(8,128)(2,1)S(1)}, u32[]{:S(2)}, u32[]{:S(2)}) collective-permute-start(bf16[64,768]{1,0:T(8,128)(2,1)S(1)} %get-tuple-element.16), channel_id=1, source_target_pairs={{0,3},{1,0},{2,1},{3,2},{4,7},{5,4},{6,5},{7,6},{8,11},{9,8},{10,9... | collective-permute-start | bytes 294920 | tf_op jit(solution)/shard_map/ppermute | solution.py:19
  27.2 0.6 %collective-permute-done.4.refs_3_ = bf16[2,64,768]{2,1,0:T(8,128)(2,1)S(1)} collective-permute-done((bf16[2,64,768]{2,1,0:T(8,128)(2,1)S(1)}, bf16[2,64,768]{2,1,0:T(8,128)(2,1)S(1)}, u32[]{:S(2)}, u32[]{:S(2)}) %collective-permute-start.4) | collective-permute-done | bytes 196640 | tf_op jit(solution)/shard_map/ppermute | solution.py:19
  27.8 0.1 collective-permute-start.8
  27.8 0.8 %collective-permute-start.5 = (bf16[64,768]{1,0:T(8,128)(2,1)S(1)}, bf16[64,768]{1,0:T(8,128)(2,1)S(1)}, u32[]{:S(2)}, u32[]{:S(2)}) collective-permute-start(bf16[64,768]{1,0:T(8,128)(2,1)S(1)} %get-tuple-element.31), channel_id=1, source_target_pairs={{0,4},{4,8},{8,12},{12,16},{16,20},{20,24},{24,28},{28,0},{1,5},{5... | collective-permute-start | bytes 294920 | tf_op jit(solution)/shard_map/ppermute | solution.py:19
  28.6 3.2 %collective-permute-done.6.refs_4_.refs_2_ = bf16[64,768]{1,0:T(8,128)(2,1)S(1)} collective-permute-done((bf16[64,768]{1,0:T(8,128)(2,1)S(1)}, bf16[64,768]{1,0:T(8,128)(2,1)S(1)}, u32[]{:S(2)}, u32[]{:S(2)}) %collective-permute-start.6) | collective-permute-done | bytes 98336 | tf_op jit(solution)/shard_map/ppermute | solution.py:19
  31.8 0.0 collective-permute-done.7.refs_5_.refs_3_
  31.8 1.0 %attend_own.1 = (f32[256,768]{1,0:T(8,128)S(1)}, f32[256,768]{1,0:T(8,128)S(1)}, f32[256,768]{1,0:T(8,128)S(1)}) custom-call(bf16[3,64,768]{2,1,0:T(8,128)(2,1)S(1)} %get-tuple-element.29.refs_0_, bf16[3,64,768]{2,1,0:T(8,128)(2,1)S(1)} %collective-permute-done.1.refs_1_, bf16[2,64,768]{2,1,0:T(8,128)(2,1)S(1)} %collective-permute-done.2.refs_2_, ...), custom_call_target="tpu_custom_call" | custom-call | flops 201326592 | bytes 1376256 | tf_op jit(solution)/shard_map/attend_own/pallas_call | solution.py:158
  32.8 0.0 collective-permute-done.8.refs_6_
  32.8 0.0 collective-permute-done.3.refs_5_.refs_1_
  32.8 1.0 %attend_prev_weights.1 = (f32[256,768]{1,0:T(8,128)S(1)}, f32[256,768]{1,0:T(8,128)S(1)}, bf16[256,1536]{1,0:T(8,128)(2,1)S(1)}, f32[6,256]{1,0:T(8,128)S(1)}) custom-call(bf16[3,64,768]{2,1,0:T(8,128)(2,1)S(1)} %get-tuple-element.29.refs_0_, bf16[3,64,768]{2,1,0:T(8,128)(2,1)S(1)} %collective-permute-done.1.refs_1_, ...), custom_call_target="tpu_custom_call" | custom-call | flops 201326592 | bytes 1376256 | tf_op jit(solution)/shard_map/attend_prev_weights/pallas_call | solution.py:169
  33.8 0.0 collective-permute-done.5.refs_2_
  33.8 1.1 %attend_prev_values.1 = (f32[256,768]{1,0:T(8,128)}, f32[6,256]{1,0:T(8,128)}) custom-call(bf16[2,64,768]{2,1,0:T(8,128)(2,1)S(1)} %collective-permute-done.refs_4_.refs_0_, bf16[2,2,64,768]{3,2,1,0:T(8,128)(2,1)S(1)} %collective-permute-done.3.refs_5_.refs_1_, bf16[64,768]{1,0:T(8,128)(2,1)S(1)} %collective-permute-done.5.refs_2_, ...), custom_call_target="tpu_custom_call" | custom-call | flops 201326592 | bytes 1376256 | tf_op jit(solution)/shard_map/attend_prev_values/pallas_call | solution.py:179
  (6 shorter events, 0.1 us)
Async XLA Ops:
  0.6 4.4 %copy-start = (bf16[64,3,3072]{2,0,1:T(8,128)(2,1)S(1)}, bf16[64,3,3072]{2,0,1:T(8,128)(2,1)}, u32[]{:S(2)}) copy-start(bf16[64,3,3072]{2,0,1:T(8,128)(2,1)} %param.1) | copy-start | bytes 3538948
  1.8 12.3 %collective-permute-start.1 = (bf16[3,64,768]{2,1,0:T(8,128)(2,1)S(1)}, bf16[3,64,768]{2,1,0:T(8,128)(2,1)S(1)}, u32[]{:S(2)}, u32[]{:S(2)}) collective-permute-start(bf16[3,64,768]{2,1,0:T(8,128)(2,1)S(1)} %get-tuple-element.28), channel_id=1, source_target_pairs={{0,1},{1,2},{2,3},{3,0},{4,5},{5,6},{6,7},{7,4},{8,9},{9,10},{10,1... | collective-permute-start | bytes 884744 | tf_op jit(solution)/shard_map/ppermute | solution.py:19
  4.9 6.0 %collective-permute-start = (bf16[2,64,768]{2,1,0:T(8,128)(2,1)S(1)}, bf16[2,64,768]{2,1,0:T(8,128)(2,1)S(1)}, u32[]{:S(2)}, u32[]{:S(2)}) collective-permute-start(bf16[2,64,768]{2,1,0:T(8,128)(2,1)S(1)} %slice.16), channel_id=1, source_target_pairs={{0,4},{4,8},{8,12},{12,16},{16,20},{20,24},{24,28},{28,0},{1,5},{5... | collective-permute-start | bytes 589832 | tf_op jit(solution)/shard_map/ppermute | solution.py:19
  11.0 7.4 %collective-permute-start.2 = (bf16[2,64,768]{2,1,0:T(8,128)(2,1)S(1)}, bf16[2,64,768]{2,1,0:T(8,128)(2,1)S(1)}, u32[]{:S(2)}, u32[]{:S(2)}) collective-permute-start(bf16[2,64,768]{2,1,0:T(8,128)(2,1)S(1)} %get-tuple-element.13), channel_id=1, source_target_pairs={{0,3},{1,0},{2,1},{3,2},{4,7},{5,4},{6,5},{7,6},{8,11},{9,8},{10,9... | collective-permute-start | bytes 589832 | tf_op jit(solution)/shard_map/ppermute | solution.py:19
  13.0 14.7 %collective-permute-start.4 = (bf16[2,64,768]{2,1,0:T(8,128)(2,1)S(1)}, bf16[2,64,768]{2,1,0:T(8,128)(2,1)S(1)}, u32[]{:S(2)}, u32[]{:S(2)}) collective-permute-start(bf16[2,64,768]{2,1,0:T(8,128)(2,1)S(1)} %get-tuple-element.14), channel_id=1, source_target_pairs={{0,2},{1,3},{2,0},{3,1},{4,6},{5,7},{6,4},{7,5},{8,10},{9,11},{10,... | collective-permute-start | bytes 589832 | tf_op jit(solution)/shard_map/ppermute | solution.py:19
  18.4 14.4 %collective-permute-start.3 = (bf16[2,2,64,768]{3,2,1,0:T(8,128)(2,1)S(1)}, bf16[2,2,64,768]{3,2,1,0:T(8,128)(2,1)S(1)}, u32[]{:S(2)}, u32[]{:S(2)}) collective-permute-start(bf16[2,2,64,768]{3,2,1,0:T(8,128)(2,1)S(1)} %pad_maximum_fusion), channel_id=1, source_target_pairs={{0,4},{4,8},{8,12},{12,16},{16,20},{20,24},{24,28},{28,0},{1,5},{5... | collective-permute-start | bytes 1179656 | tf_op jit(solution)/shard_map/ppermute | solution.py:19
  18.5 13.3 %collective-permute-start.6 = (bf16[64,768]{1,0:T(8,128)(2,1)S(1)}, bf16[64,768]{1,0:T(8,128)(2,1)S(1)}, u32[]{:S(2)}, u32[]{:S(2)}) collective-permute-start(bf16[64,768]{1,0:T(8,128)(2,1)S(1)} %get-tuple-element.15), channel_id=1, source_target_pairs={{0,2},{1,3},{2,0},{3,1},{4,6},{5,7},{6,4},{7,5},{8,10},{9,11},{10,... | collective-permute-start | bytes 294920 | tf_op jit(solution)/shard_map/ppermute | solution.py:19
  23.8 8.0 %collective-permute-start.7 = (bf16[64,768]{1,0:T(8,128)(2,1)S(1)}, bf16[64,768]{1,0:T(8,128)(2,1)S(1)}, u32[]{:S(2)}, u32[]{:S(2)}) collective-permute-start(bf16[64,768]{1,0:T(8,128)(2,1)S(1)} %get-tuple-element.16), channel_id=1, source_target_pairs={{0,3},{1,0},{2,1},{3,2},{4,7},{5,4},{6,5},{7,6},{8,11},{9,8},{10,9... | collective-permute-start | bytes 294920 | tf_op jit(solution)/shard_map/ppermute | solution.py:19
  27.8 5.1 %collective-permute-start.8 = (bf16[64,768]{1,0:T(8,128)(2,1)S(1)}, bf16[64,768]{1,0:T(8,128)(2,1)S(1)}, u32[]{:S(2)}, u32[]{:S(2)}) collective-permute-start(bf16[64,768]{1,0:T(8,128)(2,1)S(1)} %get-tuple-element.30), channel_id=1, source_target_pairs={{0,4},{4,8},{8,12},{12,16},{16,20},{20,24},{24,28},{28,0},{1,5},{5... | collective-permute-start | bytes 294920 | tf_op jit(solution)/shard_map/ppermute | solution.py:19
  27.8 6.0 %collective-permute-start.5 = (bf16[64,768]{1,0:T(8,128)(2,1)S(1)}, bf16[64,768]{1,0:T(8,128)(2,1)S(1)}, u32[]{:S(2)}, u32[]{:S(2)}) collective-permute-start(bf16[64,768]{1,0:T(8,128)(2,1)S(1)} %get-tuple-element.31), channel_id=1, source_target_pairs={{0,4},{4,8},{8,12},{12,16},{16,20},{20,24},{24,28},{28,0},{1,5},{5... | collective-permute-start | bytes 294920 | tf_op jit(solution)/shard_map/ppermute | solution.py:19

commit v9 on v7

--- a/solution.py
+++ b/solution.py
@@ -206,7 +206,7 @@
     for k in steps:
         pair = cut(1, planes_count, k)
         pairs.append(shift(after(pair, prevs[0]) if k != mid else after(pair, prevs[0], first), "uly", k))
-    singles = [shift(after(cut(0, 1, k)[0], first), "uly", k) for k in range(2, count)]
+    singles = [shift(after(cut(0, 1, k)[0], pairs[0]), "uly", k) for k in range(2, count)]
     prevs.append(shift(jnp.stack([first[1:]] + pairs[:-1]), "blk", 1))
     prevs += [shift(pairs[-1][i], "blk", 1) for i in range(2)]
     return attend(tuple(range(count)), [home, first], pairs, singles, prevs, tokens * count, width)

time: 35.1 us -> 35.1 us (level)
  no operation moved by 1% of the time
where the time goes in v9:
time: 35.1 us; the launch traced here: 34.9 us
  starting transfers between devices  15.3 us (44%)
  waiting for transfers between devices  14.5 us (41%)
  Pallas kernels  3.05 us (9%)
  local copies, waits for them, and re-layouts  1.3 us (4%)
  between operations  0.78 us (2%)
    ppermute x9, starting transfers between devices, shift(): lax.ppermute(value, axis, [(i, (i + steps) % count) for i in range(count)])  15.3 us
    ppermute x9, waiting for transfers between devices, shift(): lax.ppermute(value, axis, [(i, (i + steps) % count) for i in range(count)])  14.5 us
    dynamic_slice x2, local copies, waits for them, and re-layouts, cut(): lax.dynamic_slice(planes, (first, 0, start), (last - first, tokens, width))  1.23 us
    pallas_call x1, Pallas kernels, attend(): pl.pallas_call(functools.partial(prev_values_kernel, order, heads, group)...  1.11 us
    pallas_call x1, Pallas kernels, attend(): pl.pallas_call(functools.partial(prev_weights_kernel, order, heads, group...  0.98 us
    pallas_call x1, Pallas kernels, attend(): pl.pallas_call(functools.partial(own_kernel, order, heads, group), out_sh...  0.97 us
  transfers between devices with their start and end apart: 9, of which 5 were waited for; matrix products, arithmetic and copies ran while one was open for 0% of the time, Pallas kernels for 6%

profile of v9, /device:TPU:0, one launch (start us, length us, event | category | flops | bytes accessed | tf_op | source)
XLA Modules:
  0.0 34.9 jit_solution(17973140487431630399)
XLA Ops:
  0.6 0.0 copy-start
  0.7 1.2 %dynamic-slice_bitcast_fusion = (bf16[3,64,768]{2,1,0:T(8,128)(2,1)S(1)}, bf16[3,64,768]{2,1,0:T(8,128)(2,1)S(1)}) fusion(bf16[64,3,3072]{2,0,1:T(8,128)(2,1)} %param.1, s32[]{:T(128)S(6)} %select_n.32, s32[]{:T(128)S(6)} %select_n.30), kind=kLoop, calls=%fused_computation.1 | loop fusion | bytes 1179656 | tf_op jit(solution)/shard_map/dynamic_slice | solution.py:198
  1.8 3.1 %collective-permute-start.1 = (bf16[3,64,768]{2,1,0:T(8,128)(2,1)S(1)}, bf16[3,64,768]{2,1,0:T(8,128)(2,1)S(1)}, u32[]{:S(2)}, u32[]{:S(2)}) collective-permute-start(bf16[3,64,768]{2,1,0:T(8,128)(2,1)S(1)} %get-tuple-element.28), channel_id=1, source_target_pairs={{0,1},{1,2},{2,3},{3,0},{4,5},{5,6},{6,7},{7,4},{8,9},{9,10},{10,1... | collective-permute-start | bytes 884744 | tf_op jit(solution)/shard_map/ppermute | solution.py:19
  4.9 0.1 collective-permute-start
  5.0 0.0 copy-done
  5.1 5.9 %collective-permute-done.refs_4_.refs_0_ = bf16[2,64,768]{2,1,0:T(8,128)(2,1)S(1)} collective-permute-done((bf16[2,64,768]{2,1,0:T(8,128)(2,1)S(1)}, bf16[2,64,768]{2,1,0:T(8,128)(2,1)S(1)}, u32[]{:S(2)}, u32[]{:S(2)}) %collective-permute-start) | collective-permute-done | bytes 196640 | tf_op jit(solution)/shard_map/ppermute | solution.py:19
  11.0 2.0 %collective-permute-start.2 = (bf16[2,64,768]{2,1,0:T(8,128)(2,1)S(1)}, bf16[2,64,768]{2,1,0:T(8,128)(2,1)S(1)}, u32[]{:S(2)}, u32[]{:S(2)}) collective-permute-start(bf16[2,64,768]{2,1,0:T(8,128)(2,1)S(1)} %get-tuple-element.13), channel_id=1, source_target_pairs={{0,3},{1,0},{2,1},{3,2},{4,7},{5,4},{6,5},{7,6},{8,11},{9,8},{10,9... | collective-permute-start | bytes 589832 | tf_op jit(solution)/shard_map/ppermute | solution.py:19
  13.0 1.1 %collective-permute-done.1.refs_1_ = bf16[3,64,768]{2,1,0:T(8,128)(2,1)S(1)} collective-permute-done((bf16[3,64,768]{2,1,0:T(8,128)(2,1)S(1)}, bf16[3,64,768]{2,1,0:T(8,128)(2,1)S(1)}, u32[]{:S(2)}, u32[]{:S(2)}) %collective-permute-start.1) | collective-permute-done | bytes 294944 | tf_op jit(solution)/shard_map/ppermute | solution.py:19
  14.1 0.6 %collective-permute-start.4 = (bf16[2,64,768]{2,1,0:T(8,128)(2,1)S(1)}, bf16[2,64,768]{2,1,0:T(8,128)(2,1)S(1)}, u32[]{:S(2)}, u32[]{:S(2)}) collective-permute-start(bf16[2,64,768]{2,1,0:T(8,128)(2,1)S(1)} %get-tuple-element.14), channel_id=1, source_target_pairs={{0,2},{1,3},{2,0},{3,1},{4,6},{5,7},{6,4},{7,5},{8,10},{9,11},{10,... | collective-permute-start | bytes 589832 | tf_op jit(solution)/shard_map/ppermute | solution.py:19
  14.7 3.7 %collective-permute-done.2.refs_2_ = bf16[2,64,768]{2,1,0:T(8,128)(2,1)S(1)} collective-permute-done((bf16[2,64,768]{2,1,0:T(8,128)(2,1)S(1)}, bf16[2,64,768]{2,1,0:T(8,128)(2,1)S(1)}, u32[]{:S(2)}, u32[]{:S(2)}) %collective-permute-start.2) | collective-permute-done | bytes 196640 | tf_op jit(solution)/shard_map/ppermute | solution.py:19
  18.4 0.1 collective-permute-start.3
  18.5 5.3 %collective-permute-start.6 = (bf16[64,768]{1,0:T(8,128)(2,1)S(1)}, bf16[64,768]{1,0:T(8,128)(2,1)S(1)}, u32[]{:S(2)}, u32[]{:S(2)}) collective-permute-start(bf16[64,768]{1,0:T(8,128)(2,1)S(1)} %get-tuple-element.15), channel_id=1, source_target_pairs={{0,2},{1,3},{2,0},{3,1},{4,6},{5,7},{6,4},{7,5},{8,10},{9,11},{10,... | collective-permute-start | bytes 294920 | tf_op jit(solution)/shard_map/ppermute | solution.py:19
  23.8 3.4 %collective-permute-start.7 = (bf16[64,768]{1,0:T(8,128)(2,1)S(1)}, bf16[64,768]{1,0:T(8,128)(2,1)S(1)}, u32[]{:S(2)}, u32[]{:S(2)}) collective-permute-start(bf16[64,768]{1,0:T(8,128)(2,1)S(1)} %get-tuple-element.16), channel_id=1, source_target_pairs={{0,3},{1,0},{2,1},{3,2},{4,7},{5,4},{6,5},{7,6},{8,11},{9,8},{10,9... | collective-permute-start | bytes 294920 | tf_op jit(solution)/shard_map/ppermute | solution.py:19
  27.2 0.6 %collective-permute-done.4.refs_3_ = bf16[2,64,768]{2,1,0:T(8,128)(2,1)S(1)} collective-permute-done((bf16[2,64,768]{2,1,0:T(8,128)(2,1)S(1)}, bf16[2,64,768]{2,1,0:T(8,128)(2,1)S(1)}, u32[]{:S(2)}, u32[]{:S(2)}) %collective-permute-start.4) | collective-permute-done | bytes 196640 | tf_op jit(solution)/shard_map/ppermute | solution.py:19
  27.8 0.1 collective-permute-start.8
  27.8 0.8 %collective-permute-start.5 = (bf16[64,768]{1,0:T(8,128)(2,1)S(1)}, bf16[64,768]{1,0:T(8,128)(2,1)S(1)}, u32[]{:S(2)}, u32[]{:S(2)}) collective-permute-start(bf16[64,768]{1,0:T(8,128)(2,1)S(1)} %get-tuple-element.31), channel_id=1, source_target_pairs={{0,4},{4,8},{8,12},{12,16},{16,20},{20,24},{24,28},{28,0},{1,5},{5... | collective-permute-start | bytes 294920 | tf_op jit(solution)/shard_map/ppermute | solution.py:19
  28.6 3.2 %collective-permute-done.6.refs_4_.refs_2_ = bf16[64,768]{1,0:T(8,128)(2,1)S(1)} collective-permute-done((bf16[64,768]{1,0:T(8,128)(2,1)S(1)}, bf16[64,768]{1,0:T(8,128)(2,1)S(1)}, u32[]{:S(2)}, u32[]{:S(2)}) %collective-permute-start.6) | collective-permute-done | bytes 98336 | tf_op jit(solution)/shard_map/ppermute | solution.py:19
  31.8 0.0 collective-permute-done.7.refs_5_.refs_3_
  31.8 1.0 %attend_own.1 = (f32[256,768]{1,0:T(8,128)S(1)}, f32[256,768]{1,0:T(8,128)S(1)}, f32[256,768]{1,0:T(8,128)S(1)}) custom-call(bf16[3,64,768]{2,1,0:T(8,128)(2,1)S(1)} %get-tuple-element.29.refs_0_, bf16[3,64,768]{2,1,0:T(8,128)(2,1)S(1)} %collective-permute-done.1.refs_1_, bf16[2,64,768]{2,1,0:T(8,128)(2,1)S(1)} %collective-permute-done.2.refs_2_, ...), custom_call_target="tpu_custom_call" | custom-call | flops 201326592 | bytes 1376256 | tf_op jit(solution)/shard_map/attend_own/pallas_call | solution.py:157
  32.8 0.0 collective-permute-done.8.refs_6_
  32.8 0.0 collective-permute-done.3.refs_5_.refs_1_
  32.8 1.0 %attend_prev_weights.1 = (f32[256,768]{1,0:T(8,128)S(1)}, f32[256,768]{1,0:T(8,128)S(1)}, bf16[256,1536]{1,0:T(8,128)(2,1)S(1)}, f32[6,256]{1,0:T(8,128)S(1)}) custom-call(bf16[3,64,768]{2,1,0:T(8,128)(2,1)S(1)} %get-tuple-element.29.refs_0_, bf16[3,64,768]{2,1,0:T(8,128)(2,1)S(1)} %collective-permute-done.1.refs_1_, ...), custom_call_target="tpu_custom_call" | custom-call | flops 201326592 | bytes 1376256 | tf_op jit(solution)/shard_map/attend_prev_weights/pallas_call | solution.py:168
  33.8 0.0 collective-permute-done.5.refs_2_
  33.8 1.1 %attend_prev_values.1 = (f32[256,768]{1,0:T(8,128)}, f32[6,256]{1,0:T(8,128)}) custom-call(bf16[2,64,768]{2,1,0:T(8,128)(2,1)S(1)} %collective-permute-done.refs_4_.refs_0_, bf16[2,2,64,768]{3,2,1,0:T(8,128)(2,1)S(1)} %collective-permute-done.3.refs_5_.refs_1_, bf16[64,768]{1,0:T(8,128)(2,1)S(1)} %collective-permute-done.5.refs_2_, ...), custom_call_target="tpu_custom_call" | custom-call | flops 201326592 | bytes 1376256 | tf_op jit(solution)/shard_map/attend_prev_values/pallas_call | solution.py:178
  (6 shorter events, 0.1 us)
Async XLA Ops:
  0.6 4.4 %copy-start = (bf16[64,3,3072]{2,0,1:T(8,128)(2,1)S(1)}, bf16[64,3,3072]{2,0,1:T(8,128)(2,1)}, u32[]{:S(2)}) copy-start(bf16[64,3,3072]{2,0,1:T(8,128)(2,1)} %param.1) | copy-start | bytes 3538948
  1.8 12.3 %collective-permute-start.1 = (bf16[3,64,768]{2,1,0:T(8,128)(2,1)S(1)}, bf16[3,64,768]{2,1,0:T(8,128)(2,1)S(1)}, u32[]{:S(2)}, u32[]{:S(2)}) collective-permute-start(bf16[3,64,768]{2,1,0:T(8,128)(2,1)S(1)} %get-tuple-element.28), channel_id=1, source_target_pairs={{0,1},{1,2},{2,3},{3,0},{4,5},{5,6},{6,7},{7,4},{8,9},{9,10},{10,1... | collective-permute-start | bytes 884744 | tf_op jit(solution)/shard_map/ppermute | solution.py:19
  4.9 6.0 %collective-permute-start = (bf16[2,64,768]{2,1,0:T(8,128)(2,1)S(1)}, bf16[2,64,768]{2,1,0:T(8,128)(2,1)S(1)}, u32[]{:S(2)}, u32[]{:S(2)}) collective-permute-start(bf16[2,64,768]{2,1,0:T(8,128)(2,1)S(1)} %slice.16), channel_id=1, source_target_pairs={{0,4},{4,8},{8,12},{12,16},{16,20},{20,24},{24,28},{28,0},{1,5},{5... | collective-permute-start | bytes 589832 | tf_op jit(solution)/shard_map/ppermute | solution.py:19
  11.0 7.4 %collective-permute-start.2 = (bf16[2,64,768]{2,1,0:T(8,128)(2,1)S(1)}, bf16[2,64,768]{2,1,0:T(8,128)(2,1)S(1)}, u32[]{:S(2)}, u32[]{:S(2)}) collective-permute-start(bf16[2,64,768]{2,1,0:T(8,128)(2,1)S(1)} %get-tuple-element.13), channel_id=1, source_target_pairs={{0,3},{1,0},{2,1},{3,2},{4,7},{5,4},{6,5},{7,6},{8,11},{9,8},{10,9... | collective-permute-start | bytes 589832 | tf_op jit(solution)/shard_map/ppermute | solution.py:19
  14.1 13.6 %collective-permute-start.4 = (bf16[2,64,768]{2,1,0:T(8,128)(2,1)S(1)}, bf16[2,64,768]{2,1,0:T(8,128)(2,1)S(1)}, u32[]{:S(2)}, u32[]{:S(2)}) collective-permute-start(bf16[2,64,768]{2,1,0:T(8,128)(2,1)S(1)} %get-tuple-element.14), channel_id=1, source_target_pairs={{0,2},{1,3},{2,0},{3,1},{4,6},{5,7},{6,4},{7,5},{8,10},{9,11},{10,... | collective-permute-start | bytes 589832 | tf_op jit(solution)/shard_map/ppermute | solution.py:19
  18.4 14.4 %collective-permute-start.3 = (bf16[2,2,64,768]{3,2,1,0:T(8,128)(2,1)S(1)}, bf16[2,2,64,768]{3,2,1,0:T(8,128)(2,1)S(1)}, u32[]{:S(2)}, u32[]{:S(2)}) collective-permute-start(bf16[2,2,64,768]{3,2,1,0:T(8,128)(2,1)S(1)} %pad_maximum_fusion), channel_id=1, source_target_pairs={{0,4},{4,8},{8,12},{12,16},{16,20},{20,24},{24,28},{28,0},{1,5},{5... | collective-permute-start | bytes 1179656 | tf_op jit(solution)/shard_map/ppermute | solution.py:19
  18.5 13.3 %collective-permute-start.6 = (bf16[64,768]{1,0:T(8,128)(2,1)S(1)}, bf16[64,768]{1,0:T(8,128)(2,1)S(1)}, u32[]{:S(2)}, u32[]{:S(2)}) collective-permute-start(bf16[64,768]{1,0:T(8,128)(2,1)S(1)} %get-tuple-element.15), channel_id=1, source_target_pairs={{0,2},{1,3},{2,0},{3,1},{4,6},{5,7},{6,4},{7,5},{8,10},{9,11},{10,... | collective-permute-start | bytes 294920 | tf_op jit(solution)/shard_map/ppermute | solution.py:19
  23.8 8.0 %collective-permute-start.7 = (bf16[64,768]{1,0:T(8,128)(2,1)S(1)}, bf16[64,768]{1,0:T(8,128)(2,1)S(1)}, u32[]{:S(2)}, u32[]{:S(2)}) collective-permute-start(bf16[64,768]{1,0:T(8,128)(2,1)S(1)} %get-tuple-element.16), channel_id=1, source_target_pairs={{0,3},{1,0},{2,1},{3,2},{4,7},{5,4},{6,5},{7,6},{8,11},{9,8},{10,9... | collective-permute-start | bytes 294920 | tf_op jit(solution)/shard_map/ppermute | solution.py:19
  27.8 5.1 %collective-permute-start.8 = (bf16[64,768]{1,0:T(8,128)(2,1)S(1)}, bf16[64,768]{1,0:T(8,128)(2,1)S(1)}, u32[]{:S(2)}, u32[]{:S(2)}) collective-permute-start(bf16[64,768]{1,0:T(8,128)(2,1)S(1)} %get-tuple-element.30), channel_id=1, source_target_pairs={{0,4},{4,8},{8,12},{12,16},{16,20},{20,24},{24,28},{28,0},{1,5},{5... | collective-permute-start | bytes 294920 | tf_op jit(solution)/shard_map/ppermute | solution.py:19
  27.8 6.0 %collective-permute-start.5 = (bf16[64,768]{1,0:T(8,128)(2,1)S(1)}, bf16[64,768]{1,0:T(8,128)(2,1)S(1)}, u32[]{:S(2)}, u32[]{:S(2)}) collective-permute-start(bf16[64,768]{1,0:T(8,128)(2,1)S(1)} %get-tuple-element.31), channel_id=1, source_target_pairs={{0,4},{4,8},{8,12},{12,16},{16,20},{20,24},{24,28},{28,0},{1,5},{5... | collective-permute-start | bytes 294920 | tf_op jit(solution)/shard_map/ppermute | solution.py:19
